TPU v7x, 128 devices: a whole 4x4x4 slice. The times are simulated.
128 devices in a mesh: ctx: 32 (over z, x, core), tp: 4 (over y).
Axes of the slice: x: 4, y: 4, z: 4, core: 2. Of those that a mesh axis runs over, the one named last changes fastest.
Arguments:
- seq_input: bfloat16 [65536, 4096], P('ctx', 'tp'), may hold values from -6 to 6
- in_basis: bfloat16 [65536, 128], P('ctx'), may hold values from -1.75 to 1.75
- out_basis: bfloat16 [65536, 128], P('ctx'), may hold values from -1.75 to 1.75
- step_size: float32 [32, 65536], P('tp', 'ctx'), may hold values from 0 to 0.5, as said below
- log_decay: float32 [32, 65536], P('tp', 'ctx'), may hold values from -1 to 0, as said below
- skip_gain: float32 [32], P('tp'), may hold values from 0.5 to 1.5
- access_counts: int32 [32], P('ctx'), may hold values from 512 to 2048, as said below
- out_cotangent: bfloat16 [65536, 4096], P('ctx', 'tp'), may hold values from -6 to 6
Outputs:
- input_grad: bfloat16 [65536, 4096], P('ctx', 'tp')
- in_basis_grad: float32 [65536, 128], P('ctx')
- out_basis_grad: float32 [65536, 128], P('ctx')
- step_grad: float32 [32, 65536], P('tp', 'ctx')
- decay_grad: float32 [32, 65536], P('tp', 'ctx')
Inputs may be any that keep to these rules, and one draw needn't show every extreme that they name: `access_counts`: one index of ctx has exactly 2048 used row slots and another exactly a quarter of 2048. `log_decay`: never positive. `step_size`: Positive.
All inputs are finite; a program needn't handle non-finite values.
Results may differ from a plain program's by a relative error of at most 0.03.
Values sent between devices are 32-bit elements; how exact they have to be, the bound alone decides.
No kernel may reach another device: no remote copies, remote signals or barrier semaphores. Data moves between devices by JAX's collectives and lax.ppermute only.
A program may use at most 192 MiB of HBM per device.

v0:
```python
import jax
import jax.numpy as jnp
from jax import lax
from jax.sharding import PartitionSpec as P

GROUP = 256


def from_behind(array, axis, by):
    length = lax.axis_size(axis)
    pairs = [(i, i + by) for i in range(length) if 0 <= i + by < length]
    return lax.ppermute(array, axis, pairs)


def run_groups(inputs, basis_in, basis_out, step, decay, gain, used, start, block):
    row_count, head_count, head_width = inputs.shape
    blocks = row_count // block
    x_blocks = inputs.reshape(blocks, block, head_count, head_width)
    in_blocks = basis_in.reshape(blocks, block, basis_in.shape[1])
    out_blocks = basis_out.reshape(blocks, block, basis_out.shape[1])
    step_blocks = step.reshape(head_count, blocks, block).transpose(1, 0, 2)
    decay_blocks = decay.reshape(head_count, blocks, block).transpose(1, 0, 2)
    used_blocks = used.reshape(blocks, block)
    later = lax.broadcasted_iota(jnp.int32, (block, block), 0)
    earlier = lax.broadcasted_iota(jnp.int32, (block, block), 1)
    lower_tri = later >= earlier

    @jax.checkpoint
    def advance(state, pieces):
        x_block, in_block, out_block, step_block, decay_block, used_block = pieces
        in_half = in_block.astype(jnp.bfloat16)
        out_half = out_block.astype(jnp.bfloat16)
        cumulative = jnp.cumsum(decay_block, axis=1)
        gaps = jnp.where(lower_tri[None], cumulative[:, :, None] - cumulative[:, None, :], 0.0)
        scores = jnp.dot(out_half, in_half.T, preferred_element_type=jnp.float32)
        weights = (jnp.where(lower_tri[None], jnp.exp(gaps), 0.0) * scores[None]).astype(
            jnp.bfloat16
        )
        inject = (x_block * step_block.T[:, :, None]).astype(jnp.bfloat16)
        inner = jnp.einsum("hij,jhp->ihp", weights, inject, preferred_element_type=jnp.float32)
        carried = (
            jnp.einsum(
                "hpn,in->ihp",
                state.astype(jnp.bfloat16),
                out_half,
                preferred_element_type=jnp.float32,
            )
            * jnp.exp(cumulative).T[:, :, None]
        )
        mixed = (inner + carried + gain[None, :, None] * x_block) * used_block[:, None, None]
        tail_decay = jnp.exp(cumulative[:, -1:] - cumulative)
        scaled = (inject.astype(jnp.float32) * tail_decay.T[:, :, None]).astype(jnp.bfloat16)
        new_state = jnp.exp(cumulative[:, -1])[:, None, None] * state + jnp.einsum(
            "jhp,jn->hpn", scaled, in_half, preferred_element_type=jnp.float32
        )
        return (new_state, mixed)

    final, mixed_blocks = lax.scan(
        advance, start, (x_blocks, in_blocks, out_blocks, step_blocks, decay_blocks, used_blocks)
    )
    return (mixed_blocks.reshape(row_count, head_count, head_width), final)


def shards(
    seq_input, in_basis, out_basis, step_size, log_decay, skip_gain, access_counts, out_cotangent
):
    row_count = seq_input.shape[0]
    head_count = step_size.shape[0]
    head_width = seq_input.shape[1] // head_count
    state_width = in_basis.shape[1]
    used = (jnp.arange(row_count, dtype=jnp.int32) < access_counts[0]).astype(jnp.float32)
    inputs = seq_input.astype(jnp.float32).reshape(row_count, head_count, head_width)
    basis_in = in_basis.astype(jnp.float32)
    basis_out = out_basis.astype(jnp.float32)
    cotangent = out_cotangent.astype(jnp.float32).reshape(row_count, head_count, head_width)
    step_used = step_size * used[None]
    decay_used = log_decay * used[None]
    cumulative = jnp.cumsum(decay_used, axis=1)
    total = cumulative[:, -1]
    decay_total = jnp.exp(total)
    inject = (inputs * step_used.T[:, :, None]).astype(jnp.bfloat16)
    scaled = (
        inject.astype(jnp.float32) * jnp.exp(total[None, :] - cumulative.T)[:, :, None]
    ).astype(jnp.bfloat16)
    final_local = jnp.einsum("thp,tn->hpn", scaled, in_basis, preferred_element_type=jnp.float32)
    weighted = (cotangent * (used[:, None] * jnp.exp(cumulative.T))[:, :, None]).astype(
        jnp.bfloat16
    )
    entry_adjoint = jnp.einsum(
        "thp,tn->hpn", weighted, out_basis, preferred_element_type=jnp.float32
    )
    empty = jnp.zeros((head_count, head_width, state_width), jnp.float32)
    steps_needed = lax.axis_size("ctx") - 1

    def forward_turn(turn, state):
        return from_behind(decay_total[:, None, None] * state + final_local, "ctx", 1)

    def backward_turn(turn, adjoint):
        return from_behind(decay_total[:, None, None] * adjoint + entry_adjoint, "ctx", -1)

    start_state = lax.fori_loop(0, steps_needed, forward_turn, empty)
    exit_adjoint = lax.fori_loop(0, steps_needed, backward_turn, empty)

    def forward(x_value, in_value, out_value, step_value, decay_value):
        return run_groups(
            x_value,
            in_value,
            out_value,
            step_value * used[None],
            decay_value * used[None],
            skip_gain,
            used,
            start_state,
            GROUP,
        )

    outputs, pull = jax.vjp(forward, inputs, basis_in, basis_out, step_size, log_decay)
    grad_x, grad_in, grad_out, grad_step, grad_decay = pull((cotangent, exit_adjoint))
    grad_in, grad_out = lax.psum((grad_in, grad_out), "tp")
    input_grad = grad_x.reshape(row_count, head_count * head_width).astype(jnp.bfloat16)
    return (input_grad, grad_in, grad_out, grad_step, grad_decay)


def solution(mesh):
    placed = (
        P("ctx", "tp"),
        P("ctx", None),
        P("ctx", None),
        P("tp", "ctx"),
        P("tp", "ctx"),
        P("tp"),
        P("ctx"),
        P("ctx", "tp"),
    )
    return jax.shard_map(
        shards,
        mesh=mesh,
        in_specs=placed,
        out_specs=(P("ctx", "tp"), P("ctx", None), P("ctx", None), P("tp", "ctx"), P("tp", "ctx")),
        check_vma=False,
    )
```

profile of v0, /device:TPU:0, one launch (start us, length us, event | category | flops | bytes accessed | tf_op | source)
XLA Modules:
  0.0 1195.0 jit_solution(5537736411560697174)
XLA Ops:
  49.7 9.2 copy.49
  63.7 346.1 %while.58 = (s32[]{:T(128)}, f32[8,128,128]{2,1,0:T(8,128)S(1)}, f32[8]{0:T(128)S(1)}, f32[8,128,128]{2,1,0:T(8,128)S(1)}, s32[]{:T(128)}) while((s32[]{:T(128)}, f32[8,128,128]{2,1,0:T(8,128)S(1)}, f32[8]{0:T(128)S(1)}, f32[8,128,128]{2,1,0:T(8,128)S(1)}, s32[]{:T(128)}) %tuple.120), condition=%wide.region_5.6_spmd, body=%wide.region_4.5_spmd.sunk | while | flops 262146 | bytes 3670149 | solution.py:101
  77.2 9.0 collective-permute-start.1
  98.4 9.0 collective-permute-start.1
  109.1 9.0 collective-permute-start.1
  130.3 9.0 collective-permute-start.1
  140.9 9.0 collective-permute-start.1
  162.2 9.0 collective-permute-start.1
  172.8 9.0 collective-permute-start.1
  183.4 9.0 collective-permute-start.1
  194.0 9.0 collective-permute-start.1
  204.6 9.0 collective-permute-start.1
  215.3 9.0 collective-permute-start.1
  225.9 9.0 collective-permute-start.1
  236.5 9.0 collective-permute-start.1
  247.1 9.0 collective-permute-start.1
  257.8 10.5 collective-permute-start.1
  269.9 11.1 collective-permute-start.1
  282.6 11.1 collective-permute-start.1
  295.4 11.1 collective-permute-start.1
  308.1 11.1 collective-permute-start.1
  320.8 11.1 collective-permute-start.1
  333.6 11.1 collective-permute-start.1
  346.3 11.1 collective-permute-start.1
  359.0 11.1 collective-permute-start.1
  371.7 11.1 collective-permute-start.1
  384.5 11.1 collective-permute-start.1
  397.2 11.1 collective-permute-start.1
  409.8 39.8 %while.59 = (s32[]{:T(128)}, f32[8,128,128]{2,1,0:T(8,128)S(1)}, f32[8,8,128,128]{3,2,1,0:T(8,128)}, f32[8,8,256]{2,1,0:T(8,128)}, f32[8,256,8,128]{1,3,2,0:T(8,...) while((s32[]{:T(128)}, f32[8,128,128]{2,1,0:T(8,128)S(1)}, ...), condition=%wide.region_9.10_spmd, body=%wide.region_6.9_spmd.sunk | while | flops 68945944 | bytes 3311885 | solution.py:58
  450.2 9.0 copy.62
  461.6 397.1 %while.57 = (s32[]{:T(128)}, f32[8,128,128]{2,1,0:T(8,128)S(1)}, f32[8]{0:T(128)S(1)}, f32[8,128,128]{2,1,0:T(8,128)S(1)}, s32[]{:T(128)}) while((s32[]{:T(128)}, f32[8,128,128]{2,1,0:T(8,128)S(1)}, f32[8]{0:T(128)S(1)}, f32[8,128,128]{2,1,0:T(8,128)S(1)}, s32[]{:T(128)}) %tuple.135), condition=%wide.region_3.4_spmd, body=%wide.region_2.3_spmd.sunk | while | flops 262146 | bytes 3670149 | solution.py:102
  463.0 11.2 collective-permute-done
  475.7 12.1 %collective-permute-done = f32[8,128,128]{2,1,0:T(8,128)S(1)} collective-permute-done((f32[8,128,128]{2,1,0:T(8,128)S(1)}, f32[8,128,128]{2,1,0:T(8,128)S(1)}, u32[]{:S(2)}, u32[]{:S(2)}) %collective-permute-start) | collective-permute-done | bytes 524320 | tf_op jit(solution)/shard_map/while/body/eval_jaxpr/ppermute | solution.py:12
  489.2 11.2 collective-permute-done
  501.7 12.1 %collective-permute-done = f32[8,128,128]{2,1,0:T(8,128)S(1)} collective-permute-done((f32[8,128,128]{2,1,0:T(8,128)S(1)}, f32[8,128,128]{2,1,0:T(8,128)S(1)}, u32[]{:S(2)}, u32[]{:S(2)}) %collective-permute-start) | collective-permute-done | bytes 524320 | tf_op jit(solution)/shard_map/while/body/eval_jaxpr/ppermute | solution.py:12
  515.2 11.2 collective-permute-done
  527.8 12.0 %collective-permute-done = f32[8,128,128]{2,1,0:T(8,128)S(1)} collective-permute-done((f32[8,128,128]{2,1,0:T(8,128)S(1)}, f32[8,128,128]{2,1,0:T(8,128)S(1)}, u32[]{:S(2)}, u32[]{:S(2)}) %collective-permute-start) | collective-permute-done | bytes 524320 | tf_op jit(solution)/shard_map/while/body/eval_jaxpr/ppermute | solution.py:12
  541.3 11.2 collective-permute-done
  553.9 12.0 %collective-permute-done = f32[8,128,128]{2,1,0:T(8,128)S(1)} collective-permute-done((f32[8,128,128]{2,1,0:T(8,128)S(1)}, f32[8,128,128]{2,1,0:T(8,128)S(1)}, u32[]{:S(2)}, u32[]{:S(2)}) %collective-permute-start) | collective-permute-done | bytes 524320 | tf_op jit(solution)/shard_map/while/body/eval_jaxpr/ppermute | solution.py:12
  567.4 11.3 collective-permute-done
  580.1 11.3 collective-permute-done
  592.8 11.3 collective-permute-done
  605.6 11.3 collective-permute-done
  618.3 11.3 collective-permute-done
  631.0 11.3 collective-permute-done
  643.8 11.3 collective-permute-done
  656.5 11.3 collective-permute-done
  669.2 11.3 collective-permute-done
  681.9 11.3 collective-permute-done
  694.7 11.3 collective-permute-done
  707.4 11.3 collective-permute-done
  720.1 11.3 collective-permute-done
  732.9 11.3 collective-permute-done
  745.6 11.3 collective-permute-done
  758.3 11.3 collective-permute-done
  771.1 11.3 collective-permute-done
  783.8 11.3 collective-permute-done
  796.5 11.3 collective-permute-done
  809.2 11.3 collective-permute-done
  822.0 11.3 collective-permute-done
  834.7 11.3 collective-permute-done
  847.4 11.3 collective-permute-done
  864.6 214.4 %while.60 = (s32[]{:T(128)}, f32[8,128,128]{2,1,0:T(8,128)S(1)}, bf16[8,256,8,128]{1,3,2,0:T(8,128)(2,1)}, f32[8,256,128]{2,1,0:T(8,128)}, f32[8,256,128]{2,1,0:...) while((s32[]{:T(128)}, f32[8,128,128]{2,1,0:T(8,128)S(1)}, ...), condition=%wide.region_23.24_spmd.clone, body=%wide.region_10.23_spmd.clone.sunk | while | flops 674613248 | bytes 29334412 | solution.py:58
  1091.8 91.9 %all-reduce.5.cloned.1.call-done = (f32[2048,128]{1,0:T(8,128)}, f32[2048,128]{1,0:T(8,128)}) async-done(((f32[2048,128]{1,0:T(8,128)}, f32[2048,128]{1,0:T(8,128)}), (f32[2048,128]{1,0:T(8,128)}, f32[2048,128]{1,0:T(8,128)})) %all-reduce.5.cloned.1.call-update) | async-done | bytes 2097168 | tf_op jit(solution)/shard_map/psum | solution.py:119
  (739 shorter events, 455.4 us)
Async XLA Ops:
  7.2 1176.5 %all-reduce.5.cloned.1.call-start = ((), (), s32[]{:S(2)}) async-start(), calls=%async_computation | async-start | bytes 4194304 | tf_op jit(solution)/shard_map/psum | solution.py:119
  7.9 32.5 %copy-start.12 = (f32[2048]{0:T(1024)}, f32[2048]{0:T(1024)S(1)}, u32[]{:S(2)}) copy-start(f32[2048]{0:T(1024)S(1)} %fusion.83) | copy-start | bytes 24580
  63.8 2.8 collective-permute-start.1
  66.8 10.3 collective-permute-start.1
  77.2 10.5 collective-permute-start.1
  87.8 10.5 collective-permute-start.1
  98.4 10.5 collective-permute-start.1
  109.1 10.5 collective-permute-start.1
  119.7 10.5 collective-permute-start.1
  130.3 10.5 collective-permute-start.1
  140.9 10.5 collective-permute-start.1
  151.5 10.5 collective-permute-start.1
  162.2 10.5 collective-permute-start.1
  172.8 10.5 collective-permute-start.1
  183.4 10.5 collective-permute-start.1
  194.0 10.5 collective-permute-start.1
  204.6 10.5 collective-permute-start.1
  215.3 10.5 collective-permute-start.1
  225.9 10.5 collective-permute-start.1
  236.5 10.5 collective-permute-start.1
  247.1 10.5 collective-permute-start.1
  257.8 12.0 %collective-permute-start.1 = (f32[8,128,128]{2,1,0:T(8,128)S(1)}, f32[8,128,128]{2,1,0:T(8,128)S(1)}, u32[]{:S(2)}, u32[]{:S(2)}) collective-permute-start(f32[8,128,128]{2,1,0:T(8,128)S(1)} %multiply_add_fusion.5), channel_id=1, source_target_pairs={{0,4},{4,8},{8,12},{12,16},{16,20},{20,24},{24,28},{28,32},{32,36}... | collective-permute-start | bytes 1572872 | tf_op jit(solution)/shard_map/while/body/eval_jaxpr/ppermute | solution.py:12
  269.9 12.6 %collective-permute-start.1 = (f32[8,128,128]{2,1,0:T(8,128)S(1)}, f32[8,128,128]{2,1,0:T(8,128)S(1)}, u32[]{:S(2)}, u32[]{:S(2)}) collective-permute-start(f32[8,128,128]{2,1,0:T(8,128)S(1)} %multiply_add_fusion.5), channel_id=1, source_target_pairs={{0,4},{4,8},{8,12},{12,16},{16,20},{20,24},{24,28},{28,32},{32,36}... | collective-permute-start | bytes 1572872 | tf_op jit(solution)/shard_map/while/body/eval_jaxpr/ppermute | solution.py:12
  282.6 12.6 %collective-permute-start.1 = (f32[8,128,128]{2,1,0:T(8,128)S(1)}, f32[8,128,128]{2,1,0:T(8,128)S(1)}, u32[]{:S(2)}, u32[]{:S(2)}) collective-permute-start(f32[8,128,128]{2,1,0:T(8,128)S(1)} %multiply_add_fusion.5), channel_id=1, source_target_pairs={{0,4},{4,8},{8,12},{12,16},{16,20},{20,24},{24,28},{28,32},{32,36}... | collective-permute-start | bytes 1572872 | tf_op jit(solution)/shard_map/while/body/eval_jaxpr/ppermute | solution.py:12
  295.4 12.6 %collective-permute-start.1 = (f32[8,128,128]{2,1,0:T(8,128)S(1)}, f32[8,128,128]{2,1,0:T(8,128)S(1)}, u32[]{:S(2)}, u32[]{:S(2)}) collective-permute-start(f32[8,128,128]{2,1,0:T(8,128)S(1)} %multiply_add_fusion.5), channel_id=1, source_target_pairs={{0,4},{4,8},{8,12},{12,16},{16,20},{20,24},{24,28},{28,32},{32,36}... | collective-permute-start | bytes 1572872 | tf_op jit(solution)/shard_map/while/body/eval_jaxpr/ppermute | solution.py:12
  308.1 12.6 %collective-permute-start.1 = (f32[8,128,128]{2,1,0:T(8,128)S(1)}, f32[8,128,128]{2,1,0:T(8,128)S(1)}, u32[]{:S(2)}, u32[]{:S(2)}) collective-permute-start(f32[8,128,128]{2,1,0:T(8,128)S(1)} %multiply_add_fusion.5), channel_id=1, source_target_pairs={{0,4},{4,8},{8,12},{12,16},{16,20},{20,24},{24,28},{28,32},{32,36}... | collective-permute-start | bytes 1572872 | tf_op jit(solution)/shard_map/while/body/eval_jaxpr/ppermute | solution.py:12
  320.8 12.6 %collective-permute-start.1 = (f32[8,128,128]{2,1,0:T(8,128)S(1)}, f32[8,128,128]{2,1,0:T(8,128)S(1)}, u32[]{:S(2)}, u32[]{:S(2)}) collective-permute-start(f32[8,128,128]{2,1,0:T(8,128)S(1)} %multiply_add_fusion.5), channel_id=1, source_target_pairs={{0,4},{4,8},{8,12},{12,16},{16,20},{20,24},{24,28},{28,32},{32,36}... | collective-permute-start | bytes 1572872 | tf_op jit(solution)/shard_map/while/body/eval_jaxpr/ppermute | solution.py:12
  333.6 12.6 %collective-permute-start.1 = (f32[8,128,128]{2,1,0:T(8,128)S(1)}, f32[8,128,128]{2,1,0:T(8,128)S(1)}, u32[]{:S(2)}, u32[]{:S(2)}) collective-permute-start(f32[8,128,128]{2,1,0:T(8,128)S(1)} %multiply_add_fusion.5), channel_id=1, source_target_pairs={{0,4},{4,8},{8,12},{12,16},{16,20},{20,24},{24,28},{28,32},{32,36}... | collective-permute-start | bytes 1572872 | tf_op jit(solution)/shard_map/while/body/eval_jaxpr/ppermute | solution.py:12
  346.3 12.6 %collective-permute-start.1 = (f32[8,128,128]{2,1,0:T(8,128)S(1)}, f32[8,128,128]{2,1,0:T(8,128)S(1)}, u32[]{:S(2)}, u32[]{:S(2)}) collective-permute-start(f32[8,128,128]{2,1,0:T(8,128)S(1)} %multiply_add_fusion.5), channel_id=1, source_target_pairs={{0,4},{4,8},{8,12},{12,16},{16,20},{20,24},{24,28},{28,32},{32,36}... | collective-permute-start | bytes 1572872 | tf_op jit(solution)/shard_map/while/body/eval_jaxpr/ppermute | solution.py:12
  359.0 12.6 %collective-permute-start.1 = (f32[8,128,128]{2,1,0:T(8,128)S(1)}, f32[8,128,128]{2,1,0:T(8,128)S(1)}, u32[]{:S(2)}, u32[]{:S(2)}) collective-permute-start(f32[8,128,128]{2,1,0:T(8,128)S(1)} %multiply_add_fusion.5), channel_id=1, source_target_pairs={{0,4},{4,8},{8,12},{12,16},{16,20},{20,24},{24,28},{28,32},{32,36}... | collective-permute-start | bytes 1572872 | tf_op jit(solution)/shard_map/while/body/eval_jaxpr/ppermute | solution.py:12
  371.7 12.6 %collective-permute-start.1 = (f32[8,128,128]{2,1,0:T(8,128)S(1)}, f32[8,128,128]{2,1,0:T(8,128)S(1)}, u32[]{:S(2)}, u32[]{:S(2)}) collective-permute-start(f32[8,128,128]{2,1,0:T(8,128)S(1)} %multiply_add_fusion.5), channel_id=1, source_target_pairs={{0,4},{4,8},{8,12},{12,16},{16,20},{20,24},{24,28},{28,32},{32,36}... | collective-permute-start | bytes 1572872 | tf_op jit(solution)/shard_map/while/body/eval_jaxpr/ppermute | solution.py:12
  384.5 12.6 %collective-permute-start.1 = (f32[8,128,128]{2,1,0:T(8,128)S(1)}, f32[8,128,128]{2,1,0:T(8,128)S(1)}, u32[]{:S(2)}, u32[]{:S(2)}) collective-permute-start(f32[8,128,128]{2,1,0:T(8,128)S(1)} %multiply_add_fusion.5), channel_id=1, source_target_pairs={{0,4},{4,8},{8,12},{12,16},{16,20},{20,24},{24,28},{28,32},{32,36}... | collective-permute-start | bytes 1572872 | tf_op jit(solution)/shard_map/while/body/eval_jaxpr/ppermute | solution.py:12
  397.2 12.6 %collective-permute-start.1 = (f32[8,128,128]{2,1,0:T(8,128)S(1)}, f32[8,128,128]{2,1,0:T(8,128)S(1)}, u32[]{:S(2)}, u32[]{:S(2)}) collective-permute-start(f32[8,128,128]{2,1,0:T(8,128)S(1)} %multiply_add_fusion.5), channel_id=1, source_target_pairs={{0,4},{4,8},{8,12},{12,16},{16,20},{20,24},{24,28},{28,32},{32,36}... | collective-permute-start | bytes 1572872 | tf_op jit(solution)/shard_map/while/body/eval_jaxpr/ppermute | solution.py:12
  461.7 12.5 %collective-permute-start = (f32[8,128,128]{2,1,0:T(8,128)S(1)}, f32[8,128,128]{2,1,0:T(8,128)S(1)}, u32[]{:S(2)}, u32[]{:S(2)}) collective-permute-start(f32[8,128,128]{2,1,0:T(8,128)S(1)} %multiply_add_fusion.4), channel_id=1, source_target_pairs={{4,0},{8,4},{12,8},{16,12},{20,16},{24,20},{28,24},{32,28},{36,32}... | collective-permute-start | bytes 1572872 | tf_op jit(solution)/shard_map/while/body/eval_jaxpr/ppermute | solution.py:12
  474.4 13.4 %collective-permute-start = (f32[8,128,128]{2,1,0:T(8,128)S(1)}, f32[8,128,128]{2,1,0:T(8,128)S(1)}, u32[]{:S(2)}, u32[]{:S(2)}) collective-permute-start(f32[8,128,128]{2,1,0:T(8,128)S(1)} %multiply_add_fusion.4), channel_id=1, source_target_pairs={{4,0},{8,4},{12,8},{16,12},{20,16},{24,20},{28,24},{32,28},{36,32}... | collective-permute-start | bytes 1572872 | tf_op jit(solution)/shard_map/while/body/eval_jaxpr/ppermute | solution.py:12
  487.8 12.5 %collective-permute-start = (f32[8,128,128]{2,1,0:T(8,128)S(1)}, f32[8,128,128]{2,1,0:T(8,128)S(1)}, u32[]{:S(2)}, u32[]{:S(2)}) collective-permute-start(f32[8,128,128]{2,1,0:T(8,128)S(1)} %multiply_add_fusion.4), channel_id=1, source_target_pairs={{4,0},{8,4},{12,8},{16,12},{20,16},{24,20},{28,24},{32,28},{36,32}... | collective-permute-start | bytes 1572872 | tf_op jit(solution)/shard_map/while/body/eval_jaxpr/ppermute | solution.py:12
  500.4 13.4 %collective-permute-start = (f32[8,128,128]{2,1,0:T(8,128)S(1)}, f32[8,128,128]{2,1,0:T(8,128)S(1)}, u32[]{:S(2)}, u32[]{:S(2)}) collective-permute-start(f32[8,128,128]{2,1,0:T(8,128)S(1)} %multiply_add_fusion.4), channel_id=1, source_target_pairs={{4,0},{8,4},{12,8},{16,12},{20,16},{24,20},{28,24},{32,28},{36,32}... | collective-permute-start | bytes 1572872 | tf_op jit(solution)/shard_map/while/body/eval_jaxpr/ppermute | solution.py:12
  513.9 12.5 %collective-permute-start = (f32[8,128,128]{2,1,0:T(8,128)S(1)}, f32[8,128,128]{2,1,0:T(8,128)S(1)}, u32[]{:S(2)}, u32[]{:S(2)}) collective-permute-start(f32[8,128,128]{2,1,0:T(8,128)S(1)} %multiply_add_fusion.4), channel_id=1, source_target_pairs={{4,0},{8,4},{12,8},{16,12},{20,16},{24,20},{28,24},{32,28},{36,32}... | collective-permute-start | bytes 1572872 | tf_op jit(solution)/shard_map/while/body/eval_jaxpr/ppermute | solution.py:12
  526.5 13.3 %collective-permute-start = (f32[8,128,128]{2,1,0:T(8,128)S(1)}, f32[8,128,128]{2,1,0:T(8,128)S(1)}, u32[]{:S(2)}, u32[]{:S(2)}) collective-permute-start(f32[8,128,128]{2,1,0:T(8,128)S(1)} %multiply_add_fusion.4), channel_id=1, source_target_pairs={{4,0},{8,4},{12,8},{16,12},{20,16},{24,20},{28,24},{32,28},{36,32}... | collective-permute-start | bytes 1572872 | tf_op jit(solution)/shard_map/while/body/eval_jaxpr/ppermute | solution.py:12
  540.0 12.5 %collective-permute-start = (f32[8,128,128]{2,1,0:T(8,128)S(1)}, f32[8,128,128]{2,1,0:T(8,128)S(1)}, u32[]{:S(2)}, u32[]{:S(2)}) collective-permute-start(f32[8,128,128]{2,1,0:T(8,128)S(1)} %multiply_add_fusion.4), channel_id=1, source_target_pairs={{4,0},{8,4},{12,8},{16,12},{20,16},{24,20},{28,24},{32,28},{36,32}... | collective-permute-start | bytes 1572872 | tf_op jit(solution)/shard_map/while/body/eval_jaxpr/ppermute | solution.py:12
  552.6 13.3 %collective-permute-start = (f32[8,128,128]{2,1,0:T(8,128)S(1)}, f32[8,128,128]{2,1,0:T(8,128)S(1)}, u32[]{:S(2)}, u32[]{:S(2)}) collective-permute-start(f32[8,128,128]{2,1,0:T(8,128)S(1)} %multiply_add_fusion.4), channel_id=1, source_target_pairs={{4,0},{8,4},{12,8},{16,12},{20,16},{24,20},{28,24},{32,28},{36,32}... | collective-permute-start | bytes 1572872 | tf_op jit(solution)/shard_map/while/body/eval_jaxpr/ppermute | solution.py:12
  566.1 12.6 %collective-permute-start = (f32[8,128,128]{2,1,0:T(8,128)S(1)}, f32[8,128,128]{2,1,0:T(8,128)S(1)}, u32[]{:S(2)}, u32[]{:S(2)}) collective-permute-start(f32[8,128,128]{2,1,0:T(8,128)S(1)} %multiply_add_fusion.4), channel_id=1, source_target_pairs={{4,0},{8,4},{12,8},{16,12},{20,16},{24,20},{28,24},{32,28},{36,32}... | collective-permute-start | bytes 1572872 | tf_op jit(solution)/shard_map/while/body/eval_jaxpr/ppermute | solution.py:12
  578.8 12.6 %collective-permute-start = (f32[8,128,128]{2,1,0:T(8,128)S(1)}, f32[8,128,128]{2,1,0:T(8,128)S(1)}, u32[]{:S(2)}, u32[]{:S(2)}) collective-permute-start(f32[8,128,128]{2,1,0:T(8,128)S(1)} %multiply_add_fusion.4), channel_id=1, source_target_pairs={{4,0},{8,4},{12,8},{16,12},{20,16},{24,20},{28,24},{32,28},{36,32}... | collective-permute-start | bytes 1572872 | tf_op jit(solution)/shard_map/while/body/eval_jaxpr/ppermute | solution.py:12
  591.5 12.6 %collective-permute-start = (f32[8,128,128]{2,1,0:T(8,128)S(1)}, f32[8,128,128]{2,1,0:T(8,128)S(1)}, u32[]{:S(2)}, u32[]{:S(2)}) collective-permute-start(f32[8,128,128]{2,1,0:T(8,128)S(1)} %multiply_add_fusion.4), channel_id=1, source_target_pairs={{4,0},{8,4},{12,8},{16,12},{20,16},{24,20},{28,24},{32,28},{36,32}... | collective-permute-start | bytes 1572872 | tf_op jit(solution)/shard_map/while/body/eval_jaxpr/ppermute | solution.py:12
  604.3 12.6 %collective-permute-start = (f32[8,128,128]{2,1,0:T(8,128)S(1)}, f32[8,128,128]{2,1,0:T(8,128)S(1)}, u32[]{:S(2)}, u32[]{:S(2)}) collective-permute-start(f32[8,128,128]{2,1,0:T(8,128)S(1)} %multiply_add_fusion.4), channel_id=1, source_target_pairs={{4,0},{8,4},{12,8},{16,12},{20,16},{24,20},{28,24},{32,28},{36,32}... | collective-permute-start | bytes 1572872 | tf_op jit(solution)/shard_map/while/body/eval_jaxpr/ppermute | solution.py:12
  617.0 12.6 %collective-permute-start = (f32[8,128,128]{2,1,0:T(8,128)S(1)}, f32[8,128,128]{2,1,0:T(8,128)S(1)}, u32[]{:S(2)}, u32[]{:S(2)}) collective-permute-start(f32[8,128,128]{2,1,0:T(8,128)S(1)} %multiply_add_fusion.4), channel_id=1, source_target_pairs={{4,0},{8,4},{12,8},{16,12},{20,16},{24,20},{28,24},{32,28},{36,32}... | collective-permute-start | bytes 1572872 | tf_op jit(solution)/shard_map/while/body/eval_jaxpr/ppermute | solution.py:12
  629.7 12.6 %collective-permute-start = (f32[8,128,128]{2,1,0:T(8,128)S(1)}, f32[8,128,128]{2,1,0:T(8,128)S(1)}, u32[]{:S(2)}, u32[]{:S(2)}) collective-permute-start(f32[8,128,128]{2,1,0:T(8,128)S(1)} %multiply_add_fusion.4), channel_id=1, source_target_pairs={{4,0},{8,4},{12,8},{16,12},{20,16},{24,20},{28,24},{32,28},{36,32}... | collective-permute-start | bytes 1572872 | tf_op jit(solution)/shard_map/while/body/eval_jaxpr/ppermute | solution.py:12
  642.5 12.6 %collective-permute-start = (f32[8,128,128]{2,1,0:T(8,128)S(1)}, f32[8,128,128]{2,1,0:T(8,128)S(1)}, u32[]{:S(2)}, u32[]{:S(2)}) collective-permute-start(f32[8,128,128]{2,1,0:T(8,128)S(1)} %multiply_add_fusion.4), channel_id=1, source_target_pairs={{4,0},{8,4},{12,8},{16,12},{20,16},{24,20},{28,24},{32,28},{36,32}... | collective-permute-start | bytes 1572872 | tf_op jit(solution)/shard_map/while/body/eval_jaxpr/ppermute | solution.py:12
  655.2 12.6 %collective-permute-start = (f32[8,128,128]{2,1,0:T(8,128)S(1)}, f32[8,128,128]{2,1,0:T(8,128)S(1)}, u32[]{:S(2)}, u32[]{:S(2)}) collective-permute-start(f32[8,128,128]{2,1,0:T(8,128)S(1)} %multiply_add_fusion.4), channel_id=1, source_target_pairs={{4,0},{8,4},{12,8},{16,12},{20,16},{24,20},{28,24},{32,28},{36,32}... | collective-permute-start | bytes 1572872 | tf_op jit(solution)/shard_map/while/body/eval_jaxpr/ppermute | solution.py:12
  667.9 12.6 %collective-permute-start = (f32[8,128,128]{2,1,0:T(8,128)S(1)}, f32[8,128,128]{2,1,0:T(8,128)S(1)}, u32[]{:S(2)}, u32[]{:S(2)}) collective-permute-start(f32[8,128,128]{2,1,0:T(8,128)S(1)} %multiply_add_fusion.4), channel_id=1, source_target_pairs={{4,0},{8,4},{12,8},{16,12},{20,16},{24,20},{28,24},{32,28},{36,32}... | collective-permute-start | bytes 1572872 | tf_op jit(solution)/shard_map/while/body/eval_jaxpr/ppermute | solution.py:12
  680.6 12.6 %collective-permute-start = (f32[8,128,128]{2,1,0:T(8,128)S(1)}, f32[8,128,128]{2,1,0:T(8,128)S(1)}, u32[]{:S(2)}, u32[]{:S(2)}) collective-permute-start(f32[8,128,128]{2,1,0:T(8,128)S(1)} %multiply_add_fusion.4), channel_id=1, source_target_pairs={{4,0},{8,4},{12,8},{16,12},{20,16},{24,20},{28,24},{32,28},{36,32}... | collective-permute-start | bytes 1572872 | tf_op jit(solution)/shard_map/while/body/eval_jaxpr/ppermute | solution.py:12
  693.4 12.6 %collective-permute-start = (f32[8,128,128]{2,1,0:T(8,128)S(1)}, f32[8,128,128]{2,1,0:T(8,128)S(1)}, u32[]{:S(2)}, u32[]{:S(2)}) collective-permute-start(f32[8,128,128]{2,1,0:T(8,128)S(1)} %multiply_add_fusion.4), channel_id=1, source_target_pairs={{4,0},{8,4},{12,8},{16,12},{20,16},{24,20},{28,24},{32,28},{36,32}... | collective-permute-start | bytes 1572872 | tf_op jit(solution)/shard_map/while/body/eval_jaxpr/ppermute | solution.py:12
  706.1 12.6 %collective-permute-start = (f32[8,128,128]{2,1,0:T(8,128)S(1)}, f32[8,128,128]{2,1,0:T(8,128)S(1)}, u32[]{:S(2)}, u32[]{:S(2)}) collective-permute-start(f32[8,128,128]{2,1,0:T(8,128)S(1)} %multiply_add_fusion.4), channel_id=1, source_target_pairs={{4,0},{8,4},{12,8},{16,12},{20,16},{24,20},{28,24},{32,28},{36,32}... | collective-permute-start | bytes 1572872 | tf_op jit(solution)/shard_map/while/body/eval_jaxpr/ppermute | solution.py:12
  718.8 12.6 %collective-permute-start = (f32[8,128,128]{2,1,0:T(8,128)S(1)}, f32[8,128,128]{2,1,0:T(8,128)S(1)}, u32[]{:S(2)}, u32[]{:S(2)}) collective-permute-start(f32[8,128,128]{2,1,0:T(8,128)S(1)} %multiply_add_fusion.4), channel_id=1, source_target_pairs={{4,0},{8,4},{12,8},{16,12},{20,16},{24,20},{28,24},{32,28},{36,32}... | collective-permute-start | bytes 1572872 | tf_op jit(solution)/shard_map/while/body/eval_jaxpr/ppermute | solution.py:12
  731.6 12.6 %collective-permute-start = (f32[8,128,128]{2,1,0:T(8,128)S(1)}, f32[8,128,128]{2,1,0:T(8,128)S(1)}, u32[]{:S(2)}, u32[]{:S(2)}) collective-permute-start(f32[8,128,128]{2,1,0:T(8,128)S(1)} %multiply_add_fusion.4), channel_id=1, source_target_pairs={{4,0},{8,4},{12,8},{16,12},{20,16},{24,20},{28,24},{32,28},{36,32}... | collective-permute-start | bytes 1572872 | tf_op jit(solution)/shard_map/while/body/eval_jaxpr/ppermute | solution.py:12
  744.3 12.6 %collective-permute-start = (f32[8,128,128]{2,1,0:T(8,128)S(1)}, f32[8,128,128]{2,1,0:T(8,128)S(1)}, u32[]{:S(2)}, u32[]{:S(2)}) collective-permute-start(f32[8,128,128]{2,1,0:T(8,128)S(1)} %multiply_add_fusion.4), channel_id=1, source_target_pairs={{4,0},{8,4},{12,8},{16,12},{20,16},{24,20},{28,24},{32,28},{36,32}... | collective-permute-start | bytes 1572872 | tf_op jit(solution)/shard_map/while/body/eval_jaxpr/ppermute | solution.py:12
  757.0 12.6 %collective-permute-start = (f32[8,128,128]{2,1,0:T(8,128)S(1)}, f32[8,128,128]{2,1,0:T(8,128)S(1)}, u32[]{:S(2)}, u32[]{:S(2)}) collective-permute-start(f32[8,128,128]{2,1,0:T(8,128)S(1)} %multiply_add_fusion.4), channel_id=1, source_target_pairs={{4,0},{8,4},{12,8},{16,12},{20,16},{24,20},{28,24},{32,28},{36,32}... | collective-permute-start | bytes 1572872 | tf_op jit(solution)/shard_map/while/body/eval_jaxpr/ppermute | solution.py:12
  769.8 12.6 %collective-permute-start = (f32[8,128,128]{2,1,0:T(8,128)S(1)}, f32[8,128,128]{2,1,0:T(8,128)S(1)}, u32[]{:S(2)}, u32[]{:S(2)}) collective-permute-start(f32[8,128,128]{2,1,0:T(8,128)S(1)} %multiply_add_fusion.4), channel_id=1, source_target_pairs={{4,0},{8,4},{12,8},{16,12},{20,16},{24,20},{28,24},{32,28},{36,32}... | collective-permute-start | bytes 1572872 | tf_op jit(solution)/shard_map/while/body/eval_jaxpr/ppermute | solution.py:12
  782.5 12.6 %collective-permute-start = (f32[8,128,128]{2,1,0:T(8,128)S(1)}, f32[8,128,128]{2,1,0:T(8,128)S(1)}, u32[]{:S(2)}, u32[]{:S(2)}) collective-permute-start(f32[8,128,128]{2,1,0:T(8,128)S(1)} %multiply_add_fusion.4), channel_id=1, source_target_pairs={{4,0},{8,4},{12,8},{16,12},{20,16},{24,20},{28,24},{32,28},{36,32}... | collective-permute-start | bytes 1572872 | tf_op jit(solution)/shard_map/while/body/eval_jaxpr/ppermute | solution.py:12
  795.2 12.6 %collective-permute-start = (f32[8,128,128]{2,1,0:T(8,128)S(1)}, f32[8,128,128]{2,1,0:T(8,128)S(1)}, u32[]{:S(2)}, u32[]{:S(2)}) collective-permute-start(f32[8,128,128]{2,1,0:T(8,128)S(1)} %multiply_add_fusion.4), channel_id=1, source_target_pairs={{4,0},{8,4},{12,8},{16,12},{20,16},{24,20},{28,24},{32,28},{36,32}... | collective-permute-start | bytes 1572872 | tf_op jit(solution)/shard_map/while/body/eval_jaxpr/ppermute | solution.py:12
  807.9 12.6 %collective-permute-start = (f32[8,128,128]{2,1,0:T(8,128)S(1)}, f32[8,128,128]{2,1,0:T(8,128)S(1)}, u32[]{:S(2)}, u32[]{:S(2)}) collective-permute-start(f32[8,128,128]{2,1,0:T(8,128)S(1)} %multiply_add_fusion.4), channel_id=1, source_target_pairs={{4,0},{8,4},{12,8},{16,12},{20,16},{24,20},{28,24},{32,28},{36,32}... | collective-permute-start | bytes 1572872 | tf_op jit(solution)/shard_map/while/body/eval_jaxpr/ppermute | solution.py:12
  820.7 12.6 %collective-permute-start = (f32[8,128,128]{2,1,0:T(8,128)S(1)}, f32[8,128,128]{2,1,0:T(8,128)S(1)}, u32[]{:S(2)}, u32[]{:S(2)}) collective-permute-start(f32[8,128,128]{2,1,0:T(8,128)S(1)} %multiply_add_fusion.4), channel_id=1, source_target_pairs={{4,0},{8,4},{12,8},{16,12},{20,16},{24,20},{28,24},{32,28},{36,32}... | collective-permute-start | bytes 1572872 | tf_op jit(solution)/shard_map/while/body/eval_jaxpr/ppermute | solution.py:12
  833.4 12.6 %collective-permute-start = (f32[8,128,128]{2,1,0:T(8,128)S(1)}, f32[8,128,128]{2,1,0:T(8,128)S(1)}, u32[]{:S(2)}, u32[]{:S(2)}) collective-permute-start(f32[8,128,128]{2,1,0:T(8,128)S(1)} %multiply_add_fusion.4), channel_id=1, source_target_pairs={{4,0},{8,4},{12,8},{16,12},{20,16},{24,20},{28,24},{32,28},{36,32}... | collective-permute-start | bytes 1572872 | tf_op jit(solution)/shard_map/while/body/eval_jaxpr/ppermute | solution.py:12
  846.1 12.6 %collective-permute-start = (f32[8,128,128]{2,1,0:T(8,128)S(1)}, f32[8,128,128]{2,1,0:T(8,128)S(1)}, u32[]{:S(2)}, u32[]{:S(2)}) collective-permute-start(f32[8,128,128]{2,1,0:T(8,128)S(1)} %multiply_add_fusion.4), channel_id=1, source_target_pairs={{4,0},{8,4},{12,8},{16,12},{20,16},{24,20},{28,24},{32,28},{36,32}... | collective-permute-start | bytes 1572872 | tf_op jit(solution)/shard_map/while/body/eval_jaxpr/ppermute | solution.py:12
  (86 other events, 412.8 us)
Sparse Core Ops, SparseCore 0:
  1079.2 104.4 all-reduce.4
where the time goes:
time: 1200 us; the launch traced here: 1190 us
  waiting for transfers between devices  491 us (41%)
  starting transfers between devices  336 us (28%)
  local copies, waits for them, and re-layouts  159 us (13%)
  other arithmetic  98.4 us (8%)
  matrix products  93.4 us (8%)
  between operations  14.8 us (1%)
    ppermute x62, waiting for transfers between devices, from_behind(): return lax.ppermute(array, axis, pairs)  399 us
    ppermute x62, starting transfers between devices, from_behind(): return lax.ppermute(array, axis, pairs)  336 us
    psum x1, waiting for transfers between devices, shards(): grad_in, grad_out = lax.psum((grad_in, grad_out), 'tp')  91.9 us
    dot_general x16, matrix products, advance(): jnp.einsum('hij,jhp->ihp', weights, inject, preferred_element_type=jnp.fl...  40.3 us
    squeeze x32, local copies, waits for them, and re-layouts, run_groups(): lax.scan(advance, start, (x_blocks, in_blocks, out_blocks, step_blocks, d...  36.9 us
    another operation x67, other arithmetic  34.5 us
    unnamed x20, local copies, waits for them, and re-layouts  27.6 us
  transfers between devices with their start and end apart: 63, of which 63 were waited for; matrix products, arithmetic and copies ran while one was open for 1% of the time, Pallas kernels for 0%

commit v1 on v0

v1 whole, which is shorter than its diff:
```python
import jax
import jax.numpy as jnp
from jax import lax
from jax.experimental import pallas as pl
from jax.experimental.pallas import tpu as pltpu
from jax.sharding import PartitionSpec as P

L = 256
F32 = jnp.float32
BF16 = jnp.bfloat16
VMEM_LIMIT = 56 * 1024 * 1024


def mm(a, b, ca, cb):
    return lax.dot_general(a, b, (((ca,), (cb,)), ((), ())), preferred_element_type=F32)


def running(rows, reverse):
    j = lax.broadcasted_iota(jnp.int32, (L, L), 0)
    i = lax.broadcasted_iota(jnp.int32, (L, L), 1)
    tri = ((j >= i) if reverse else (j <= i)).astype(F32)
    return lax.dot_general(
        rows, tri, (((1,), (0,)), ((), ())),
        precision=lax.Precision.HIGHEST, preferred_element_type=F32,
    )


def spread(v, width):
    return jnp.concatenate(
        [jnp.broadcast_to(v[h : h + 1, :], (1, width)) for h in range(v.shape[0])], axis=1
    )


def states_kernel(
    count, x_ref, g_ref, b_ref, c_ref, step_ref, decay_ref,
    cum_ref, col_ref, s_ref, a_ref, send_ref, s_acc, a_acc, tot,
):
    heads = step_ref.shape[0]
    blocks = step_ref.shape[1] // L
    width = x_ref.shape[1] // heads
    k = pl.program_id(0)

    @pl.when(k == 0)
    def _():
        s_acc[...] = jnp.zeros_like(s_acc)
        a_acc[...] = jnp.zeros_like(a_acc)
        for n in range(blocks):
            sl = pl.ds(n * L, L)
            at = n * L + lax.broadcasted_iota(jnp.int32, (heads, L), 1)
            used = (at < count[0]).astype(F32)
            st = step_ref[:, sl] * used
            cum = running(decay_ref[:, sl] * used, False)
            cum_ref[:, sl] = cum
            total = cum[:, L - 1 :]
            tot[n] = jnp.broadcast_to(total, (heads, 128))
            rows = jnp.concatenate(
                [st, jnp.exp(cum) * used, jnp.exp(total - cum), cum, used,
                 jnp.zeros((128 - 5 * heads, L), F32)], axis=0
            )
            col_ref[sl, :] = rows.T

    s_ref[0] = s_acc[...]
    rows = pl.ds(pl.multiple_of(k * L, L), L)
    parts = []
    for h in range(heads):
        cs = slice(h * width, (h + 1) * width)
        u = (x_ref[:, cs].astype(F32) * col_ref[rows, h : h + 1]).astype(BF16)
        e = col_ref[rows, 2 * heads + h : 2 * heads + h + 1]
        parts.append((u.astype(F32) * e).astype(BF16))
    scaled = jnp.concatenate(parts, axis=1)
    s_new = spread(jnp.exp(tot[k][:, :1]), width) * s_acc[...] + mm(b_ref[...].T, scaled, 1, 0)
    s_acc[...] = s_new

    back = blocks - 1 - k
    a_ref[0] = a_acc[...]
    rows = pl.ds(pl.multiple_of(back * L, L), L)
    parts = []
    for h in range(heads):
        cs = slice(h * width, (h + 1) * width)
        e = col_ref[rows, heads + h : heads + h + 1]
        parts.append((g_ref[:, cs].astype(F32) * e).astype(BF16))
    dq = jnp.concatenate(parts, axis=1)
    a_new = spread(jnp.exp(tot[back][:, :1]), width) * a_acc[...] + mm(c_ref[...].T, dq, 1, 0)
    a_acc[...] = a_new

    @pl.when(k == blocks - 1)
    def _():
        whole = tot[0]
        for n in range(1, blocks):
            whole = whole + tot[n]
        d = jnp.exp(whole)
        n_dev = send_ref.shape[0]
        each = s_acc.shape[0] // n_dev
        for i in range(n_dev):
            send_ref[i, 2 * each] = d
            for h in range(heads):
                cs = slice(h * width, (h + 1) * width)
                send_ref[i, 0:each, h, :] = s_acc[i * each : (i + 1) * each, cs]
                send_ref[i, each : 2 * each, h, :] = a_acc[i * each : (i + 1) * each, cs]


def local_states(count, x, g, b, c, step, decay, devices):
    heads, rows = step.shape
    blocks = rows // L
    n = b.shape[1]
    wide = x.shape[1]
    each = n // devices
    fwd = lambda k: (k, 0)
    rev = lambda k: (blocks - 1 - k, 0)
    whole = lambda k: (0, 0)
    return pl.pallas_call(
        states_kernel,
        grid=(blocks,),
        in_specs=[
            pl.BlockSpec(memory_space=pltpu.SMEM),
            pl.BlockSpec((L, wide), fwd),
            pl.BlockSpec((L, wide), rev),
            pl.BlockSpec((L, n), fwd),
            pl.BlockSpec((L, n), rev),
            pl.BlockSpec((heads, rows), whole),
            pl.BlockSpec((heads, rows), whole),
        ],
        out_specs=[
            pl.BlockSpec((heads, rows), whole),
            pl.BlockSpec((rows, 128), whole),
            pl.BlockSpec((1, n, wide), lambda k: (k, 0, 0)),
            pl.BlockSpec((1, n, wide), lambda k: (blocks - 1 - k, 0, 0)),
            pl.BlockSpec((devices, 2 * each + 1, heads, 128), lambda k: (0, 0, 0, 0)),
        ],
        out_shape=[
            jax.ShapeDtypeStruct((heads, rows), F32),
            jax.ShapeDtypeStruct((rows, 128), F32),
            jax.ShapeDtypeStruct((blocks, n, wide), F32),
            jax.ShapeDtypeStruct((blocks, n, wide), F32),
            jax.ShapeDtypeStruct((devices, 2 * each + 1, heads, 128), F32),
        ],
        scratch_shapes=[
            pltpu.VMEM((n, wide), F32),
            pltpu.VMEM((n, wide), F32),
            pltpu.VMEM((blocks, heads, 128), F32),
        ],
        compiler_params=pltpu.CompilerParams(vmem_limit_bytes=VMEM_LIMIT),
        name="local_states",
    )(count, x, g, b, c, step, decay)


def scan_kernel(got_ref, out_ref):
    devices, parts = got_ref.shape[0], got_ref.shape[1]
    each = (parts - 1) // 2
    zero = jnp.zeros((each,) + got_ref.shape[2:], F32)
    s = zero
    a = zero
    for i in range(devices):
        out_ref[i, 0:each] = s
        s = got_ref[i, 2 * each][None] * s + got_ref[i, 0:each]
        r = devices - 1 - i
        out_ref[r, each : 2 * each] = a
        a = got_ref[r, 2 * each][None] * a + got_ref[r, each : 2 * each]


def scan_devices(got):
    devices, parts, heads, lanes = got.shape
    return pl.pallas_call(
        scan_kernel,
        out_shape=jax.ShapeDtypeStruct((devices, parts - 1, heads, lanes), F32),
        compiler_params=pltpu.CompilerParams(vmem_limit_bytes=VMEM_LIMIT),
        name="scan_devices",
    )(got)


def inner_kernel(x_ref, g_ref, b_ref, c_ref, cum_ref, col_ref,
                 du_ref, db_ref, dc_ref, q_ref, r_ref):
    heads = cum_ref.shape[0]
    width = x_ref.shape[1] // heads
    b = b_ref[...]
    c = c_ref[...]
    score = mm(b, c, 1, 1)
    j = lax.broadcasted_iota(jnp.int32, (L, L), 0)
    i = lax.broadcasted_iota(jnp.int32, (L, L), 1)
    keep = j <= i
    used = col_ref[:, 4 * heads : 4 * heads + 1]
    lane = lax.broadcasted_iota(jnp.int32, (L, 128), 1)
    dscore = jnp.zeros((L, L), F32)
    r_all = jnp.zeros((L, 128), F32)
    for h in range(heads):
        cs = slice(h * width, (h + 1) * width)
        dy = (g_ref[:, cs].astype(F32) * used).astype(BF16)
        u = (x_ref[:, cs].astype(F32) * col_ref[:, h : h + 1]).astype(BF16)
        gap = cum_ref[h : h + 1, :] - col_ref[:, 3 * heads + h : 3 * heads + h + 1]
        fade = jnp.exp(jnp.where(keep, gap, -1e30))
        w = (fade * score).astype(BF16)
        dw = mm(u, dy, 1, 1)
        dscore = dscore + dw * fade
        prod = dw * w.astype(F32)
        q_ref[h : h + 1, :] = jnp.sum(prod, axis=0, keepdims=True)
        r_all = jnp.where(lane == h, jnp.sum(prod, axis=1, keepdims=True), r_all)
        du_ref[:, cs] = mm(w, dy, 1, 0).astype(BF16)
    r_ref[...] = r_all
    ds = dscore.astype(BF16)
    db_ref[...] = mm(ds, c, 1, 0)
    dc_ref[...] = mm(ds.T, b, 1, 0)


def within(x, g, b, c, cum, col):
    heads, rows = cum.shape
    blocks = rows // L
    n = b.shape[1]
    wide = x.shape[1]
    fwd = lambda k: (k, 0)
    return pl.pallas_call(
        inner_kernel,
        grid=(blocks,),
        in_specs=[
            pl.BlockSpec((L, wide), fwd),
            pl.BlockSpec((L, wide), fwd),
            pl.BlockSpec((L, n), fwd),
            pl.BlockSpec((L, n), fwd),
            pl.BlockSpec((heads, L), lambda k: (0, k)),
            pl.BlockSpec((L, 128), fwd),
        ],
        out_specs=[
            pl.BlockSpec((L, wide), fwd),
            pl.BlockSpec((L, n), fwd),
            pl.BlockSpec((L, n), fwd),
            pl.BlockSpec((heads, L), lambda k: (0, k)),
            pl.BlockSpec((L, 128), fwd),
        ],
        out_shape=[
            jax.ShapeDtypeStruct((rows, wide), BF16),
            jax.ShapeDtypeStruct((rows, n), F32),
            jax.ShapeDtypeStruct((rows, n), F32),
            jax.ShapeDtypeStruct((heads, rows), F32),
            jax.ShapeDtypeStruct((rows, 128), F32),
        ],
        compiler_params=pltpu.CompilerParams(vmem_limit_bytes=VMEM_LIMIT),
        name="within_blocks",
    )(x, g, b, c, cum, col)


def outer_kernel(count, gain, x_ref, g_ref, b_ref, c_ref, cum_ref, col_ref, s_ref, a_ref, got_ref,
                 du_ref, db1_ref, dc1_ref, q_ref, r_ref,
                 dx_ref, db_ref, dc_ref, dstep_ref, ddecay_ref, s0, a0):
    heads = cum_ref.shape[0]
    blocks = cum_ref.shape[1] // L
    width = x_ref.shape[1] // heads
    n = b_ref.shape[1]
    k = pl.program_id(0)
    each = got_ref.shape[1] // 2

    @pl.when(k == 0)
    def _():
        for h in range(heads):
            cs = slice(h * width, (h + 1) * width)
            s0[:, cs] = got_ref[:, 0:each, h, :].reshape(n, width)
            a0[:, cs] = got_ref[:, each : 2 * each, h, :].reshape(n, width)

    before = jnp.zeros((heads, 1), F32)
    after = jnp.zeros((heads, 1), F32)
    own = jnp.zeros((heads, 1), F32)
    for m in range(blocks):
        t = cum_ref[:, m * L + L - 1 : m * L + L]
        before = before + jnp.where(m < k, t, 0.0)
        after = after + jnp.where(m > k, t, 0.0)
        own = own + jnp.where(m == k, t, 0.0)
    state = s_ref[0] + spread(jnp.exp(before), width) * s0[...]
    adj = a_ref[0] + spread(jnp.exp(after), width) * a0[...]
    state_h = state.astype(BF16)
    adj_h = adj.astype(BF16)
    b = b_ref[...]
    c = c_ref[...]
    carried = mm(c, state_h, 1, 0)
    dscaled = mm(b, adj_h, 1, 0)
    used = col_ref[:, 4 * heads : 4 * heads + 1]
    lane = lax.broadcasted_iota(jnp.int32, (L, 128), 1)
    packed = -r_ref[...]
    dqs, scs = [], []
    inflow = []
    fed = []
    for h in range(heads):
        cs = slice(h * width, (h + 1) * width)
        st = col_ref[:, h : h + 1]
        e = col_ref[:, heads + h : heads + h + 1]
        tail = col_ref[:, 2 * heads + h : 2 * heads + h + 1]
        x = x_ref[:, cs].astype(F32)
        g = g_ref[:, cs].astype(F32)
        dq = g * e
        dqs.append(dq.astype(BF16))
        u = (x * st).astype(BF16).astype(F32)
        sc = u * tail
        scs.append(sc.astype(BF16))
        ds = dscaled[:, cs]
        out = sc * ds
        local = dq * carried[:, cs] - out
        fed.append(jnp.sum(out, axis=0, keepdims=True))
        du = du_ref[:, cs].astype(F32) + ds * tail
        dx_ref[:, cs] = ((gain[h] * used) * g + du * st).astype(BF16)
        q2 = jnp.sum(local, axis=1, keepdims=True)
        dst = jnp.sum(x * du, axis=1, keepdims=True)
        packed = jnp.where(lane == h, packed + q2, packed)
        packed = jnp.where(lane == heads + h, dst, packed)
        inflow.append(jnp.sum(adj[:, cs] * state[:, cs], axis=0, keepdims=True))
    dq_all = jnp.concatenate(dqs, axis=1)
    sc_all = jnp.concatenate(scs, axis=1)
    dc_ref[...] = dc1_ref[...] + mm(dq_all, state_h, 1, 1)
    db_ref[...] = db1_ref[...] + mm(sc_all, adj_h, 1, 1)
    flow = jnp.sum(jnp.concatenate(inflow, axis=0), axis=1, keepdims=True) * jnp.exp(own)
    flow = flow + jnp.sum(jnp.concatenate(fed, axis=0), axis=1, keepdims=True)
    rows = packed.T
    at = k * L + lax.broadcasted_iota(jnp.int32, (heads, L), 1)
    live = (at < count[0]).astype(F32)
    dcum = rows[0:heads] + q_ref[...]
    ddecay_ref[...] = (running(dcum, True) + flow) * live
    dstep_ref[...] = rows[heads : 2 * heads] * live


def across(count, gain, x, g, b, c, cum, col, s, a, got, du, db1, dc1, q, r):
    heads, rows = cum.shape
    blocks = rows // L
    n = b.shape[1]
    wide = x.shape[1]
    fwd = lambda k: (k, 0)
    side = lambda k: (0, k)
    return pl.pallas_call(
        outer_kernel,
        grid=(blocks,),
        in_specs=[
            pl.BlockSpec(memory_space=pltpu.SMEM),
            pl.BlockSpec(memory_space=pltpu.SMEM),
            pl.BlockSpec((L, wide), fwd),
            pl.BlockSpec((L, wide), fwd),
            pl.BlockSpec((L, n), fwd),
            pl.BlockSpec((L, n), fwd),
            pl.BlockSpec((heads, rows), lambda k: (0, 0)),
            pl.BlockSpec((L, 128), fwd),
            pl.BlockSpec((1, n, wide), lambda k: (k, 0, 0)),
            pl.BlockSpec((1, n, wide), lambda k: (k, 0, 0)),
            pl.BlockSpec(got.shape, lambda k: (0, 0, 0, 0)),
            pl.BlockSpec((L, wide), fwd),
            pl.BlockSpec((L, n), fwd),
            pl.BlockSpec((L, n), fwd),
            pl.BlockSpec((heads, L), side),
            pl.BlockSpec((L, 128), fwd),
        ],
        out_specs=[
            pl.BlockSpec((L, wide), fwd),
            pl.BlockSpec((L, n), fwd),
            pl.BlockSpec((L, n), fwd),
            pl.BlockSpec((heads, L), side),
            pl.BlockSpec((heads, L), side),
        ],
        out_shape=[
            jax.ShapeDtypeStruct((rows, wide), BF16),
            jax.ShapeDtypeStruct((rows, n), F32),
            jax.ShapeDtypeStruct((rows, n), F32),
            jax.ShapeDtypeStruct((heads, rows), F32),
            jax.ShapeDtypeStruct((heads, rows), F32),
        ],
        scratch_shapes=[pltpu.VMEM((n, wide), F32), pltpu.VMEM((n, wide), F32)],
        compiler_params=pltpu.CompilerParams(vmem_limit_bytes=VMEM_LIMIT),
        name="across_blocks",
    )(count, gain, x, g, b, c, cum, col, s, a, got, du, db1, dc1, q, r)


def total_over_tp(first, second):
    up = [(i, (i + 1) % 4) for i in range(4)]
    down = [(i, (i + 3) % 4) for i in range(4)]
    me = lax.axis_index("tp")
    rows, n = first.shape
    one = first.reshape(4, rows // 4, n)
    two = second.reshape(4, rows // 4, n)
    pick = lambda v, k: lax.dynamic_index_in_dim(v, (me + k) % 4, 0, keepdims=False)
    send = lambda v, way: lax.ppermute(v, "tp", way)
    a1 = send(pick(one, 2), up)
    b1 = send(pick(two, 2), down)
    a2 = send(pick(one, 3), down)
    b2 = send(pick(two, 1), up)
    a3 = send(a1 + pick(one, 1), up)
    b3 = send(b1 + pick(two, 3), down)
    ra = pick(one, 0) + a2 + a3
    rb = pick(two, 0) + b2 + b3
    ga1, gb1 = send(ra, up), send(rb, down)
    ga2, gb2 = send(ra, down), send(rb, up)
    ga3, gb3 = send(ga1, up), send(gb1, down)

    def whole(own, from_below, from_above, far):
        out = jnp.zeros((4,) + own.shape, F32)
        for k, v in ((0, own), (3, from_below), (1, from_above), (2, far)):
            out = lax.dynamic_update_index_in_dim(out, v, (me + k) % 4, 0)
        return out.reshape(rows, n)

    return whole(ra, ga1, ga2, ga3), whole(rb, gb2, gb1, gb3)


def shards(x, b, c, step, decay, gain, count, g):
    devices = lax.axis_size("ctx")
    cum, col, s, a, send = local_states(count, x, g, b, c, step, decay, devices)
    got = lax.all_to_all(send, "ctx", 0, 0, tiled=True)
    du, db1, dc1, q, r = within(x, g, b, c, cum, col)
    out = scan_devices(got)
    got = lax.all_to_all(out, "ctx", 0, 0, tiled=True)
    dx, db, dc, dstep, ddecay = across(
        count, gain, x, g, b, c, cum, col, s, a, got, du, db1, dc1, q, r
    )
    db, dc = total_over_tp(db, dc)
    return dx, db, dc, dstep, ddecay


def solution(mesh):
    placed = (
        P("ctx", "tp"), P("ctx", None), P("ctx", None), P("tp", "ctx"),
        P("tp", "ctx"), P("tp"), P("ctx"), P("ctx", "tp"),
    )
    return jax.shard_map(
        shards,
        mesh=mesh,
        in_specs=placed,
        out_specs=(P("ctx", "tp"), P("ctx", None), P("ctx", None), P("tp", "ctx"), P("tp", "ctx")),
        check_vma=False,
    )
```

time: 1200 us -> 147 us (0.12)
  waiting for transfers between devices: 491 us -> 23.9 us
  starting transfers between devices: 336 us -> 19 us
  local copies, waits for them, and re-layouts: 159 us -> 4.33 us
  other arithmetic: 98.4 us -> 3.97 us
  matrix products: 93.4 us -> 0 us
  Pallas kernels: 0 us -> 66.1 us
  blocking collectives: 0 us -> 27.4 us
  between operations: 14.8 us -> 1.46 us
    ppermute x62 -> x12, waiting for transfers between devices: 399 us -> 23.9 us  [total_over_tp(): send = lambda v, way: lax.ppermute(v, 'tp', way)]
    ppermute x62 -> x12, starting transfers between devices: 336 us -> 15 us  [total_over_tp(): send = lambda v, way: lax.ppermute(v, 'tp', way)]
    dot_general x90 -> x0, matrix products: 93.4 us -> none  [the longest x16 40.3 us: advance(): jnp.einsum('hij,jhp->ihp', weights, inject, preferred_element_type=jnp.fl...]
    psum x1 -> x0, waiting for transfers between devices: 91.9 us -> none  [shards(): grad_in, grad_out = lax.psum((grad_in, grad_out), 'tp')]
    pallas_call x0 -> x4, Pallas kernels: none -> 66.1 us  [the longest x1 26.2 us: across(): pl.pallas_call(outer_kernel, grid=(blocks,), in_specs=[pl.BlockSpec(memor...]
    squeeze x32 -> x2, local copies, waits for them, and re-layouts: 36.9 us -> 2.14 us  [total_over_tp(): lax.dynamic_index_in_dim(v, (me + k) % 4, 0, keepdims=False)]
    another operation x67 -> x0, other arithmetic: 34.5 us -> none
    all_to_all x0 -> x1, blocking collectives: none -> 27.4 us  [shards(): got = lax.all_to_all(send, 'ctx', 0, 0, tiled=True)]
  transfers between devices with their start and end apart: 63 -> 13, of which waited for: 63 -> 9; matrix products, arithmetic and copies ran while one was open for 1% -> 4% of each run, Pallas kernels for 0% -> 15%
where the time goes in v1:
time: 147 us; the launch traced here: 146 us
  Pallas kernels  66.1 us (45%)
  blocking collectives  27.4 us (19%)
  waiting for transfers between devices  23.9 us (16%)
  starting transfers between devices  19 us (13%)
  local copies, waits for them, and re-layouts  4.33 us (3%)
  other arithmetic  3.97 us (3%)
    all_to_all x1, blocking collectives, shards(): got = lax.all_to_all(send, 'ctx', 0, 0, tiled=True)  27.4 us
    pallas_call x1, Pallas kernels, across(): pl.pallas_call(outer_kernel, grid=(blocks,), in_specs=[pl.BlockSpec(memor...  26.2 us
    ppermute x12, waiting for transfers between devices, total_over_tp(): send = lambda v, way: lax.ppermute(v, 'tp', way)  23.9 us
    pallas_call x1, Pallas kernels, within(): pl.pallas_call(inner_kernel, grid=(blocks,), in_specs=[pl.BlockSpec((L, w...  21.3 us
    pallas_call x1, Pallas kernels, local_states(): pl.pallas_call(states_kernel, grid=(blocks,), in_specs=[pl.BlockSpec(memo...  16.3 us
    ppermute x12, starting transfers between devices, total_over_tp(): send = lambda v, way: lax.ppermute(v, 'tp', way)  15 us
    all_to_all x1, starting transfers between devices, shards(): got = lax.all_to_all(out, 'ctx', 0, 0, tiled=True)  3.93 us
  transfers between devices with their start and end apart: 13, of which 9 were waited for; matrix products, arithmetic and copies ran while one was open for 4% of the time, Pallas kernels for 15%

profile of v1, /device:TPU:0, one launch (start us, length us, event | category | flops | bytes accessed | tf_op | source)
XLA Modules:
  0.0 146.1 jit_solution(4252282217226556299)
XLA Ops:
  1.3 16.3 %local_states.1 = (f32[8,2048]{1,0:T(8,128)}, f32[2048,128]{1,0:T(8,128)}, f32[8,128,1024]{2,1,0:T(8,128)}, f32[8,128,1024]{2,1,0:T(8,128)}, f32[32,9,8,128]{3,2,1,0:T(8,128)}) custom-call(s32[1]{0:T(128)S(6)} %copy.21.count, bf16[2048,1024]{1,0:T(8,128)(2,1)} %x_ref.5, bf16[2048,1024]{1,0:T(8,128)(2,1)} %g_ref.5, bf16[2048,128]{1,0:T(8,128)(2,1)} %b_ref.5, ...), custom_call_target="tpu_custom_call" | custom-call | tf_op jit(solution)/shard_map/local_states/pallas_call | solution.py:111
  17.6 27.4 %all_to_all.10.got_ref = f32[32,9,8,128]{3,2,1,0:T(8,128)} all-to-all(f32[32,9,8,128]{3,2,1,0:T(8,128)} %get-tuple-element.24), channel_id=1, replica_groups=mesh['ctx'=32,'tp'=4] {'ctx'}, dimensions={0} | all-to-all | bytes 2359296 | tf_op jit(solution)/shard_map/all_to_all | solution.py:397
  45.0 2.3 %scan_devices.1 = f32[32,8,8,128]{3,2,1,0:T(8,128)} custom-call(f32[32,9,8,128]{3,2,1,0:T(8,128)} %all_to_all.10.got_ref), custom_call_target="tpu_custom_call" | custom-call | tf_op jit(solution)/shard_map/scan_devices/pallas_call | solution.py:163
  47.3 3.9 %all-to-all-start.1 = ((f32[32,8,8,128]{3,2,1,0:T(8,128)}), f32[32,8,8,128]{3,2,1,0:T(8,128)S(1)}, u32[]{:S(2)}, u32[]{:S(2)}) async-start(f32[32,8,8,128]{3,2,1,0:T(8,128)} %scan_devices.1), calls=%async_computation.1 | async-start | bytes 2097152 | tf_op jit(solution)/shard_map/all_to_all | solution.py:400
  51.2 21.3 %within_blocks.1 = (bf16[2048,1024]{1,0:T(8,128)(2,1)}, f32[2048,128]{1,0:T(8,128)}, f32[2048,128]{1,0:T(8,128)}, f32[8,2048]{1,0:T(8,128)}, f32[2048,128]{1,0:T(8,128)}) custom-call(bf16[2048,1024]{1,0:T(8,128)(2,1)} %x_ref.5, bf16[2048,1024]{1,0:T(8,128)(2,1)} %g_ref.5, bf16[2048,128]{1,0:T(8,128)(2,1)} %b_ref.5, bf16[2048,128]{1,0:T(8,128)(2,1)} %c_ref.5, ...), custom_call_target="tpu_custom_call" | custom-call | tf_op jit(solution)/shard_map/within_blocks/pallas_call | solution.py:210
  72.5 0.0 all-to-all-done.1.got_ref
  72.5 0.0 copy-start
  72.5 1.0 copy-done
  73.5 26.2 %across_blocks.1 = (bf16[2048,1024]{1,0:T(8,128)(2,1)}, f32[2048,128]{1,0:T(8,128)}, f32[2048,128]{1,0:T(8,128)}, f32[8,2048]{1,0:T(8,128)}, f32[8,2048]{1,0:T(8,128)}) custom-call(s32[1]{0:T(128)S(6)} %copy.21.count, f32[8]{0:T(128)} %gain.1, bf16[2048,1024]{1,0:T(8,128)(2,1)} %x_ref.5, bf16[2048,1024]{1,0:T(8,128)(2,1)} %g_ref.5, bf16[2048,128]{1,0:T(8,128)(2,1)} %b_ref.5, ...), custom_call_target="tpu_custom_call" | custom-call | tf_op jit(solution)/shard_map/across_blocks/pallas_call | solution.py:323
  99.7 1.1 dynamic-slice_bitcast_fusion.3
  100.8 1.6 %collective-permute-start.1 = (f32[512,128]{1,0:T(8,128)S(1)}, f32[512,128]{1,0:T(8,128)S(1)}, u32[]{:S(2)}, u32[]{:S(2)}) collective-permute-start(f32[512,128]{1,0:T(8,128)S(1)} %get-tuple-element.42), channel_id=1, source_target_pairs={{0,1},{1,2},{2,3},{3,0},{4,5},{5,6},{6,7},{7,4},{8,9},{9,10},{10,1... | collective-permute-start | bytes 786440 | tf_op jit(solution)/shard_map/ppermute | solution.py:372
  102.5 1.1 dynamic-slice_bitcast_fusion.1
  103.5 1.7 %collective-permute-start.7 = (f32[512,128]{1,0:T(8,128)S(1)}, f32[512,128]{1,0:T(8,128)S(1)}, u32[]{:S(2)}, u32[]{:S(2)}) collective-permute-start(f32[512,128]{1,0:T(8,128)S(1)} %get-tuple-element.40), channel_id=1, source_target_pairs={{0,3},{1,0},{2,1},{3,2},{4,7},{5,4},{6,5},{7,6},{8,11},{9,8},{10,9... | collective-permute-start | bytes 786440 | tf_op jit(solution)/shard_map/ppermute | solution.py:372
  105.3 1.8 %collective-permute-start = (f32[512,128]{1,0:T(8,128)S(1)}, f32[512,128]{1,0:T(8,128)S(1)}, u32[]{:S(2)}, u32[]{:S(2)}) collective-permute-start(f32[512,128]{1,0:T(8,128)S(1)} %get-tuple-element.41), channel_id=1, source_target_pairs={{0,3},{1,0},{2,1},{3,2},{4,7},{5,4},{6,5},{7,6},{8,11},{9,8},{10,9... | collective-permute-start | bytes 786440 | tf_op jit(solution)/shard_map/ppermute | solution.py:372
  107.1 3.5 %collective-permute-done.1 = f32[512,128]{1,0:T(8,128)S(1)} collective-permute-done((f32[512,128]{1,0:T(8,128)S(1)}, f32[512,128]{1,0:T(8,128)S(1)}, u32[]{:S(2)}, u32[]{:S(2)}) %collective-permute-start.1) | collective-permute-done | bytes 262176 | tf_op jit(solution)/shard_map/ppermute | solution.py:372
  110.5 1.0 bitcast_add_fusion.2
  111.5 0.4 collective-permute-start.2
  111.9 1.6 %collective-permute-start.6 = (f32[512,128]{1,0:T(8,128)S(1)}, f32[512,128]{1,0:T(8,128)S(1)}, u32[]{:S(2)}, u32[]{:S(2)}) collective-permute-start(f32[512,128]{1,0:T(8,128)S(1)} %get-tuple-element.39), channel_id=1, source_target_pairs={{0,1},{1,2},{2,3},{3,0},{4,5},{5,6},{6,7},{7,4},{8,9},{9,10},{10,1... | collective-permute-start | bytes 786440 | tf_op jit(solution)/shard_map/ppermute | solution.py:372
  113.5 0.0 collective-permute-done.7
  113.5 1.0 bitcast_add_fusion
  114.5 2.3 %collective-permute-start.8 = (f32[512,128]{1,0:T(8,128)S(1)}, f32[512,128]{1,0:T(8,128)S(1)}, u32[]{:S(2)}, u32[]{:S(2)}) collective-permute-start(f32[512,128]{1,0:T(8,128)S(1)} %bitcast_add_fusion), channel_id=1, source_target_pairs={{0,3},{1,0},{2,1},{3,2},{4,7},{5,4},{6,5},{7,6},{8,11},{9,8},{10,9... | collective-permute-start | bytes 786440 | tf_op jit(solution)/shard_map/ppermute | solution.py:372
  116.7 1.7 %collective-permute-done = f32[512,128]{1,0:T(8,128)S(1)} collective-permute-done((f32[512,128]{1,0:T(8,128)S(1)}, f32[512,128]{1,0:T(8,128)S(1)}, u32[]{:S(2)}, u32[]{:S(2)}) %collective-permute-start) | collective-permute-done | bytes 262176 | tf_op jit(solution)/shard_map/ppermute | solution.py:372
  118.4 3.6 %collective-permute-done.2 = f32[512,128]{1,0:T(8,128)S(1)} collective-permute-done((f32[512,128]{1,0:T(8,128)S(1)}, f32[512,128]{1,0:T(8,128)S(1)}, u32[]{:S(2)}, u32[]{:S(2)}) %collective-permute-start.2) | collective-permute-done | bytes 262176 | tf_op jit(solution)/shard_map/ppermute | solution.py:372
  122.0 0.1 broadcast.7.clone
  122.1 1.0 bitcast_dynamic-update-slice_fusion.7
  123.1 0.1 collective-permute-start.3
  123.2 4.5 %collective-permute-done.6 = f32[512,128]{1,0:T(8,128)S(1)} collective-permute-done((f32[512,128]{1,0:T(8,128)S(1)}, f32[512,128]{1,0:T(8,128)S(1)}, u32[]{:S(2)}, u32[]{:S(2)}) %collective-permute-start.6) | collective-permute-done | bytes 262176 | tf_op jit(solution)/shard_map/ppermute | solution.py:372
  127.7 0.0 collective-permute-done.8
  127.7 0.1 broadcast.7.clone.1
  127.7 1.0 bitcast_dynamic-update-slice_fusion.3
  128.7 0.6 collective-permute-start.10
  129.3 1.5 %collective-permute-start.9 = (f32[512,128]{1,0:T(8,128)S(1)}, f32[512,128]{1,0:T(8,128)S(1)}, u32[]{:S(2)}, u32[]{:S(2)}) collective-permute-start(f32[512,128]{1,0:T(8,128)S(1)} %get-tuple-element.36), channel_id=1, source_target_pairs={{0,1},{1,2},{2,3},{3,0},{4,5},{5,6},{6,7},{7,4},{8,9},{9,10},{10,1... | collective-permute-start | bytes 786440 | tf_op jit(solution)/shard_map/ppermute | solution.py:372
  130.8 1.7 %collective-permute-start.4 = (f32[512,128]{1,0:T(8,128)S(1)}, f32[512,128]{1,0:T(8,128)S(1)}, u32[]{:S(2)}, u32[]{:S(2)}) collective-permute-start(f32[512,128]{1,0:T(8,128)S(1)} %get-tuple-element.38), channel_id=1, source_target_pairs={{0,3},{1,0},{2,1},{3,2},{4,7},{5,4},{6,5},{7,6},{8,11},{9,8},{10,9... | collective-permute-start | bytes 786440 | tf_op jit(solution)/shard_map/ppermute | solution.py:372
  132.6 1.1 collective-permute-done.3
  133.6 0.0 collective-permute-start.5
  133.6 4.4 %collective-permute-done.10 = f32[512,128]{1,0:T(8,128)S(1)} collective-permute-done((f32[512,128]{1,0:T(8,128)S(1)}, f32[512,128]{1,0:T(8,128)S(1)}, u32[]{:S(2)}, u32[]{:S(2)}) %collective-permute-start.10) | collective-permute-done | bytes 262176 | tf_op jit(solution)/shard_map/ppermute | solution.py:372
  138.0 1.7 %collective-permute-start.11 = (f32[512,128]{1,0:T(8,128)S(1)}, f32[512,128]{1,0:T(8,128)S(1)}, u32[]{:S(2)}, u32[]{:S(2)}) collective-permute-start(f32[512,128]{1,0:T(8,128)S(1)} %collective-permute-done.10), channel_id=1, source_target_pairs={{0,3},{1,0},{2,1},{3,2},{4,7},{5,4},{6,5},{7,6},{8,11},{9,8},{10,9... | collective-permute-start | bytes 786440 | tf_op jit(solution)/shard_map/ppermute | solution.py:372
  139.8 0.0 collective-permute-done.9
  139.9 2.4 %collective-permute-done.4 = f32[512,128]{1,0:T(8,128)S(1)} collective-permute-done((f32[512,128]{1,0:T(8,128)S(1)}, f32[512,128]{1,0:T(8,128)S(1)}, u32[]{:S(2)}, u32[]{:S(2)}) %collective-permute-start.4) | collective-permute-done | bytes 262176 | tf_op jit(solution)/shard_map/ppermute | solution.py:372
  142.3 0.6 collective-permute-done.5
  142.9 0.0 copy-start.2
  142.9 2.2 %collective-permute-done.11 = f32[512,128]{1,0:T(8,128)S(1)} collective-permute-done((f32[512,128]{1,0:T(8,128)S(1)}, f32[512,128]{1,0:T(8,128)S(1)}, u32[]{:S(2)}, u32[]{:S(2)}) %collective-permute-start.11) | collective-permute-done | bytes 262176 | tf_op jit(solution)/shard_map/ppermute | solution.py:372
  145.1 0.0 copy-start.1
  145.1 0.0 copy-done.2
  145.1 1.0 copy-done.1
  (6 shorter events, 0.1 us)
Async XLA Ops:
  47.3 25.2 %all-to-all-start.1 = ((f32[32,8,8,128]{3,2,1,0:T(8,128)}), f32[32,8,8,128]{3,2,1,0:T(8,128)S(1)}, u32[]{:S(2)}, u32[]{:S(2)}) async-start(f32[32,8,8,128]{3,2,1,0:T(8,128)} %scan_devices.1), calls=%async_computation.1 | async-start | bytes 2097152 | tf_op jit(solution)/shard_map/all_to_all | solution.py:400
  72.5 1.0 copy-start
  100.8 9.7 %collective-permute-start.1 = (f32[512,128]{1,0:T(8,128)S(1)}, f32[512,128]{1,0:T(8,128)S(1)}, u32[]{:S(2)}, u32[]{:S(2)}) collective-permute-start(f32[512,128]{1,0:T(8,128)S(1)} %get-tuple-element.42), channel_id=1, source_target_pairs={{0,1},{1,2},{2,3},{3,0},{4,5},{5,6},{6,7},{7,4},{8,9},{9,10},{10,1... | collective-permute-start | bytes 786440 | tf_op jit(solution)/shard_map/ppermute | solution.py:372
  103.5 9.9 %collective-permute-start.7 = (f32[512,128]{1,0:T(8,128)S(1)}, f32[512,128]{1,0:T(8,128)S(1)}, u32[]{:S(2)}, u32[]{:S(2)}) collective-permute-start(f32[512,128]{1,0:T(8,128)S(1)} %get-tuple-element.40), channel_id=1, source_target_pairs={{0,3},{1,0},{2,1},{3,2},{4,7},{5,4},{6,5},{7,6},{8,11},{9,8},{10,9... | collective-permute-start | bytes 786440 | tf_op jit(solution)/shard_map/ppermute | solution.py:372
  105.3 13.1 %collective-permute-start = (f32[512,128]{1,0:T(8,128)S(1)}, f32[512,128]{1,0:T(8,128)S(1)}, u32[]{:S(2)}, u32[]{:S(2)}) collective-permute-start(f32[512,128]{1,0:T(8,128)S(1)} %get-tuple-element.41), channel_id=1, source_target_pairs={{0,3},{1,0},{2,1},{3,2},{4,7},{5,4},{6,5},{7,6},{8,11},{9,8},{10,9... | collective-permute-start | bytes 786440 | tf_op jit(solution)/shard_map/ppermute | solution.py:372
  111.5 10.5 %collective-permute-start.2 = (f32[512,128]{1,0:T(8,128)S(1)}, f32[512,128]{1,0:T(8,128)S(1)}, u32[]{:S(2)}, u32[]{:S(2)}) collective-permute-start(f32[512,128]{1,0:T(8,128)S(1)} %bitcast_add_fusion.2), channel_id=1, source_target_pairs={{0,1},{1,2},{2,3},{3,0},{4,5},{5,6},{6,7},{7,4},{8,9},{9,10},{10,1... | collective-permute-start | bytes 786440 | tf_op jit(solution)/shard_map/ppermute | solution.py:372
  111.9 15.8 %collective-permute-start.6 = (f32[512,128]{1,0:T(8,128)S(1)}, f32[512,128]{1,0:T(8,128)S(1)}, u32[]{:S(2)}, u32[]{:S(2)}) collective-permute-start(f32[512,128]{1,0:T(8,128)S(1)} %get-tuple-element.39), channel_id=1, source_target_pairs={{0,1},{1,2},{2,3},{3,0},{4,5},{5,6},{6,7},{7,4},{8,9},{9,10},{10,1... | collective-permute-start | bytes 786440 | tf_op jit(solution)/shard_map/ppermute | solution.py:372
  114.5 13.2 %collective-permute-start.8 = (f32[512,128]{1,0:T(8,128)S(1)}, f32[512,128]{1,0:T(8,128)S(1)}, u32[]{:S(2)}, u32[]{:S(2)}) collective-permute-start(f32[512,128]{1,0:T(8,128)S(1)} %bitcast_add_fusion), channel_id=1, source_target_pairs={{0,3},{1,0},{2,1},{3,2},{4,7},{5,4},{6,5},{7,6},{8,11},{9,8},{10,9... | collective-permute-start | bytes 786440 | tf_op jit(solution)/shard_map/ppermute | solution.py:372
  123.1 10.5 %collective-permute-start.3 = (f32[512,128]{1,0:T(8,128)S(1)}, f32[512,128]{1,0:T(8,128)S(1)}, u32[]{:S(2)}, u32[]{:S(2)}) collective-permute-start(f32[512,128]{1,0:T(8,128)S(1)} %get-tuple-element.38), channel_id=1, source_target_pairs={{0,1},{1,2},{2,3},{3,0},{4,5},{5,6},{6,7},{7,4},{8,9},{9,10},{10,1... | collective-permute-start | bytes 786440 | tf_op jit(solution)/shard_map/ppermute | solution.py:372
  128.7 9.3 %collective-permute-start.10 = (f32[512,128]{1,0:T(8,128)S(1)}, f32[512,128]{1,0:T(8,128)S(1)}, u32[]{:S(2)}, u32[]{:S(2)}) collective-permute-start(f32[512,128]{1,0:T(8,128)S(1)} %get-tuple-element.36), channel_id=1, source_target_pairs={{0,3},{1,0},{2,1},{3,2},{4,7},{5,4},{6,5},{7,6},{8,11},{9,8},{10,9... | collective-permute-start | bytes 786440 | tf_op jit(solution)/shard_map/ppermute | solution.py:372
  129.3 10.5 %collective-permute-start.9 = (f32[512,128]{1,0:T(8,128)S(1)}, f32[512,128]{1,0:T(8,128)S(1)}, u32[]{:S(2)}, u32[]{:S(2)}) collective-permute-start(f32[512,128]{1,0:T(8,128)S(1)} %get-tuple-element.36), channel_id=1, source_target_pairs={{0,1},{1,2},{2,3},{3,0},{4,5},{5,6},{6,7},{7,4},{8,9},{9,10},{10,1... | collective-permute-start | bytes 786440 | tf_op jit(solution)/shard_map/ppermute | solution.py:372
  130.8 11.5 %collective-permute-start.4 = (f32[512,128]{1,0:T(8,128)S(1)}, f32[512,128]{1,0:T(8,128)S(1)}, u32[]{:S(2)}, u32[]{:S(2)}) collective-permute-start(f32[512,128]{1,0:T(8,128)S(1)} %get-tuple-element.38), channel_id=1, source_target_pairs={{0,3},{1,0},{2,1},{3,2},{4,7},{5,4},{6,5},{7,6},{8,11},{9,8},{10,9... | collective-permute-start | bytes 786440 | tf_op jit(solution)/shard_map/ppermute | solution.py:372
  133.6 9.2 %collective-permute-start.5 = (f32[512,128]{1,0:T(8,128)S(1)}, f32[512,128]{1,0:T(8,128)S(1)}, u32[]{:S(2)}, u32[]{:S(2)}) collective-permute-start(f32[512,128]{1,0:T(8,128)S(1)} %collective-permute-done.3), channel_id=1, source_target_pairs={{0,1},{1,2},{2,3},{3,0},{4,5},{5,6},{6,7},{7,4},{8,9},{9,10},{10,1... | collective-permute-start | bytes 786440 | tf_op jit(solution)/shard_map/ppermute | solution.py:372
  138.0 7.1 %collective-permute-start.11 = (f32[512,128]{1,0:T(8,128)S(1)}, f32[512,128]{1,0:T(8,128)S(1)}, u32[]{:S(2)}, u32[]{:S(2)}) collective-permute-start(f32[512,128]{1,0:T(8,128)S(1)} %collective-permute-done.10), channel_id=1, source_target_pairs={{0,3},{1,0},{2,1},{3,2},{4,7},{5,4},{6,5},{7,6},{8,11},{9,8},{10,9... | collective-permute-start | bytes 786440 | tf_op jit(solution)/shard_map/ppermute | solution.py:372
  142.9 2.2 %copy-start.2 = (f32[4,512,128]{2,1,0:T(8,128)}, f32[4,512,128]{2,1,0:T(8,128)S(1)}, u32[]{:S(2)}) copy-start(f32[4,512,128]{2,1,0:T(8,128)S(1)} %bitcast_dynamic-update-slice_fusion.4) | copy-start | bytes 3145732
  145.1 1.0 copy-start.1

commit v2 on v1

v2 whole, which is shorter than its diff:
```python
import jax
import jax.numpy as jnp
from jax import lax
from jax.experimental import pallas as pl
from jax.experimental.pallas import tpu as pltpu
from jax.sharding import PartitionSpec as P

L = 256
F32 = jnp.float32
BF16 = jnp.bfloat16
FIRST, SECOND = 4, 2
VMEM_LIMIT = 56 * 1024 * 1024


def mm(a, b, ca, cb):
    return lax.dot_general(a, b, (((ca,), (cb,)), ((), ())), preferred_element_type=F32)


def running(rows, reverse):
    j = lax.broadcasted_iota(jnp.int32, (L, L), 0)
    i = lax.broadcasted_iota(jnp.int32, (L, L), 1)
    tri = ((j >= i) if reverse else (j <= i)).astype(F32)
    return lax.dot_general(
        rows, tri, (((1,), (0,)), ((), ())),
        precision=lax.Precision.HIGHEST, preferred_element_type=F32,
    )


def spread(v, width):
    return jnp.concatenate(
        [jnp.broadcast_to(v[h : h + 1, :], (1, width)) for h in range(v.shape[0])], axis=1
    )


def faded(ref, by):
    heads = by.shape[1]
    width = ref.shape[1] // heads
    return jnp.concatenate(
        [
            (ref[:, h * width : (h + 1) * width].astype(F32) * by[:, h : h + 1]).astype(BF16)
            for h in range(heads)
        ],
        axis=1,
    )


def states_kernel(
    count, x_ref, g_ref, b_ref, c_ref, step_ref, decay_ref,
    cum_ref, col_ref, s_ref, a_ref, send_ref, s_acc, a_acc, tot,
):
    heads = step_ref.shape[0]
    blocks = step_ref.shape[1] // L
    width = x_ref.shape[1] // heads
    k = pl.program_id(0)

    @pl.when(k == 0)
    def _():
        s_acc[...] = jnp.zeros_like(s_acc)
        a_acc[...] = jnp.zeros_like(a_acc)
        lives = []
        for n in range(blocks):
            at = n * L + lax.broadcasted_iota(jnp.int32, (heads, L), 1)
            lives.append((at < count[0]).astype(F32))
        sums = running(
            jnp.concatenate(
                [decay_ref[:, n * L : (n + 1) * L] * lives[n] for n in range(blocks)], axis=0
            ),
            False,
        )
        for n in range(blocks):
            sl = pl.ds(n * L, L)
            used = lives[n]
            st = step_ref[:, sl] * used
            cum = sums[n * heads : (n + 1) * heads]
            cum_ref[:, sl] = cum
            total = cum[:, L - 1 :]
            tot[n] = jnp.broadcast_to(total, (heads, 128))
            rows = jnp.concatenate(
                [st, jnp.exp(cum) * used, jnp.exp(total - cum) * st, cum, used,
                 jnp.zeros((128 - 5 * heads, L), F32)], axis=0
            )
            col_ref[sl, :] = rows.T

    s_ref[0] = s_acc[...].astype(BF16)
    rows = pl.ds(pl.multiple_of(k * L, L), L)
    sc = faded(x_ref, col_ref[rows, 2 * heads : 3 * heads])
    s_acc[...] = spread(jnp.exp(tot[k][:, :1]), width) * s_acc[...] + mm(
        b_ref[...].T, sc, 1, 0
    )

    back = blocks - 1 - k
    a_ref[0] = a_acc[...].astype(BF16)
    rows = pl.ds(pl.multiple_of(back * L, L), L)
    dq = faded(g_ref, col_ref[rows, heads : 2 * heads])
    a_acc[...] = spread(jnp.exp(tot[back][:, :1]), width) * a_acc[...] + mm(
        c_ref[...].T, dq, 1, 0
    )

    @pl.when(k == blocks - 1)
    def _():
        whole = tot[0]
        for n in range(1, blocks):
            whole = whole + tot[n]
        d = jnp.exp(whole)
        n_dev = send_ref.shape[0]
        each = s_acc.shape[0] // n_dev
        wide = s_acc.shape[1]
        for i in range(n_dev):
            send_ref[i, 0:each, 0:wide] = s_acc[i * each : (i + 1) * each, :]
            send_ref[i, each : 2 * each, 0:wide] = a_acc[i * each : (i + 1) * each, :]
            send_ref[i, :, wide:] = d


def local_states(count, x, g, b, c, step, decay, devices):
    heads, rows = step.shape
    blocks = rows // L
    n = b.shape[1]
    wide = x.shape[1]
    each = n // devices
    fwd = lambda k: (k, 0)
    rev = lambda k: (blocks - 1 - k, 0)
    whole = lambda k: (0, 0)
    return pl.pallas_call(
        states_kernel,
        grid=(blocks,),
        in_specs=[
            pl.BlockSpec(memory_space=pltpu.SMEM),
            pl.BlockSpec((L, wide), fwd),
            pl.BlockSpec((L, wide), rev),
            pl.BlockSpec((L, n), fwd),
            pl.BlockSpec((L, n), rev),
            pl.BlockSpec((heads, rows), whole),
            pl.BlockSpec((heads, rows), whole),
        ],
        out_specs=[
            pl.BlockSpec((heads, rows), whole),
            pl.BlockSpec((rows, 128), whole),
            pl.BlockSpec((1, n, wide), lambda k: (k, 0, 0)),
            pl.BlockSpec((1, n, wide), lambda k: (blocks - 1 - k, 0, 0)),
            pl.BlockSpec((devices, 2 * each, wide + 128), lambda k: (0, 0, 0)),
        ],
        out_shape=[
            jax.ShapeDtypeStruct((heads, rows), F32),
            jax.ShapeDtypeStruct((rows, 128), F32),
            jax.ShapeDtypeStruct((blocks, n, wide), BF16),
            jax.ShapeDtypeStruct((blocks, n, wide), BF16),
            jax.ShapeDtypeStruct((devices, 2 * each, wide + 128), F32),
        ],
        scratch_shapes=[
            pltpu.VMEM((n, wide), F32),
            pltpu.VMEM((n, wide), F32),
            pltpu.VMEM((blocks, heads, 128), F32),
        ],
        compiler_params=pltpu.CompilerParams(vmem_limit_bytes=VMEM_LIMIT),
        name="local_states",
    )(count, x, g, b, c, step, decay)


def scan_kernel(got_ref, out_ref):
    devices, both, wide = out_ref.shape
    each = both // 2
    heads = got_ref.shape[1]
    width = wide // heads

    def fade(i):
        d = got_ref[i, :, wide:]
        return jnp.concatenate(
            [jnp.broadcast_to(d[h : h + 1, :width], (each, width)) for h in range(heads)], axis=1
        )

    s = jnp.zeros((each, wide), F32)
    a = jnp.zeros((each, wide), F32)
    for i in range(devices):
        out_ref[i, 0:each, :] = s
        s = fade(i) * s + got_ref[i, 0:each, 0:wide]
        r = devices - 1 - i
        out_ref[r, each:both, :] = a
        a = fade(r) * a + got_ref[r, each:both, 0:wide]


def scan_devices(got):
    devices, both, lanes = got.shape
    return pl.pallas_call(
        scan_kernel,
        out_shape=jax.ShapeDtypeStruct((devices, both, lanes - 128), F32),
        compiler_params=pltpu.CompilerParams(vmem_limit_bytes=VMEM_LIMIT),
        name="scan_devices",
    )(got)


def inner_kernel(gain, x_ref, g_ref, b_ref, c_ref, cum_ref, col_ref,
                 *rest):
    dx_ref, db_ref, dc_ref, q_ref, r_ref = rest[-5:]
    heads = cum_ref.shape[0]
    width = x_ref.shape[1] // heads
    b = b_ref[...]
    c = c_ref[...]
    score = mm(b, c, 1, 1)
    j = lax.broadcasted_iota(jnp.int32, (L, L), 0)
    i = lax.broadcasted_iota(jnp.int32, (L, L), 1)
    keep = j <= i
    used = col_ref[:, 4 * heads : 4 * heads + 1]
    lane = lax.broadcasted_iota(jnp.int32, (L, 128), 1)
    dscore = jnp.zeros((L, L), F32)
    r_all = jnp.zeros((L, 128), F32)
    for h in range(heads):
        cs = slice(h * width, (h + 1) * width)
        live_g = g_ref[:, cs].astype(F32) * used
        dy = live_g.astype(BF16)
        x = x_ref[:, cs].astype(F32)
        st = col_ref[:, h : h + 1]
        u = (x * st).astype(BF16)
        gap = cum_ref[h : h + 1, :] - col_ref[:, 3 * heads + h : 3 * heads + h + 1]
        fade = jnp.exp(jnp.where(keep, gap, -1e30))
        w = (fade * score).astype(BF16)
        dw = mm(u, dy, 1, 1)
        dscore = dscore + dw * fade
        prod = dw * w.astype(F32)
        q_ref[h : h + 1, :] = jnp.sum(prod, axis=0, keepdims=True)
        du = mm(w, dy, 1, 0)
        dx_ref[:, cs] = (gain[h] * live_g + du * st).astype(BF16)
        r_all = jnp.where(lane == 2 * heads + h, jnp.sum(prod, axis=1, keepdims=True), r_all)
        r_all = jnp.where(lane == 3 * heads + h, jnp.sum(x * du, axis=1, keepdims=True), r_all)
    r_ref[...] = r_all
    ds = dscore.astype(BF16)
    db_ref[...] = mm(ds, c, 1, 0)
    dc_ref[...] = mm(ds.T, b, 1, 0)


def within(gain, x, g, b, c, cum, col, first, blocks, earlier):
    heads = cum.shape[0]
    n = b.shape[1]
    wide = x.shape[1]
    rows = x.shape[0]
    at = lambda k: (first + k, 0)
    return pl.pallas_call(
        inner_kernel,
        grid=(blocks,),
        in_specs=[
            pl.BlockSpec(memory_space=pltpu.SMEM),
            pl.BlockSpec((L, wide), at),
            pl.BlockSpec((L, wide), at),
            pl.BlockSpec((L, n), at),
            pl.BlockSpec((L, n), at),
            pl.BlockSpec((heads, L), lambda k: (0, first + k)),
            pl.BlockSpec((L, 128), at),
        ] + [pl.BlockSpec(memory_space=pl.ANY)] * len(earlier),
        out_specs=[
            pl.BlockSpec((L, wide), at),
            pl.BlockSpec((L, n), at),
            pl.BlockSpec((L, n), at),
            pl.BlockSpec((heads, L), lambda k: (0, first + k)),
            pl.BlockSpec((L, 128), at),
        ],
        out_shape=[
            jax.ShapeDtypeStruct((rows, wide), BF16),
            jax.ShapeDtypeStruct((rows, n), F32),
            jax.ShapeDtypeStruct((rows, n), F32),
            jax.ShapeDtypeStruct((heads, rows), F32),
            jax.ShapeDtypeStruct((rows, 128), F32),
        ],
        input_output_aliases={7 + i: i for i in range(len(earlier))},
        compiler_params=pltpu.CompilerParams(vmem_limit_bytes=VMEM_LIMIT),
        name="within_blocks",
    )(gain, x, g, b, c, cum, col, *earlier)


def basis_kernel(me, cum_ref, s_ref, a_ref, x_ref, g_ref, col_ref, got_ref, db1_ref, dc1_ref,
                 state_ref, adj_ref, flow_ref, up_ref, down_ref, mid_ref, own_ref, s0, a0):
    heads = cum_ref.shape[0]
    blocks = cum_ref.shape[1] // L
    n, wide = s0.shape
    width = wide // heads
    k = pl.program_id(0)
    each = got_ref.shape[1] // 2

    @pl.when(k == 0)
    def _():
        for i in range(got_ref.shape[0]):
            s0[i * each : (i + 1) * each, :] = got_ref[i, 0:each, :]
            a0[i * each : (i + 1) * each, :] = got_ref[i, each : 2 * each, :]

    before = jnp.zeros((heads, 1), F32)
    after = jnp.zeros((heads, 1), F32)
    own = jnp.zeros((heads, 1), F32)
    for m in range(blocks):
        t = cum_ref[:, m * L + L - 1 : m * L + L]
        before = before + jnp.where(m < k, t, 0.0)
        after = after + jnp.where(m > k, t, 0.0)
        own = own + jnp.where(m == k, t, 0.0)
    state = s_ref[0].astype(F32) + spread(jnp.exp(before), width) * s0[...]
    adj = a_ref[0].astype(F32) + spread(jnp.exp(after), width) * a0[...]
    state_h = state.astype(BF16)
    adj_h = adj.astype(BF16)
    state_ref[0] = state_h
    adj_ref[0] = adj_h
    dc = dc1_ref[...] + mm(faded(g_ref, col_ref[:, heads : 2 * heads]), state_h, 1, 1)
    db = db1_ref[...] + mm(faded(x_ref, col_ref[:, 2 * heads : 3 * heads]), adj_h, 1, 1)
    inflow = jnp.concatenate(
        [
            jnp.sum(
                adj[:, h * width : (h + 1) * width] * state[:, h * width : (h + 1) * width],
                axis=0, keepdims=True,
            )
            for h in range(heads)
        ],
        axis=0,
    )
    flow = jnp.sum(inflow, axis=1, keepdims=True) * jnp.exp(own)
    flow_ref[0] = jnp.broadcast_to(flow, (heads, 128))

    per = blocks // 4
    turn = lax.rem(lax.div(k, per) - me[0] + 4, 4)
    at = pl.ds(pl.multiple_of(lax.rem(k, per) * L, L), L)

    @pl.when(turn == 0)
    def _():
        own_ref[0, at, :] = db
        own_ref[1, at, :] = dc

    @pl.when(turn == 1)
    def _():
        mid_ref[0, at, :] = db
        up_ref[1, at, :] = dc

    @pl.when(turn == 2)
    def _():
        up_ref[0, at, :] = db
        down_ref[0, at, :] = dc

    @pl.when(turn == 3)
    def _():
        down_ref[1, at, :] = db
        mid_ref[1, at, :] = dc


def basis_grads(me, cum, s, a, x, g, col, got, db1, dc1):
    heads, rows = cum.shape
    n, wide = s.shape[1:]
    blocks = rows // L
    at = lambda k: (k, 0)
    layer = pl.BlockSpec((1, n, wide), lambda k: (k, 0, 0))
    pair = pl.BlockSpec((2, rows // 4, n), lambda k: (0, 0, 0))

    return pl.pallas_call(
        basis_kernel,
        grid=(blocks,),
        in_specs=[
            pl.BlockSpec(memory_space=pltpu.SMEM),
            pl.BlockSpec((heads, rows), lambda k: (0, 0)),
            layer,
            layer,
            pl.BlockSpec((L, wide), at),
            pl.BlockSpec((L, wide), at),
            pl.BlockSpec((L, 128), at),
            pl.BlockSpec(got.shape, lambda k: (0, 0, 0)),
            pl.BlockSpec((L, n), at),
            pl.BlockSpec((L, n), at),
        ],
        out_specs=[layer, layer, pl.BlockSpec((1, heads, 128), lambda k: (k, 0, 0)),
                   pair, pair, pair, pair],
        out_shape=[
            jax.ShapeDtypeStruct((blocks, n, wide), BF16),
            jax.ShapeDtypeStruct((blocks, n, wide), BF16),
            jax.ShapeDtypeStruct((blocks, heads, 128), F32),
        ] + [jax.ShapeDtypeStruct((2, rows // 4, n), F32)] * 4,
        scratch_shapes=[pltpu.VMEM((n, wide), F32), pltpu.VMEM((n, wide), F32)],
        compiler_params=pltpu.CompilerParams(vmem_limit_bytes=VMEM_LIMIT),
        name="basis_grads",
    )(me, cum, s, a, x, g, col, got, db1, dc1)


def row_kernel(first, count, x_ref, b_ref, c_ref, cum_ref, step_ref, col_ref, g_ref,
               state_ref, adj_ref, flow_ref, dx1_ref, q_ref, r_ref, *rest):
    dx_ref, dstep_ref, ddecay_ref = rest[-3:]
    heads = cum_ref.shape[0]
    width = x_ref.shape[1] // heads
    k = first + pl.program_id(0)
    carried = mm(c_ref[...], state_ref[0], 1, 0)
    fed = mm(b_ref[...], adj_ref[0], 1, 0)
    lane = lax.broadcasted_iota(jnp.int32, (L, 128), 1)
    packed = r_ref[...]
    for h in range(heads):
        cs = slice(h * width, (h + 1) * width)
        ts = col_ref[:, 2 * heads + h : 2 * heads + h + 1]
        ds = fed[:, cs]
        dx_ref[:, cs] = (dx1_ref[:, cs].astype(F32) + ds * ts).astype(BF16)
        a = jnp.sum(x_ref[:, cs].astype(F32) * ds, axis=1, keepdims=True)
        q = jnp.sum(g_ref[:, cs].astype(F32) * carried[:, cs], axis=1, keepdims=True)
        packed = jnp.where(lane == h, a, packed)
        packed = jnp.where(lane == heads + h, q, packed)
    rows = packed.T
    at = k * L + lax.broadcasted_iota(jnp.int32, (heads, L), 1)
    live = (at < count[0]).astype(F32)
    cum = cum_ref[...]
    more = jnp.exp(cum[:, L - 1 :] - cum) * rows[0:heads]
    mine = step_ref[...] * live * more
    flow = flow_ref[0][:, :1] + jnp.sum(mine, axis=1, keepdims=True)
    paid = jnp.exp(cum) * live * rows[heads : 2 * heads]
    dcum = q_ref[...] + paid - rows[2 * heads : 3 * heads] - mine
    ddecay_ref[...] = (running(dcum, True) + flow) * live
    dstep_ref[...] = (rows[3 * heads : 4 * heads] + more) * live


def row_grads(first, blocks, count, x, b, c, cum, step, col, g, state, adj, flow, dx1, q, r, earlier):
    heads, rows = cum.shape
    n = b.shape[1]
    wide = x.shape[1]
    at = lambda k: (first + k, 0)
    side = lambda k: (0, first + k)
    layer = pl.BlockSpec((1, n, wide), lambda k: (first + k, 0, 0))
    args = [count, x, b, c, cum, step, col, g, state, adj, flow, dx1, q, r]
    specs = [
        pl.BlockSpec(memory_space=pltpu.SMEM),
        pl.BlockSpec((L, wide), at),
        pl.BlockSpec((L, n), at),
        pl.BlockSpec((L, n), at),
        pl.BlockSpec((heads, L), side),
        pl.BlockSpec((heads, L), side),
        pl.BlockSpec((L, 128), at),
        pl.BlockSpec((L, wide), at),
        layer,
        layer,
        pl.BlockSpec((1, heads, 128), lambda k: (first + k, 0, 0)),
        pl.BlockSpec((L, wide), at),
        pl.BlockSpec((heads, L), lambda k: (0, first + k)),
        pl.BlockSpec((L, 128), at),
    ]
    alias = {}
    for i, v in enumerate(earlier):
        alias[len(args)] = i
        args.append(v)
        specs.append(pl.BlockSpec(memory_space=pl.ANY))

    def kernel(*refs):
        row_kernel(first, *refs)

    return pl.pallas_call(
        kernel,
        grid=(blocks,),
        in_specs=specs,
        out_specs=[
            pl.BlockSpec((L, wide), at),
            pl.BlockSpec((heads, L), side),
            pl.BlockSpec((heads, L), side),
        ],
        out_shape=[
            jax.ShapeDtypeStruct((rows, wide), BF16),
            jax.ShapeDtypeStruct((heads, rows), F32),
            jax.ShapeDtypeStruct((heads, rows), F32),
        ],
        input_output_aliases=alias,
        compiler_params=pltpu.CompilerParams(vmem_limit_bytes=VMEM_LIMIT),
        name="row_grads",
    )(*args)


def up(v):
    return lax.ppermute(v, "tp", [(i, (i + 1) % 4) for i in range(4)])


def down(v):
    return lax.ppermute(v, "tp", [(i, (i + 3) % 4) for i in range(4)])


def shards(x, b, c, step, decay, gain, count, g):
    devices = lax.axis_size("ctx")
    blocks = x.shape[0] // L
    me = lax.axis_index("tp")
    mine = me.astype(jnp.int32).reshape(1)
    cum, col, s, a, send = local_states(count, x, g, b, c, step, decay, devices)
    got = lax.all_to_all(send, "ctx", 0, 0, tiled=True)
    inner = within(gain, x, g, b, c, cum, col, 0, blocks // 2, ())
    got, inner = lax.optimization_barrier((got, inner))
    out = scan_devices(got)
    got = lax.all_to_all(out, "ctx", 0, 0, tiled=True)
    inner = within(gain, x, g, b, c, cum, col, blocks // 2, blocks // 2, inner)
    got, inner = lax.optimization_barrier((got, inner))
    dx1, db1, dc1, q, r = inner
    state, adj, flow, up1, down1, mid, own = basis_grads(
        mine, cum, s, a, x, g, col, got, db1, dc1
    )
    rows = lambda first, number, state, before: row_grads(
        first, number, count, x, b, c, cum, step, col, g, state, adj, flow, dx1, q, r, before
    )
    u, d = up(up1), down(down1)
    done = rows(0, FIRST, state, ())
    u, d, state, done = lax.optimization_barrier((u, d, state, done))
    p, w = up(u[0] + mid[0]), down(d[0] + mid[1])
    done = rows(FIRST, SECOND, state, done)
    p, w, state, done = lax.optimization_barrier((p, w, state, done))
    own = jnp.stack([own[0] + d[1] + p, own[1] + u[1] + w])
    below, above = up(own), down(own)
    done = rows(FIRST + SECOND, blocks - FIRST - SECOND, state, done)
    below, above, done = lax.optimization_barrier((below, above, done))
    dx, dstep, ddecay = done
    far = (up(below[0]), down(above[1]))
    db = jnp.zeros((4, b.shape[0] // 4, b.shape[1]), F32)
    dc = db
    for k, v in ((0, own), (3, below), (1, above), (2, far)):
        at = ((me + k) % 4, 0, 0)
        db = lax.dynamic_update_slice(db, v[0][None], at)
        dc = lax.dynamic_update_slice(dc, v[1][None], at)
    return dx, db.reshape(b.shape), dc.reshape(c.shape), dstep, ddecay


def solution(mesh):
    placed = (
        P("ctx", "tp"), P("ctx", None), P("ctx", None), P("tp", "ctx"),
        P("tp", "ctx"), P("tp"), P("ctx"), P("ctx", "tp"),
    )
    return jax.shard_map(
        shards,
        mesh=mesh,
        in_specs=placed,
        out_specs=(P("ctx", "tp"), P("ctx", None), P("ctx", None), P("tp", "ctx"), P("tp", "ctx")),
        check_vma=False,
    )
```

time: 147 us -> 133 us (0.905)
  blocking collectives: 27.4 us -> 0 us
  Pallas kernels: 66.1 us -> 75.4 us
  starting transfers between devices: 19 us -> 25.1 us
  other arithmetic: 3.97 us -> 0.98 us
  waiting for transfers between devices: 23.9 us -> 26.3 us
    all_to_all x1 -> x0, blocking collectives: 27.4 us -> none  [shards(): got = lax.all_to_all(send, 'ctx', 0, 0, tiled=True)]
    pallas_call x3 -> x7, Pallas kernels: 49.8 us -> 62.3 us  [the longest x2 26.5 us: within(): pl.pallas_call(inner_kernel, grid=(blocks,), in_specs=[pl.BlockSpec(memor...]
    all_to_all x0 -> x1, starting transfers between devices: none -> 8.25 us  [shards(): got = lax.all_to_all(send, 'ctx', 0, 0, tiled=True)]
    ppermute x12 -> x8, waiting for transfers between devices: 23.9 us -> 16.4 us  [the longest x4 12.5 us: up(): return lax.ppermute(v, 'tp', [(i, (i + 1) % 4) for i in range(4)])]
    all_to_all x0 -> x1, waiting for transfers between devices: none -> 5.78 us  [shards(): got = lax.all_to_all(send, 'ctx', 0, 0, tiled=True)]
    all_to_all x1, waiting for transfers between devices: 0.01 us -> 4.1 us  [shards(): got = lax.all_to_all(out, 'ctx', 0, 0, tiled=True)]
    pallas_call x1, Pallas kernels: 16.3 us -> 13 us  [local_states(): pl.pallas_call(states_kernel, grid=(blocks,), in_specs=[pl.BlockSpec(memo...]
    ppermute x12 -> x8, starting transfers between devices: 15 us -> 12.9 us  [the longest x4 8.63 us: down(): return lax.ppermute(v, 'tp', [(i, (i + 3) % 4) for i in range(4)])]
  transfers between devices with their start and end apart: 13 -> 10, of which waited for: 9 -> 6; matrix products, arithmetic and copies ran while one was open for 4% -> 0% of each run, Pallas kernels for 15% -> 35%
where the time goes in v2:
time: 133 us; the launch traced here: 132 us
  Pallas kernels  75.4 us (57%)
  waiting for transfers between devices  26.3 us (20%)
  starting transfers between devices  25.1 us (19%)
  local copies, waits for them, and re-layouts  3.22 us (2%)
  between operations  1.42 us (1%)
    pallas_call x2, Pallas kernels, within(): pl.pallas_call(inner_kernel, grid=(blocks,), in_specs=[pl.BlockSpec(memor...  26.5 us
    pallas_call x3, Pallas kernels, row_grads(): pl.pallas_call(kernel, grid=(blocks,), in_specs=specs, out_specs=[pl.Bloc...  19.7 us
    pallas_call x1, Pallas kernels, basis_grads(): pl.pallas_call(basis_kernel, grid=(blocks,), in_specs=[pl.BlockSpec(memor...  13.7 us
    pallas_call x1, Pallas kernels, local_states(): pl.pallas_call(states_kernel, grid=(blocks,), in_specs=[pl.BlockSpec(memo...  13 us
    ppermute x4, waiting for transfers between devices, up(): return lax.ppermute(v, 'tp', [(i, (i + 1) % 4) for i in range(4)])  12.5 us
    ppermute x4, starting transfers between devices, down(): return lax.ppermute(v, 'tp', [(i, (i + 3) % 4) for i in range(4)])  8.63 us
    all_to_all x1, starting transfers between devices, shards(): got = lax.all_to_all(send, 'ctx', 0, 0, tiled=True)  8.25 us
    all_to_all x1, waiting for transfers between devices, shards(): got = lax.all_to_all(send, 'ctx', 0, 0, tiled=True)  5.78 us
  transfers between devices with their start and end apart: 10, of which 6 were waited for; matrix products, arithmetic and copies ran while one was open for 0% of the time, Pallas kernels for 35%

profile of v2, /device:TPU:0, one launch (start us, length us, event | category | flops | bytes accessed | tf_op | source)
XLA Modules:
  0.0 132.4 jit_solution(8439617187182559934)
XLA Ops:
  1.3 13.0 %local_states.1 = (f32[8,2048]{1,0:T(8,128)}, f32[2048,128]{1,0:T(8,128)}, bf16[8,128,1024]{2,1,0:T(8,128)(2,1)}, bf16[8,128,1024]{2,1,0:T(8,128)(2,1)}, f32[32,8,1152]{2,1,0:T(8,128)}) custom-call(s32[1]{0:T(128)S(6)} %copy.43.count.refs_0_, bf16[2048,1024]{1,0:T(8,128)(2,1)} %refs_1_.5, bf16[2048,1024]{1,0:T(8,128)(2,1)} %refs_7_.5, ...), custom_call_target="tpu_custom_call" | custom-call | tf_op jit(solution)/shard_map/local_states/pallas_call | solution.py:123
  14.3 8.3 %all-to-all-start = ((f32[32,8,1152]{2,1,0:T(8,128)}), f32[32,8,1152]{2,1,0:T(8,128)S(1)}, u32[]{:S(2)}, u32[]{:S(2)}) async-start(f32[32,8,1152]{2,1,0:T(8,128)} %get-tuple-element.69), calls=%async_computation | async-start | bytes 2359296 | tf_op jit(solution)/shard_map/all_to_all | solution.py:472
  22.6 13.2 %within_blocks.2 = (bf16[2048,1024]{1,0:T(8,128)(2,1)}, f32[2048,128]{1,0:T(8,128)}, f32[2048,128]{1,0:T(8,128)}, f32[8,2048]{1,0:T(8,128)}, f32[2048,128]{1,0:T(8,128)}) custom-call(f32[8]{0:T(128)} %gain.3, bf16[2048,1024]{1,0:T(8,128)(2,1)} %refs_1_.5, bf16[2048,1024]{1,0:T(8,128)(2,1)} %refs_7_.5, bf16[2048,128]{1,0:T(8,128)(2,1)} %refs_2_.5, ...), custom_call_target="tpu_custom_call" | custom-call | tf_op jit(solution)/shard_map/within_blocks/pallas_call | solution.py:236
  35.8 5.8 %all-to-all-done.got_ref = f32[32,8,1152]{2,1,0:T(8,128)S(1)} async-done(((f32[32,8,1152]{2,1,0:T(8,128)}), f32[32,8,1152]{2,1,0:T(8,128)S(1)}, u32[]{:S(2)}, u32[]{:S(2)}) %all-to-all-start) | async-done | bytes 1179680 | tf_op jit(solution)/shard_map/all_to_all | solution.py:472
  41.6 0.0 copy-start
  41.6 1.0 copy-done
  42.6 2.6 %scan_devices.1 = f32[32,8,1024]{2,1,0:T(8,128)} custom-call(f32[32,8,1152]{2,1,0:T(8,128)} %copy-done), custom_call_target="tpu_custom_call" | custom-call | tf_op jit(solution)/shard_map/scan_devices/pallas_call | solution.py:183
  45.1 3.9 %all-to-all-start.1 = ((f32[32,8,1024]{2,1,0:T(8,128)}), f32[32,8,1024]{2,1,0:T(8,128)S(1)}, u32[]{:S(2)}, u32[]{:S(2)}) async-start(f32[32,8,1024]{2,1,0:T(8,128)} %scan_devices.1), calls=%async_computation.1 | async-start | bytes 2097152 | tf_op jit(solution)/shard_map/all_to_all | solution.py:476
  49.1 13.2 %within_blocks.3 = (bf16[2048,1024]{1,0:T(8,128)(2,1)}, f32[2048,128]{1,0:T(8,128)}, f32[2048,128]{1,0:T(8,128)}, f32[8,2048]{1,0:T(8,128)}, f32[2048,128]{1,0:T(8,128)}) custom-call(f32[8]{0:T(128)} %gain.3, bf16[2048,1024]{1,0:T(8,128)(2,1)} %refs_1_.5, ...), custom_call_target="tpu_custom_call", output_to_operand_aliasing={{0}: (7, {}), {1}: (8, {}), {2}: (9, {}), {3}: (10, {}), {4... | custom-call | tf_op jit(solution)/shard_map/within_blocks/pallas_call | solution.py:236
  62.3 4.1 %all-to-all-done.1.got_ref = f32[32,8,1024]{2,1,0:T(8,128)S(1)} async-done(((f32[32,8,1024]{2,1,0:T(8,128)}), f32[32,8,1024]{2,1,0:T(8,128)S(1)}, u32[]{:S(2)}, u32[]{:S(2)}) %all-to-all-start.1) | async-done | bytes 1048608 | tf_op jit(solution)/shard_map/all_to_all | solution.py:476
  66.4 0.0 copy-start.1
  66.4 1.0 copy-done.1
  67.4 13.7 %basis_grads.1 = (bf16[8,128,1024]{2,1,0:T(8,128)(2,1)}, bf16[8,128,1024]{2,1,0:T(8,128)(2,1)}, f32[8,8,128]{2,1,0:T(8,128)}, f32[2,512,128]{2,1,0:T(8,128)}, f3...) custom-call(s32[1]{0:T(128)} %bitcast.me, f32[8,2048]{1,0:T(8,128)} %get-tuple-element.65.cum_ref.refs_4_, ...), custom_call_target="tpu_custom_call" | custom-call | tf_op jit(solution)/shard_map/basis_grads/pallas_call | solution.py:345
  81.0 1.7 %collective-permute-start = (f32[2,512,128]{2,1,0:T(8,128)}, f32[2,512,128]{2,1,0:T(8,128)S(1)}, u32[]{:S(2)}, u32[]{:S(2)}) collective-permute-start(f32[2,512,128]{2,1,0:T(8,128)} %get-tuple-element.90), channel_id=1, source_target_pairs={{0,1},{1,2},{2,3},{3,0},{4,5},{5,6},{6,7},{7,4},{8,9},{9,10},{10,1... | collective-permute-start | bytes 1572872 | tf_op jit(solution)/shard_map/ppermute | solution.py:459
  82.7 1.7 %collective-permute-start.1 = (f32[2,512,128]{2,1,0:T(8,128)}, f32[2,512,128]{2,1,0:T(8,128)S(1)}, u32[]{:S(2)}, u32[]{:S(2)}) collective-permute-start(f32[2,512,128]{2,1,0:T(8,128)} %get-tuple-element.91), channel_id=1, source_target_pairs={{0,3},{1,0},{2,1},{3,2},{4,7},{5,4},{6,5},{7,6},{8,11},{9,8},{10,9... | collective-permute-start | bytes 1572872 | tf_op jit(solution)/shard_map/ppermute | solution.py:463
  84.4 0.0 copy-start.5
  84.4 8.8 %row_grads.3 = (bf16[2048,1024]{1,0:T(8,128)(2,1)}, f32[8,2048]{1,0:T(8,128)}, f32[8,2048]{1,0:T(8,128)}) custom-call(s32[1]{0:T(128)S(6)} %copy.43.count.refs_0_, bf16[2048,1024]{1,0:T(8,128)(2,1)} %refs_1_.5, bf16[2048,128]{1,0:T(8,128)(2,1)} %refs_2_.5, bf16[2048,128]{1,0:T(8,128)(2,1)} %refs_3_.5, f32[8,2048]{1,0:T(8,128)} %get-tuple-element.65.cum_ref.refs_4_, ...), custom_call_target="tpu_custom_call" | custom-call | tf_op jit(solution)/shard_map/row_grads/pallas_call | solution.py:438
  93.1 3.4 %collective-permute-done = f32[2,512,128]{2,1,0:T(8,128)S(1)} collective-permute-done((f32[2,512,128]{2,1,0:T(8,128)}, f32[2,512,128]{2,1,0:T(8,128)S(1)}, u32[]{:S(2)}, u32[]{:S(2)}) %collective-permute-start) | collective-permute-done | bytes 524320 | tf_op jit(solution)/shard_map/ppermute | solution.py:459
  96.6 0.0 collective-permute-done.1
  96.6 0.0 copy-done.5
  96.6 0.1 add_bitcast_fusion
  96.6 1.6 %collective-permute-start.2 = (f32[512,128]{1,0:T(8,128)S(1)}, f32[512,128]{1,0:T(8,128)S(1)}, u32[]{:S(2)}, u32[]{:S(2)}) collective-permute-start(f32[512,128]{1,0:T(8,128)S(1)} %get-tuple-element.136), channel_id=1, source_target_pairs={{0,1},{1,2},{2,3},{3,0},{4,5},{5,6},{6,7},{7,4},{8,9},{9,10},{10,1... | collective-permute-start | bytes 786440 | tf_op jit(solution)/shard_map/ppermute | solution.py:459
  98.3 1.7 %collective-permute-start.3 = (f32[512,128]{1,0:T(8,128)S(1)}, f32[512,128]{1,0:T(8,128)S(1)}, u32[]{:S(2)}, u32[]{:S(2)}) collective-permute-start(f32[512,128]{1,0:T(8,128)S(1)} %get-tuple-element.135), channel_id=1, source_target_pairs={{0,3},{1,0},{2,1},{3,2},{4,7},{5,4},{6,5},{7,6},{8,11},{9,8},{10,9... | collective-permute-start | bytes 786440 | tf_op jit(solution)/shard_map/ppermute | solution.py:463
  100.0 0.0 copy-start.4
  100.0 5.5 %row_grads.4 = (bf16[2048,1024]{1,0:T(8,128)(2,1)}, f32[8,2048]{1,0:T(8,128)}, f32[8,2048]{1,0:T(8,128)}) custom-call(s32[1]{0:T(128)S(6)} %copy.43.count.refs_0_, bf16[2048,1024]{1,0:T(8,128)(2,1)} %refs_1_.5, bf16[2048,128]{1,0:T(8,128)(2,1)} %refs_2_.5, bf16[2048,128]{1,0:T(8,128)(2,1)} %refs_3_.5, ...), custom_call_target="tpu_custom_call", output_to_operand_aliasing={{0}: (14, {}), {1}: (15, {}), {2}: (16, {})} | custom-call | tf_op jit(solution)/shard_map/row_grads/pallas_call | solution.py:438
  105.4 0.0 collective-permute-done.2
  105.5 0.0 collective-permute-done.3
  105.5 0.1 broadcast_in_dim.9.clone.1
  105.5 0.0 copy-done.4
  105.6 0.1 broadcast_in_dim.9.clone
  105.7 0.8 pad_maximum_fusion
  106.6 1.0 collective-permute-start.4
  107.6 2.3 %collective-permute-start.5 = (f32[2,512,128]{2,1,0:T(8,128)}, f32[2,512,128]{2,1,0:T(8,128)S(1)}, u32[]{:S(2)}, u32[]{:S(2)}) collective-permute-start(f32[2,512,128]{2,1,0:T(8,128)} %pad_maximum_fusion), channel_id=1, source_target_pairs={{0,3},{1,0},{2,1},{3,2},{4,7},{5,4},{6,5},{7,6},{8,11},{9,8},{10,9... | collective-permute-start | bytes 1572872 | tf_op jit(solution)/shard_map/ppermute | solution.py:463
  109.8 5.4 %row_grads.5 = (bf16[2048,1024]{1,0:T(8,128)(2,1)}, f32[8,2048]{1,0:T(8,128)}, f32[8,2048]{1,0:T(8,128)}) custom-call(s32[1]{0:T(128)S(6)} %copy.43.count.refs_0_, bf16[2048,1024]{1,0:T(8,128)(2,1)} %refs_1_.5, bf16[2048,128]{1,0:T(8,128)(2,1)} %refs_2_.5, bf16[2048,128]{1,0:T(8,128)(2,1)} %refs_3_.5, ...), custom_call_target="tpu_custom_call", output_to_operand_aliasing={{0}: (14, {}), {1}: (15, {}), {2}: (16, {})} | custom-call | tf_op jit(solution)/shard_map/row_grads/pallas_call | solution.py:438
  115.2 5.4 %collective-permute-done.4 = f32[2,512,128]{2,1,0:T(8,128)S(1)} collective-permute-done((f32[2,512,128]{2,1,0:T(8,128)}, f32[2,512,128]{2,1,0:T(8,128)S(1)}, u32[]{:S(2)}, u32[]{:S(2)}) %collective-permute-start.4) | collective-permute-done | bytes 524320 | tf_op jit(solution)/shard_map/ppermute | solution.py:459
  120.7 0.0 collective-permute-done.5
  120.7 0.1 slice_dynamic-update-slice_fusion
  120.7 0.1 slice_bitcast_fusion
  120.8 3.0 %collective-permute-start.7 = (f32[512,128]{1,0:T(8,128)S(1)}, f32[512,128]{1,0:T(8,128)S(1)}, u32[]{:S(2)}, u32[]{:S(2)}) collective-permute-start(f32[512,128]{1,0:T(8,128)S(1)} %get-tuple-element.129), channel_id=1, source_target_pairs={{0,3},{1,0},{2,1},{3,2},{4,7},{5,4},{6,5},{7,6},{8,11},{9,8},{10,9... | collective-permute-start | bytes 786440 | tf_op jit(solution)/shard_map/ppermute | solution.py:463
  123.8 0.0 collective-permute-start.6
  123.8 3.9 %collective-permute-done.7 = f32[512,128]{1,0:T(8,128)S(1)} collective-permute-done((f32[512,128]{1,0:T(8,128)S(1)}, f32[512,128]{1,0:T(8,128)S(1)}, u32[]{:S(2)}, u32[]{:S(2)}) %collective-permute-start.7) | collective-permute-done | bytes 262176 | tf_op jit(solution)/shard_map/ppermute | solution.py:463
  127.7 0.0 copy-start.2
  127.7 3.7 %collective-permute-done.6 = f32[512,128]{1,0:T(8,128)S(1)} collective-permute-done((f32[512,128]{1,0:T(8,128)S(1)}, f32[512,128]{1,0:T(8,128)S(1)}, u32[]{:S(2)}, u32[]{:S(2)}) %collective-permute-start.6) | collective-permute-done | bytes 262176 | tf_op jit(solution)/shard_map/ppermute | solution.py:459
  131.4 0.0 copy-start.3
  131.4 0.0 copy-done.2
  131.4 1.0 copy-done.3
  (4 shorter events, 0.1 us)
Async XLA Ops:
  14.3 27.3 %all-to-all-start = ((f32[32,8,1152]{2,1,0:T(8,128)}), f32[32,8,1152]{2,1,0:T(8,128)S(1)}, u32[]{:S(2)}, u32[]{:S(2)}) async-start(f32[32,8,1152]{2,1,0:T(8,128)} %get-tuple-element.69), calls=%async_computation | async-start | bytes 2359296 | tf_op jit(solution)/shard_map/all_to_all | solution.py:472
  41.6 1.0 copy-start
  45.1 21.3 %all-to-all-start.1 = ((f32[32,8,1024]{2,1,0:T(8,128)}), f32[32,8,1024]{2,1,0:T(8,128)S(1)}, u32[]{:S(2)}, u32[]{:S(2)}) async-start(f32[32,8,1024]{2,1,0:T(8,128)} %scan_devices.1), calls=%async_computation.1 | async-start | bytes 2097152 | tf_op jit(solution)/shard_map/all_to_all | solution.py:476
  66.4 1.0 copy-start.1
  81.0 15.5 %collective-permute-start = (f32[2,512,128]{2,1,0:T(8,128)}, f32[2,512,128]{2,1,0:T(8,128)S(1)}, u32[]{:S(2)}, u32[]{:S(2)}) collective-permute-start(f32[2,512,128]{2,1,0:T(8,128)} %get-tuple-element.90), channel_id=1, source_target_pairs={{0,1},{1,2},{2,3},{3,0},{4,5},{5,6},{6,7},{7,4},{8,9},{9,10},{10,1... | collective-permute-start | bytes 1572872 | tf_op jit(solution)/shard_map/ppermute | solution.py:459
  82.7 13.9 %collective-permute-start.1 = (f32[2,512,128]{2,1,0:T(8,128)}, f32[2,512,128]{2,1,0:T(8,128)S(1)}, u32[]{:S(2)}, u32[]{:S(2)}) collective-permute-start(f32[2,512,128]{2,1,0:T(8,128)} %get-tuple-element.91), channel_id=1, source_target_pairs={{0,3},{1,0},{2,1},{3,2},{4,7},{5,4},{6,5},{7,6},{8,11},{9,8},{10,9... | collective-permute-start | bytes 1572872 | tf_op jit(solution)/shard_map/ppermute | solution.py:463
  84.4 12.2 %copy-start.5 = (f32[2,512,128]{2,1,0:T(8,128)S(1)}, f32[2,512,128]{2,1,0:T(8,128)}, u32[]{:S(2)}) copy-start(f32[2,512,128]{2,1,0:T(8,128)} %get-tuple-element.103) | copy-start | bytes 1572868
  96.6 8.8 %collective-permute-start.2 = (f32[512,128]{1,0:T(8,128)S(1)}, f32[512,128]{1,0:T(8,128)S(1)}, u32[]{:S(2)}, u32[]{:S(2)}) collective-permute-start(f32[512,128]{1,0:T(8,128)S(1)} %get-tuple-element.136), channel_id=1, source_target_pairs={{0,1},{1,2},{2,3},{3,0},{4,5},{5,6},{6,7},{7,4},{8,9},{9,10},{10,1... | collective-permute-start | bytes 786440 | tf_op jit(solution)/shard_map/ppermute | solution.py:459
  98.3 7.2 %collective-permute-start.3 = (f32[512,128]{1,0:T(8,128)S(1)}, f32[512,128]{1,0:T(8,128)S(1)}, u32[]{:S(2)}, u32[]{:S(2)}) collective-permute-start(f32[512,128]{1,0:T(8,128)S(1)} %get-tuple-element.135), channel_id=1, source_target_pairs={{0,3},{1,0},{2,1},{3,2},{4,7},{5,4},{6,5},{7,6},{8,11},{9,8},{10,9... | collective-permute-start | bytes 786440 | tf_op jit(solution)/shard_map/ppermute | solution.py:463
  100.0 5.6 %copy-start.4 = (f32[2,512,128]{2,1,0:T(8,128)S(1)}, f32[2,512,128]{2,1,0:T(8,128)}, u32[]{:S(2)}) copy-start(f32[2,512,128]{2,1,0:T(8,128)} %get-tuple-element.89) | copy-start | bytes 1572868
  106.6 14.1 %collective-permute-start.4 = (f32[2,512,128]{2,1,0:T(8,128)}, f32[2,512,128]{2,1,0:T(8,128)S(1)}, u32[]{:S(2)}, u32[]{:S(2)}) collective-permute-start(f32[2,512,128]{2,1,0:T(8,128)} %pad_maximum_fusion), channel_id=1, source_target_pairs={{0,1},{1,2},{2,3},{3,0},{4,5},{5,6},{6,7},{7,4},{8,9},{9,10},{10,1... | collective-permute-start | bytes 1572872 | tf_op jit(solution)/shard_map/ppermute | solution.py:459
  107.6 13.1 %collective-permute-start.5 = (f32[2,512,128]{2,1,0:T(8,128)}, f32[2,512,128]{2,1,0:T(8,128)S(1)}, u32[]{:S(2)}, u32[]{:S(2)}) collective-permute-start(f32[2,512,128]{2,1,0:T(8,128)} %pad_maximum_fusion), channel_id=1, source_target_pairs={{0,3},{1,0},{2,1},{3,2},{4,7},{5,4},{6,5},{7,6},{8,11},{9,8},{10,9... | collective-permute-start | bytes 1572872 | tf_op jit(solution)/shard_map/ppermute | solution.py:463
  120.8 6.9 %collective-permute-start.7 = (f32[512,128]{1,0:T(8,128)S(1)}, f32[512,128]{1,0:T(8,128)S(1)}, u32[]{:S(2)}, u32[]{:S(2)}) collective-permute-start(f32[512,128]{1,0:T(8,128)S(1)} %get-tuple-element.129), channel_id=1, source_target_pairs={{0,3},{1,0},{2,1},{3,2},{4,7},{5,4},{6,5},{7,6},{8,11},{9,8},{10,9... | collective-permute-start | bytes 786440 | tf_op jit(solution)/shard_map/ppermute | solution.py:463
  123.8 7.6 %collective-permute-start.6 = (f32[512,128]{1,0:T(8,128)S(1)}, f32[512,128]{1,0:T(8,128)S(1)}, u32[]{:S(2)}, u32[]{:S(2)}) collective-permute-start(f32[512,128]{1,0:T(8,128)S(1)} %get-tuple-element.133), channel_id=1, source_target_pairs={{0,1},{1,2},{2,3},{3,0},{4,5},{5,6},{6,7},{7,4},{8,9},{9,10},{10,1... | collective-permute-start | bytes 786440 | tf_op jit(solution)/shard_map/ppermute | solution.py:459
  127.7 3.7 %copy-start.2 = (f32[4,512,128]{2,1,0:T(8,128)}, f32[4,512,128]{2,1,0:T(8,128)S(1)}, u32[]{:S(2)}) copy-start(f32[4,512,128]{2,1,0:T(8,128)S(1)} %bitcast_dynamic-update-slice_fusion) | copy-start | bytes 3145732
  131.4 1.0 copy-start.3

commit v3 on v2

--- a/solution.py
+++ b/solution.py
@@ -8,7 +8,8 @@
 L = 256
 F32 = jnp.float32
 BF16 = jnp.bfloat16
-FIRST, SECOND = 4, 2
+PER = 2
+FIRST = 5
 VMEM_LIMIT = 56 * 1024 * 1024
 
 
@@ -81,22 +82,27 @@
             )
             col_ref[sl, :] = rows.T
 
-    s_ref[0] = s_acc[...].astype(BF16)
-    rows = pl.ds(pl.multiple_of(k * L, L), L)
-    sc = faded(x_ref, col_ref[rows, 2 * heads : 3 * heads])
-    s_acc[...] = spread(jnp.exp(tot[k][:, :1]), width) * s_acc[...] + mm(
-        b_ref[...].T, sc, 1, 0
-    )
-
-    back = blocks - 1 - k
-    a_ref[0] = a_acc[...].astype(BF16)
-    rows = pl.ds(pl.multiple_of(back * L, L), L)
-    dq = faded(g_ref, col_ref[rows, heads : 2 * heads])
-    a_acc[...] = spread(jnp.exp(tot[back][:, :1]), width) * a_acc[...] + mm(
-        c_ref[...].T, dq, 1, 0
-    )
-
-    @pl.when(k == blocks - 1)
+    for j in range(PER):
+        n = k * PER + j
+        s_ref[j] = s_acc[...].astype(BF16)
+        rows = pl.ds(pl.multiple_of(n * L, L), L)
+        at = slice(j * L, (j + 1) * L)
+        sc = faded(x_ref.at[at, :], col_ref[rows, 2 * heads : 3 * heads])
+        s_acc[...] = spread(jnp.exp(tot[n][:, :1]), width) * s_acc[...] + mm(
+            b_ref[at, :].T, sc, 1, 0
+        )
+
+        m = PER - 1 - j
+        n = blocks - 1 - n
+        a_ref[m] = a_acc[...].astype(BF16)
+        rows = pl.ds(pl.multiple_of(n * L, L), L)
+        at = slice(m * L, (m + 1) * L)
+        dq = faded(g_ref.at[at, :], col_ref[rows, heads : 2 * heads])
+        a_acc[...] = spread(jnp.exp(tot[n][:, :1]), width) * a_acc[...] + mm(
+            c_ref[at, :].T, dq, 1, 0
+        )
+
+    @pl.when(k == blocks // PER - 1)
     def _():
         whole = tot[0]
         for n in range(1, blocks):
@@ -118,25 +124,26 @@
     wide = x.shape[1]
     each = n // devices
     fwd = lambda k: (k, 0)
-    rev = lambda k: (blocks - 1 - k, 0)
+    last = blocks // PER - 1
+    rev = lambda k: (last - k, 0)
     whole = lambda k: (0, 0)
     return pl.pallas_call(
         states_kernel,
-        grid=(blocks,),
+        grid=(blocks // PER,),
         in_specs=[
             pl.BlockSpec(memory_space=pltpu.SMEM),
-            pl.BlockSpec((L, wide), fwd),
-            pl.BlockSpec((L, wide), rev),
-            pl.BlockSpec((L, n), fwd),
-            pl.BlockSpec((L, n), rev),
+            pl.BlockSpec((PER * L, wide), fwd),
+            pl.BlockSpec((PER * L, wide), rev),
+            pl.BlockSpec((PER * L, n), fwd),
+            pl.BlockSpec((PER * L, n), rev),
             pl.BlockSpec((heads, rows), whole),
             pl.BlockSpec((heads, rows), whole),
         ],
         out_specs=[
             pl.BlockSpec((heads, rows), whole),
             pl.BlockSpec((rows, 128), whole),
-            pl.BlockSpec((1, n, wide), lambda k: (k, 0, 0)),
-            pl.BlockSpec((1, n, wide), lambda k: (blocks - 1 - k, 0, 0)),
+            pl.BlockSpec((PER, n, wide), lambda k: (k, 0, 0)),
+            pl.BlockSpec((PER, n, wide), lambda k: (last - k, 0, 0)),
             pl.BlockSpec((devices, 2 * each, wide + 128), lambda k: (0, 0, 0)),
         ],
         out_shape=[
@@ -188,7 +195,7 @@
     )(got)
 
 
-def inner_kernel(gain, x_ref, g_ref, b_ref, c_ref, cum_ref, col_ref,
+def inner_kernel(gain, x_ref, g_ref, b_ref, c_ref, cum_ref, col_ref, s_ref, a_ref,
                  *rest):
     dx_ref, db_ref, dc_ref, q_ref, r_ref = rest[-5:]
     heads = cum_ref.shape[0]
@@ -201,6 +208,8 @@
     keep = j <= i
     used = col_ref[:, 4 * heads : 4 * heads + 1]
     lane = lax.broadcasted_iota(jnp.int32, (L, 128), 1)
+    state = s_ref[0]
+    adj = a_ref[0]
     dscore = jnp.zeros((L, L), F32)
     r_all = jnp.zeros((L, 128), F32)
     for h in range(heads):
@@ -222,12 +231,14 @@
         r_all = jnp.where(lane == 2 * heads + h, jnp.sum(prod, axis=1, keepdims=True), r_all)
         r_all = jnp.where(lane == 3 * heads + h, jnp.sum(x * du, axis=1, keepdims=True), r_all)
     r_ref[...] = r_all
-    ds = dscore.astype(BF16)
-    db_ref[...] = mm(ds, c, 1, 0)
-    dc_ref[...] = mm(ds.T, b, 1, 0)
-
-
-def within(gain, x, g, b, c, cum, col, first, blocks, earlier):
+    dscore = dscore.astype(BF16)
+    sc = faded(x_ref, col_ref[:, 2 * heads : 3 * heads])
+    dq = faded(g_ref, col_ref[:, heads : 2 * heads])
+    db_ref[...] = mm(dscore, c, 1, 0) + mm(sc, adj, 1, 1)
+    dc_ref[...] = mm(dscore.T, b, 1, 0) + mm(dq, state, 1, 1)
+
+
+def within(gain, x, g, b, c, cum, col, s, a, first, blocks, earlier):
     heads = cum.shape[0]
     n = b.shape[1]
     wide = x.shape[1]
@@ -244,6 +255,8 @@
             pl.BlockSpec((L, n), at),
             pl.BlockSpec((heads, L), lambda k: (0, first + k)),
             pl.BlockSpec((L, 128), at),
+            pl.BlockSpec((1, n, wide), lambda k: (first + k, 0, 0)),
+            pl.BlockSpec((1, n, wide), lambda k: (first + k, 0, 0)),
         ] + [pl.BlockSpec(memory_space=pl.ANY)] * len(earlier),
         out_specs=[
             pl.BlockSpec((L, wide), at),
@@ -259,125 +272,125 @@
             jax.ShapeDtypeStruct((heads, rows), F32),
             jax.ShapeDtypeStruct((rows, 128), F32),
         ],
-        input_output_aliases={7 + i: i for i in range(len(earlier))},
+        input_output_aliases={9 + i: i for i in range(len(earlier))},
         compiler_params=pltpu.CompilerParams(vmem_limit_bytes=VMEM_LIMIT),
         name="within_blocks",
-    )(gain, x, g, b, c, cum, col, *earlier)
-
-
-def basis_kernel(me, cum_ref, s_ref, a_ref, x_ref, g_ref, col_ref, got_ref, db1_ref, dc1_ref,
-                 state_ref, adj_ref, flow_ref, up_ref, down_ref, mid_ref, own_ref, s0, a0):
+    )(gain, x, g, b, c, cum, col, s, a, *earlier)
+
+
+def unpack(got_ref, s0, a0):
+    each = got_ref.shape[1] // 2
+    for i in range(got_ref.shape[0]):
+        s0[i * each : (i + 1) * each, :] = got_ref[i, 0:each, :]
+        a0[i * each : (i + 1) * each, :] = got_ref[i, each : 2 * each, :]
+
+
+def totals(cum_ref, k):
     heads = cum_ref.shape[0]
-    blocks = cum_ref.shape[1] // L
-    n, wide = s0.shape
-    width = wide // heads
-    k = pl.program_id(0)
-    each = got_ref.shape[1] // 2
-
-    @pl.when(k == 0)
-    def _():
-        for i in range(got_ref.shape[0]):
-            s0[i * each : (i + 1) * each, :] = got_ref[i, 0:each, :]
-            a0[i * each : (i + 1) * each, :] = got_ref[i, each : 2 * each, :]
-
     before = jnp.zeros((heads, 1), F32)
     after = jnp.zeros((heads, 1), F32)
     own = jnp.zeros((heads, 1), F32)
-    for m in range(blocks):
+    for m in range(cum_ref.shape[1] // L):
         t = cum_ref[:, m * L + L - 1 : m * L + L]
         before = before + jnp.where(m < k, t, 0.0)
         after = after + jnp.where(m > k, t, 0.0)
         own = own + jnp.where(m == k, t, 0.0)
-    state = s_ref[0].astype(F32) + spread(jnp.exp(before), width) * s0[...]
-    adj = a_ref[0].astype(F32) + spread(jnp.exp(after), width) * a0[...]
-    state_h = state.astype(BF16)
-    adj_h = adj.astype(BF16)
-    state_ref[0] = state_h
-    adj_ref[0] = adj_h
-    dc = dc1_ref[...] + mm(faded(g_ref, col_ref[:, heads : 2 * heads]), state_h, 1, 1)
-    db = db1_ref[...] + mm(faded(x_ref, col_ref[:, 2 * heads : 3 * heads]), adj_h, 1, 1)
-    inflow = jnp.concatenate(
-        [
-            jnp.sum(
-                adj[:, h * width : (h + 1) * width] * state[:, h * width : (h + 1) * width],
-                axis=0, keepdims=True,
-            )
-            for h in range(heads)
-        ],
-        axis=0,
-    )
-    flow = jnp.sum(inflow, axis=1, keepdims=True) * jnp.exp(own)
-    flow_ref[0] = jnp.broadcast_to(flow, (heads, 128))
+    return before, after, own
+
+
+def basis_kernel(me, cum_ref, x_ref, g_ref, col_ref, got_ref, db1_ref, dc1_ref,
+                 up_ref, down_ref, mid_ref, own_ref, s0, a0):
+    heads = cum_ref.shape[0]
+    blocks = cum_ref.shape[1] // L
+    width = s0.shape[1] // heads
+    k = pl.program_id(0)
+
+    @pl.when(k == 0)
+    def _():
+        unpack(got_ref, s0, a0)
 
     per = blocks // 4
-    turn = lax.rem(lax.div(k, per) - me[0] + 4, 4)
-    at = pl.ds(pl.multiple_of(lax.rem(k, per) * L, L), L)
+    dbs, dcs = [], []
+    for j in range(per):
+        at = slice(j * L, (j + 1) * L)
+        before, after, _ = totals(cum_ref, k * per + j)
+        state = (spread(jnp.exp(before), width) * s0[...]).astype(BF16)
+        adj = (spread(jnp.exp(after), width) * a0[...]).astype(BF16)
+        e = col_ref[at, heads : 2 * heads]
+        ts = col_ref[at, 2 * heads : 3 * heads]
+        dcs.append(dc1_ref[at, :] + mm(faded(g_ref.at[at, :], e), state, 1, 1))
+        dbs.append(db1_ref[at, :] + mm(faded(x_ref.at[at, :], ts), adj, 1, 1))
+    db = jnp.concatenate(dbs, axis=0)
+    dc = jnp.concatenate(dcs, axis=0)
+    turn = lax.rem(k - me[0] + 4, 4)
 
     @pl.when(turn == 0)
     def _():
-        own_ref[0, at, :] = db
-        own_ref[1, at, :] = dc
+        own_ref[0] = db
+        own_ref[1] = dc
 
     @pl.when(turn == 1)
     def _():
-        mid_ref[0, at, :] = db
-        up_ref[1, at, :] = dc
+        mid_ref[0] = db
+        up_ref[1] = dc
 
     @pl.when(turn == 2)
     def _():
-        up_ref[0, at, :] = db
-        down_ref[0, at, :] = dc
+        up_ref[0] = db
+        down_ref[0] = dc
 
     @pl.when(turn == 3)
     def _():
-        down_ref[1, at, :] = db
-        mid_ref[1, at, :] = dc
-
-
-def basis_grads(me, cum, s, a, x, g, col, got, db1, dc1):
+        down_ref[1] = db
+        mid_ref[1] = dc
+
+
+def basis_grads(me, cum, x, g, col, got, db1, dc1):
     heads, rows = cum.shape
-    n, wide = s.shape[1:]
-    blocks = rows // L
+    n = db1.shape[1]
+    wide = x.shape[1]
+    part = rows // 4
     at = lambda k: (k, 0)
-    layer = pl.BlockSpec((1, n, wide), lambda k: (k, 0, 0))
     pair = pl.BlockSpec((2, rows // 4, n), lambda k: (0, 0, 0))
 
     return pl.pallas_call(
         basis_kernel,
-        grid=(blocks,),
+        grid=(4,),
         in_specs=[
             pl.BlockSpec(memory_space=pltpu.SMEM),
             pl.BlockSpec((heads, rows), lambda k: (0, 0)),
-            layer,
-            layer,
-            pl.BlockSpec((L, wide), at),
-            pl.BlockSpec((L, wide), at),
-            pl.BlockSpec((L, 128), at),
+            pl.BlockSpec((part, wide), at),
+            pl.BlockSpec((part, wide), at),
+            pl.BlockSpec((part, 128), at),
             pl.BlockSpec(got.shape, lambda k: (0, 0, 0)),
-            pl.BlockSpec((L, n), at),
-            pl.BlockSpec((L, n), at),
-        ],
-        out_specs=[layer, layer, pl.BlockSpec((1, heads, 128), lambda k: (k, 0, 0)),
-                   pair, pair, pair, pair],
-        out_shape=[
-            jax.ShapeDtypeStruct((blocks, n, wide), BF16),
-            jax.ShapeDtypeStruct((blocks, n, wide), BF16),
-            jax.ShapeDtypeStruct((blocks, heads, 128), F32),
-        ] + [jax.ShapeDtypeStruct((2, rows // 4, n), F32)] * 4,
+            pl.BlockSpec((part, n), at),
+            pl.BlockSpec((part, n), at),
+        ],
+        out_specs=[pair, pair, pair, pair],
+        out_shape=[jax.ShapeDtypeStruct((2, rows // 4, n), F32)] * 4,
         scratch_shapes=[pltpu.VMEM((n, wide), F32), pltpu.VMEM((n, wide), F32)],
         compiler_params=pltpu.CompilerParams(vmem_limit_bytes=VMEM_LIMIT),
         name="basis_grads",
-    )(me, cum, s, a, x, g, col, got, db1, dc1)
+    )(me, cum, x, g, col, got, db1, dc1)
 
 
 def row_kernel(first, count, x_ref, b_ref, c_ref, cum_ref, step_ref, col_ref, g_ref,
-               state_ref, adj_ref, flow_ref, dx1_ref, q_ref, r_ref, *rest):
-    dx_ref, dstep_ref, ddecay_ref = rest[-3:]
+               s_ref, a_ref, got_ref, dx1_ref, q_ref, r_ref, *rest):
+    dx_ref, dstep_ref, ddecay_ref, s0, a0 = rest[-5:]
     heads = cum_ref.shape[0]
     width = x_ref.shape[1] // heads
     k = first + pl.program_id(0)
-    carried = mm(c_ref[...], state_ref[0], 1, 0)
-    fed = mm(b_ref[...], adj_ref[0], 1, 0)
+
+    @pl.when(pl.program_id(0) == 0)
+    def _():
+        unpack(got_ref, s0, a0)
+
+    before, after, own = totals(cum_ref, k)
+    state = s_ref[0].astype(F32) + spread(jnp.exp(before), width) * s0[...]
+    adj = a_ref[0].astype(F32) + spread(jnp.exp(after), width) * a0[...]
+    carried = mm(c_ref[...], state.astype(BF16), 1, 0)
+    fed = mm(b_ref[...], adj.astype(BF16), 1, 0)
+    inflow = []
     lane = lax.broadcasted_iota(jnp.int32, (L, 128), 1)
     packed = r_ref[...]
     for h in range(heads):
@@ -389,39 +402,41 @@
         q = jnp.sum(g_ref[:, cs].astype(F32) * carried[:, cs], axis=1, keepdims=True)
         packed = jnp.where(lane == h, a, packed)
         packed = jnp.where(lane == heads + h, q, packed)
+        inflow.append(jnp.sum(adj[:, cs] * state[:, cs], axis=0, keepdims=True))
     rows = packed.T
     at = k * L + lax.broadcasted_iota(jnp.int32, (heads, L), 1)
     live = (at < count[0]).astype(F32)
-    cum = cum_ref[...]
-    more = jnp.exp(cum[:, L - 1 :] - cum) * rows[0:heads]
+    cum = cum_ref[:, pl.ds(pl.multiple_of(k * L, L), L)]
+    more = jnp.exp(own - cum) * rows[0:heads]
     mine = step_ref[...] * live * more
-    flow = flow_ref[0][:, :1] + jnp.sum(mine, axis=1, keepdims=True)
+    flow = jnp.sum(jnp.concatenate(inflow, axis=0), axis=1, keepdims=True) * jnp.exp(own)
+    flow = flow + jnp.sum(mine, axis=1, keepdims=True)
     paid = jnp.exp(cum) * live * rows[heads : 2 * heads]
     dcum = q_ref[...] + paid - rows[2 * heads : 3 * heads] - mine
     ddecay_ref[...] = (running(dcum, True) + flow) * live
     dstep_ref[...] = (rows[3 * heads : 4 * heads] + more) * live
 
 
-def row_grads(first, blocks, count, x, b, c, cum, step, col, g, state, adj, flow, dx1, q, r, earlier):
+def row_grads(first, blocks, count, x, b, c, cum, step, col, g, s, a, got, dx1, q, r, earlier):
     heads, rows = cum.shape
     n = b.shape[1]
     wide = x.shape[1]
     at = lambda k: (first + k, 0)
     side = lambda k: (0, first + k)
     layer = pl.BlockSpec((1, n, wide), lambda k: (first + k, 0, 0))
-    args = [count, x, b, c, cum, step, col, g, state, adj, flow, dx1, q, r]
+    args = [count, x, b, c, cum, step, col, g, s, a, got, dx1, q, r]
     specs = [
         pl.BlockSpec(memory_space=pltpu.SMEM),
         pl.BlockSpec((L, wide), at),
         pl.BlockSpec((L, n), at),
         pl.BlockSpec((L, n), at),
-        pl.BlockSpec((heads, L), side),
+        pl.BlockSpec((heads, rows), lambda k: (0, 0)),
         pl.BlockSpec((heads, L), side),
         pl.BlockSpec((L, 128), at),
         pl.BlockSpec((L, wide), at),
         layer,
         layer,
-        pl.BlockSpec((1, heads, 128), lambda k: (first + k, 0, 0)),
+        pl.BlockSpec(got.shape, lambda k: (0, 0, 0)),
         pl.BlockSpec((L, wide), at),
         pl.BlockSpec((heads, L), lambda k: (0, first + k)),
         pl.BlockSpec((L, 128), at),
@@ -449,6 +464,7 @@
             jax.ShapeDtypeStruct((heads, rows), F32),
             jax.ShapeDtypeStruct((heads, rows), F32),
         ],
+        scratch_shapes=[pltpu.VMEM((n, wide), F32), pltpu.VMEM((n, wide), F32)],
         input_output_aliases=alias,
         compiler_params=pltpu.CompilerParams(vmem_limit_bytes=VMEM_LIMIT),
         name="row_grads",
@@ -470,28 +486,25 @@
     mine = me.astype(jnp.int32).reshape(1)
     cum, col, s, a, send = local_states(count, x, g, b, c, step, decay, devices)
     got = lax.all_to_all(send, "ctx", 0, 0, tiled=True)
-    inner = within(gain, x, g, b, c, cum, col, 0, blocks // 2, ())
+    inner = within(gain, x, g, b, c, cum, col, s, a, 0, blocks // 2, ())
     got, inner = lax.optimization_barrier((got, inner))
     out = scan_devices(got)
     got = lax.all_to_all(out, "ctx", 0, 0, tiled=True)
-    inner = within(gain, x, g, b, c, cum, col, blocks // 2, blocks // 2, inner)
+    inner = within(gain, x, g, b, c, cum, col, s, a, blocks // 2, blocks // 2, inner)
     got, inner = lax.optimization_barrier((got, inner))
     dx1, db1, dc1, q, r = inner
-    state, adj, flow, up1, down1, mid, own = basis_grads(
-        mine, cum, s, a, x, g, col, got, db1, dc1
-    )
+    up1, down1, mid, own = basis_grads(mine, cum, x, g, col, got, db1, dc1)
     rows = lambda first, number, state, before: row_grads(
-        first, number, count, x, b, c, cum, step, col, g, state, adj, flow, dx1, q, r, before
+        first, number, count, x, b, c, cum, step, col, g, state, a, got, dx1, q, r, before
     )
     u, d = up(up1), down(down1)
-    done = rows(0, FIRST, state, ())
-    u, d, state, done = lax.optimization_barrier((u, d, state, done))
+    done = rows(0, FIRST, s, ())
+    u, d, state, done = lax.optimization_barrier((u, d, s, done))
     p, w = up(u[0] + mid[0]), down(d[0] + mid[1])
-    done = rows(FIRST, SECOND, state, done)
-    p, w, state, done = lax.optimization_barrier((p, w, state, done))
     own = jnp.stack([own[0] + d[1] + p, own[1] + u[1] + w])
+    own, state, done = lax.optimization_barrier((own, state, done))
     below, above = up(own), down(own)
-    done = rows(FIRST + SECOND, blocks - FIRST - SECOND, state, done)
+    done = rows(FIRST, blocks - FIRST, state, done)
     below, above, done = lax.optimization_barrier((below, above, done))
     dx, dstep, ddecay = done
     far = (up(below[0]), down(above[1]))

time: 133 us -> 130 us (0.977)
  waiting for transfers between devices: 26.3 us -> 18.3 us
  Pallas kernels: 75.4 us -> 78.8 us
  starting transfers between devices: 25.1 us -> 26.7 us
    pallas_call x2, Pallas kernels: 26.5 us -> 34.6 us  [within(): pl.pallas_call(inner_kernel, grid=(blocks,), in_specs=[pl.BlockSpec(memor...]
    pallas_call x2, Pallas kernels: 26.7 us -> 22.2 us  [the longest x1 11.8 us: local_states(): pl.pallas_call(states_kernel, grid=(blocks // PER,), in_specs=[pl.BlockSp...]
    all_to_all x1, waiting for transfers between devices: 4.1 us -> 0.01 us  [shards(): got = lax.all_to_all(out, 'ctx', 0, 0, tiled=True)]
    all_to_all x1, waiting for transfers between devices: 5.78 us -> 1.73 us  [shards(): got = lax.all_to_all(send, 'ctx', 0, 0, tiled=True)]
    all_to_all x1, starting transfers between devices: 3.93 us -> 5.66 us  [shards(): got = lax.all_to_all(out, 'ctx', 0, 0, tiled=True)]
    pallas_call x3 -> x2, Pallas kernels: 19.7 us -> 19.4 us  [row_grads(): pl.pallas_call(kernel, grid=(blocks,), in_specs=specs, out_specs=[pl.Bloc...]
  transfers between devices with their start and end apart: 10 -> 10, of which waited for: 6 -> 6; matrix products, arithmetic and copies ran while one was open for 0% -> 0% of each run, Pallas kernels for 35% -> 42%
where the time goes in v3:
time: 130 us
  Pallas kernels  78.8 us (61%)
  starting transfers between devices  26.7 us (21%)
  waiting for transfers between devices  18.3 us (14%)
  local copies, waits for them, and re-layouts  4.31 us (3%)
  between operations  1.44 us (1%)
    pallas_call x2, Pallas kernels, within(): pl.pallas_call(inner_kernel, grid=(blocks,), in_specs=[pl.BlockSpec(memor...  34.6 us
    pallas_call x2, Pallas kernels, row_grads(): pl.pallas_call(kernel, grid=(blocks,), in_specs=specs, out_specs=[pl.Bloc...  19.4 us
    ppermute x4, waiting for transfers between devices, up(): return lax.ppermute(v, 'tp', [(i, (i + 1) % 4) for i in range(4)])  12.7 us
    pallas_call x1, Pallas kernels, local_states(): pl.pallas_call(states_kernel, grid=(blocks // PER,), in_specs=[pl.BlockSp...  11.8 us
    pallas_call x1, Pallas kernels, basis_grads(): pl.pallas_call(basis_kernel, grid=(4,), in_specs=[pl.BlockSpec(memory_spa...  10.4 us
    ppermute x4, starting transfers between devices, down(): return lax.ppermute(v, 'tp', [(i, (i + 3) % 4) for i in range(4)])  8.45 us
    all_to_all x1, starting transfers between devices, shards(): got = lax.all_to_all(send, 'ctx', 0, 0, tiled=True)  8.26 us
    all_to_all x1, starting transfers between devices, shards(): got = lax.all_to_all(out, 'ctx', 0, 0, tiled=True)  5.66 us
  transfers between devices with their start and end apart: 10, of which 6 were waited for; matrix products, arithmetic and copies ran while one was open for 0% of the time, Pallas kernels for 42%

profile of v3, /device:TPU:0, one launch (start us, length us, event | category | flops | bytes accessed | tf_op | source)
XLA Modules:
  0.0 129.7 jit_solution(16321577596119245110)
XLA Ops:
  1.3 11.8 %local_states.1 = (f32[8,2048]{1,0:T(8,128)}, f32[2048,128]{1,0:T(8,128)}, bf16[8,128,1024]{2,1,0:T(8,128)(2,1)}, bf16[8,128,1024]{2,1,0:T(8,128)(2,1)}, f32[32,8,1152]{2,1,0:T(8,128)}) custom-call(s32[1]{0:T(128)S(6)} %copy.37.count.refs_0_, bf16[2048,1024]{1,0:T(8,128)(2,1)} %refs_1_.3, bf16[2048,1024]{1,0:T(8,128)(2,1)} %refs_7_.3, ...), custom_call_target="tpu_custom_call" | custom-call | tf_op jit(solution)/shard_map/local_states/pallas_call | solution.py:130
  13.1 8.3 %all-to-all-start = ((f32[32,8,1152]{2,1,0:T(8,128)}), f32[32,8,1152]{2,1,0:T(8,128)S(1)}, u32[]{:S(2)}, u32[]{:S(2)}) async-start(f32[32,8,1152]{2,1,0:T(8,128)} %get-tuple-element.60), calls=%async_computation | async-start | bytes 2359296 | tf_op jit(solution)/shard_map/all_to_all | solution.py:488
  21.4 17.3 %within_blocks.2 = (bf16[2048,1024]{1,0:T(8,128)(2,1)}, f32[2048,128]{1,0:T(8,128)}, f32[2048,128]{1,0:T(8,128)}, f32[8,2048]{1,0:T(8,128)}, f32[2048,128]{1,0:T(8,128)}) custom-call(f32[8]{0:T(128)} %gain.3, bf16[2048,1024]{1,0:T(8,128)(2,1)} %refs_1_.3, bf16[2048,1024]{1,0:T(8,128)(2,1)} %refs_7_.3, bf16[2048,128]{1,0:T(8,128)(2,1)} %refs_2_.3, ...), custom_call_target="tpu_custom_call" | custom-call | tf_op jit(solution)/shard_map/within_blocks/pallas_call | solution.py:247
  38.7 1.7 %all-to-all-done.got_ref = f32[32,8,1152]{2,1,0:T(8,128)S(1)} async-done(((f32[32,8,1152]{2,1,0:T(8,128)}), f32[32,8,1152]{2,1,0:T(8,128)S(1)}, u32[]{:S(2)}, u32[]{:S(2)}) %all-to-all-start) | async-done | bytes 1179680 | tf_op jit(solution)/shard_map/all_to_all | solution.py:488
  40.4 0.0 copy-start.1
  40.4 1.0 copy-done.1
  41.4 2.6 %scan_devices.1 = f32[32,8,1024]{2,1,0:T(8,128)} custom-call(f32[32,8,1152]{2,1,0:T(8,128)} %copy-done.1), custom_call_target="tpu_custom_call" | custom-call | tf_op jit(solution)/shard_map/scan_devices/pallas_call | solution.py:190
  44.0 5.7 %all-to-all-start.1 = ((f32[32,8,1024]{2,1,0:T(8,128)}), f32[32,8,1024]{2,1,0:T(8,128)S(1)}, u32[]{:S(2)}, u32[]{:S(2)}) async-start(f32[32,8,1024]{2,1,0:T(8,128)} %scan_devices.1), calls=%async_computation.1 | async-start | bytes 2097152 | tf_op jit(solution)/shard_map/all_to_all | solution.py:492
  49.7 17.3 %within_blocks.3 = (bf16[2048,1024]{1,0:T(8,128)(2,1)}, f32[2048,128]{1,0:T(8,128)}, f32[2048,128]{1,0:T(8,128)}, f32[8,2048]{1,0:T(8,128)}, f32[2048,128]{1,0:T(8,128)}) custom-call(f32[8]{0:T(128)} %gain.3, bf16[2048,1024]{1,0:T(8,128)(2,1)} %refs_1_.3, ...), custom_call_target="tpu_custom_call", output_to_operand_aliasing={{0}: (9, {}), {1}: (10, {}), {2}: (11, {}), {3}: (12, {}), ... | custom-call | tf_op jit(solution)/shard_map/within_blocks/pallas_call | solution.py:247
  67.0 0.0 all-to-all-done.1.got_ref.refs_10_
  67.0 0.0 copy-start
  67.0 1.0 copy-done
  68.0 10.4 %basis_grads.1 = (f32[2,512,128]{2,1,0:T(8,128)}, f32[2,512,128]{2,1,0:T(8,128)}, f32[2,512,128]{2,1,0:T(8,128)}, f32[2,512,128]{2,1,0:T(8,128)}) custom-call(s32[1]{0:T(128)} %bitcast.me, f32[8,2048]{1,0:T(8,128)} %get-tuple-element.58.cum_ref.refs_4_, bf16[2048,1024]{1,0:T(8,128)(2,1)} %refs_1_.3, bf16[2048,1024]{1,0:T(8,128)(2,1)} %refs_7_.3, ...), custom_call_target="tpu_custom_call" | custom-call | tf_op jit(solution)/shard_map/basis_grads/pallas_call | solution.py:356
  78.4 1.6 %collective-permute-start = (f32[2,512,128]{2,1,0:T(8,128)}, f32[2,512,128]{2,1,0:T(8,128)S(1)}, u32[]{:S(2)}, u32[]{:S(2)}) collective-permute-start(f32[2,512,128]{2,1,0:T(8,128)} %get-tuple-element.83), channel_id=1, source_target_pairs={{0,1},{1,2},{2,3},{3,0},{4,5},{5,6},{6,7},{7,4},{8,9},{9,10},{10,1... | collective-permute-start | bytes 1572872 | tf_op jit(solution)/shard_map/ppermute | solution.py:475
  80.0 0.0 copy-start.4
  80.0 0.0 copy-start.5
  80.0 1.7 %collective-permute-start.1 = (f32[2,512,128]{2,1,0:T(8,128)}, f32[2,512,128]{2,1,0:T(8,128)S(1)}, u32[]{:S(2)}, u32[]{:S(2)}) collective-permute-start(f32[2,512,128]{2,1,0:T(8,128)} %get-tuple-element.84), channel_id=1, source_target_pairs={{0,3},{1,0},{2,1},{3,2},{4,7},{5,4},{6,5},{7,6},{8,11},{9,8},{10,9... | collective-permute-start | bytes 1572872 | tf_op jit(solution)/shard_map/ppermute | solution.py:479
  81.6 11.4 %row_grads.2 = (bf16[2048,1024]{1,0:T(8,128)(2,1)}, f32[8,2048]{1,0:T(8,128)}, f32[8,2048]{1,0:T(8,128)}) custom-call(s32[1]{0:T(128)S(6)} %copy.37.count.refs_0_, bf16[2048,1024]{1,0:T(8,128)(2,1)} %refs_1_.3, bf16[2048,128]{1,0:T(8,128)(2,1)} %refs_2_.3, bf16[2048,128]{1,0:T(8,128)(2,1)} %refs_3_.3, f32[8,2048]{1,0:T(8,128)} %get-tuple-element.58.cum_ref.refs_4_, ...), custom_call_target="tpu_custom_call" | custom-call | tf_op jit(solution)/shard_map/row_grads/pallas_call | solution.py:453
  93.0 1.0 collective-permute-done
  94.0 0.0 collective-permute-done.1
  94.0 0.0 copy-done.4
  94.0 0.1 add_bitcast_fusion.1
  94.1 1.7 %collective-permute-start.2 = (f32[512,128]{1,0:T(8,128)S(1)}, f32[512,128]{1,0:T(8,128)S(1)}, u32[]{:S(2)}, u32[]{:S(2)}) collective-permute-start(f32[512,128]{1,0:T(8,128)S(1)} %get-tuple-element.119), channel_id=1, source_target_pairs={{0,1},{1,2},{2,3},{3,0},{4,5},{5,6},{6,7},{7,4},{8,9},{9,10},{10,1... | collective-permute-start | bytes 786440 | tf_op jit(solution)/shard_map/ppermute | solution.py:475
  95.7 1.6 %collective-permute-start.3 = (f32[512,128]{1,0:T(8,128)S(1)}, f32[512,128]{1,0:T(8,128)S(1)}, u32[]{:S(2)}, u32[]{:S(2)}) collective-permute-start(f32[512,128]{1,0:T(8,128)S(1)} %get-tuple-element.120), channel_id=1, source_target_pairs={{0,3},{1,0},{2,1},{3,2},{4,7},{5,4},{6,5},{7,6},{8,11},{9,8},{10,9... | collective-permute-start | bytes 786440 | tf_op jit(solution)/shard_map/ppermute | solution.py:479
  97.4 5.7 %collective-permute-done.2 = f32[512,128]{1,0:T(8,128)S(1)} collective-permute-done((f32[512,128]{1,0:T(8,128)S(1)}, f32[512,128]{1,0:T(8,128)S(1)}, u32[]{:S(2)}, u32[]{:S(2)}) %collective-permute-start.2) | collective-permute-done | bytes 262176 | tf_op jit(solution)/shard_map/ppermute | solution.py:475
  103.1 0.0 collective-permute-done.3
  103.1 0.0 copy-done.5
  103.1 0.1 fusion.1
  103.2 1.1 collective-permute-start.4
  104.3 2.2 %collective-permute-start.5 = (f32[2,512,128]{2,1,0:T(8,128)S(1)}, f32[2,512,128]{2,1,0:T(8,128)S(1)}, u32[]{:S(2)}, u32[]{:S(2)}) collective-permute-start(f32[2,512,128]{2,1,0:T(8,128)S(1)} %pad_maximum_fusion), channel_id=1, source_target_pairs={{0,3},{1,0},{2,1},{3,2},{4,7},{5,4},{6,5},{7,6},{8,11},{9,8},{10,9... | collective-permute-start | bytes 1572872 | tf_op jit(solution)/shard_map/ppermute | solution.py:479
  106.5 8.0 %row_grads.3 = (bf16[2048,1024]{1,0:T(8,128)(2,1)}, f32[8,2048]{1,0:T(8,128)}, f32[8,2048]{1,0:T(8,128)}) custom-call(s32[1]{0:T(128)S(6)} %copy.37.count.refs_0_, bf16[2048,1024]{1,0:T(8,128)(2,1)} %refs_1_.3, bf16[2048,128]{1,0:T(8,128)(2,1)} %refs_2_.3, bf16[2048,128]{1,0:T(8,128)(2,1)} %refs_3_.3, ...), custom_call_target="tpu_custom_call", output_to_operand_aliasing={{0}: (14, {}), {1}: (15, {}), {2}: (16, {})} | custom-call | tf_op jit(solution)/shard_map/row_grads/pallas_call | solution.py:453
  114.5 0.1 broadcast_in_dim.9.clone
  114.6 0.1 broadcast_in_dim.9.clone.1
  114.7 2.3 %collective-permute-done.4 = f32[2,512,128]{2,1,0:T(8,128)} collective-permute-done((f32[2,512,128]{2,1,0:T(8,128)S(1)}, f32[2,512,128]{2,1,0:T(8,128)}, u32[]{:S(2)}, u32[]{:S(2)}) %collective-permute-start.4) | collective-permute-done | bytes 524320 | tf_op jit(solution)/shard_map/ppermute | solution.py:475
  117.0 0.0 collective-permute-done.5
  117.0 1.1 slice_dynamic-update-slice_fusion
  118.1 0.1 slice_bitcast_fusion
  118.2 2.9 %collective-permute-start.7 = (f32[512,128]{1,0:T(8,128)S(1)}, f32[512,128]{1,0:T(8,128)S(1)}, u32[]{:S(2)}, u32[]{:S(2)}) collective-permute-start(f32[512,128]{1,0:T(8,128)S(1)} %get-tuple-element.111), channel_id=1, source_target_pairs={{0,3},{1,0},{2,1},{3,2},{4,7},{5,4},{6,5},{7,6},{8,11},{9,8},{10,9... | collective-permute-start | bytes 786440 | tf_op jit(solution)/shard_map/ppermute | solution.py:479
  121.1 0.0 collective-permute-start.6
  121.1 3.9 %collective-permute-done.7 = f32[512,128]{1,0:T(8,128)S(1)} collective-permute-done((f32[512,128]{1,0:T(8,128)S(1)}, f32[512,128]{1,0:T(8,128)S(1)}, u32[]{:S(2)}, u32[]{:S(2)}) %collective-permute-start.7) | collective-permute-done | bytes 262176 | tf_op jit(solution)/shard_map/ppermute | solution.py:479
  125.0 0.0 copy-start.3
  125.0 3.7 %collective-permute-done.6 = f32[512,128]{1,0:T(8,128)S(1)} collective-permute-done((f32[512,128]{1,0:T(8,128)S(1)}, f32[512,128]{1,0:T(8,128)S(1)}, u32[]{:S(2)}, u32[]{:S(2)}) %collective-permute-start.6) | collective-permute-done | bytes 262176 | tf_op jit(solution)/shard_map/ppermute | solution.py:475
  128.7 0.0 copy-start.2
  128.7 0.0 copy-done.3
  128.7 1.0 copy-done.2
  (5 shorter events, 0.1 us)
Async XLA Ops:
  13.1 27.3 %all-to-all-start = ((f32[32,8,1152]{2,1,0:T(8,128)}), f32[32,8,1152]{2,1,0:T(8,128)S(1)}, u32[]{:S(2)}, u32[]{:S(2)}) async-start(f32[32,8,1152]{2,1,0:T(8,128)} %get-tuple-element.60), calls=%async_computation | async-start | bytes 2359296 | tf_op jit(solution)/shard_map/all_to_all | solution.py:488
  40.4 1.0 copy-start.1
  44.0 23.0 %all-to-all-start.1 = ((f32[32,8,1024]{2,1,0:T(8,128)}), f32[32,8,1024]{2,1,0:T(8,128)S(1)}, u32[]{:S(2)}, u32[]{:S(2)}) async-start(f32[32,8,1024]{2,1,0:T(8,128)} %scan_devices.1), calls=%async_computation.1 | async-start | bytes 2097152 | tf_op jit(solution)/shard_map/all_to_all | solution.py:492
  67.0 1.0 copy-start
  78.4 15.6 %collective-permute-start = (f32[2,512,128]{2,1,0:T(8,128)}, f32[2,512,128]{2,1,0:T(8,128)S(1)}, u32[]{:S(2)}, u32[]{:S(2)}) collective-permute-start(f32[2,512,128]{2,1,0:T(8,128)} %get-tuple-element.83), channel_id=1, source_target_pairs={{0,1},{1,2},{2,3},{3,0},{4,5},{5,6},{6,7},{7,4},{8,9},{9,10},{10,1... | collective-permute-start | bytes 1572872 | tf_op jit(solution)/shard_map/ppermute | solution.py:475
  80.0 14.0 %copy-start.4 = (f32[2,512,128]{2,1,0:T(8,128)S(1)}, f32[2,512,128]{2,1,0:T(8,128)}, u32[]{:S(2)}) copy-start(f32[2,512,128]{2,1,0:T(8,128)} %get-tuple-element.93) | copy-start | bytes 1572868
  80.0 23.1 %copy-start.5 = (f32[2,512,128]{2,1,0:T(8,128)S(1)}, f32[2,512,128]{2,1,0:T(8,128)}, u32[]{:S(2)}) copy-start(f32[2,512,128]{2,1,0:T(8,128)} %get-tuple-element.82) | copy-start | bytes 1572868
  80.0 14.0 %collective-permute-start.1 = (f32[2,512,128]{2,1,0:T(8,128)}, f32[2,512,128]{2,1,0:T(8,128)S(1)}, u32[]{:S(2)}, u32[]{:S(2)}) collective-permute-start(f32[2,512,128]{2,1,0:T(8,128)} %get-tuple-element.84), channel_id=1, source_target_pairs={{0,3},{1,0},{2,1},{3,2},{4,7},{5,4},{6,5},{7,6},{8,11},{9,8},{10,9... | collective-permute-start | bytes 1572872 | tf_op jit(solution)/shard_map/ppermute | solution.py:479
  94.1 9.0 %collective-permute-start.2 = (f32[512,128]{1,0:T(8,128)S(1)}, f32[512,128]{1,0:T(8,128)S(1)}, u32[]{:S(2)}, u32[]{:S(2)}) collective-permute-start(f32[512,128]{1,0:T(8,128)S(1)} %get-tuple-element.119), channel_id=1, source_target_pairs={{0,1},{1,2},{2,3},{3,0},{4,5},{5,6},{6,7},{7,4},{8,9},{9,10},{10,1... | collective-permute-start | bytes 786440 | tf_op jit(solution)/shard_map/ppermute | solution.py:475
  95.7 7.4 %collective-permute-start.3 = (f32[512,128]{1,0:T(8,128)S(1)}, f32[512,128]{1,0:T(8,128)S(1)}, u32[]{:S(2)}, u32[]{:S(2)}) collective-permute-start(f32[512,128]{1,0:T(8,128)S(1)} %get-tuple-element.120), channel_id=1, source_target_pairs={{0,3},{1,0},{2,1},{3,2},{4,7},{5,4},{6,5},{7,6},{8,11},{9,8},{10,9... | collective-permute-start | bytes 786440 | tf_op jit(solution)/shard_map/ppermute | solution.py:479
  103.2 13.8 %collective-permute-start.4 = (f32[2,512,128]{2,1,0:T(8,128)S(1)}, f32[2,512,128]{2,1,0:T(8,128)}, u32[]{:S(2)}, u32[]{:S(2)}) collective-permute-start(f32[2,512,128]{2,1,0:T(8,128)S(1)} %pad_maximum_fusion), channel_id=1, source_target_pairs={{0,1},{1,2},{2,3},{3,0},{4,5},{5,6},{6,7},{7,4},{8,9},{9,10},{10,1... | collective-permute-start | bytes 1572872 | tf_op jit(solution)/shard_map/ppermute | solution.py:475
  104.3 12.8 %collective-permute-start.5 = (f32[2,512,128]{2,1,0:T(8,128)S(1)}, f32[2,512,128]{2,1,0:T(8,128)S(1)}, u32[]{:S(2)}, u32[]{:S(2)}) collective-permute-start(f32[2,512,128]{2,1,0:T(8,128)S(1)} %pad_maximum_fusion), channel_id=1, source_target_pairs={{0,3},{1,0},{2,1},{3,2},{4,7},{5,4},{6,5},{7,6},{8,11},{9,8},{10,9... | collective-permute-start | bytes 1572872 | tf_op jit(solution)/shard_map/ppermute | solution.py:479
  118.2 6.8 %collective-permute-start.7 = (f32[512,128]{1,0:T(8,128)S(1)}, f32[512,128]{1,0:T(8,128)S(1)}, u32[]{:S(2)}, u32[]{:S(2)}) collective-permute-start(f32[512,128]{1,0:T(8,128)S(1)} %get-tuple-element.111), channel_id=1, source_target_pairs={{0,3},{1,0},{2,1},{3,2},{4,7},{5,4},{6,5},{7,6},{8,11},{9,8},{10,9... | collective-permute-start | bytes 786440 | tf_op jit(solution)/shard_map/ppermute | solution.py:479
  121.1 7.6 %collective-permute-start.6 = (f32[512,128]{1,0:T(8,128)S(1)}, f32[512,128]{1,0:T(8,128)S(1)}, u32[]{:S(2)}, u32[]{:S(2)}) collective-permute-start(f32[512,128]{1,0:T(8,128)S(1)} %get-tuple-element.115), channel_id=1, source_target_pairs={{0,1},{1,2},{2,3},{3,0},{4,5},{5,6},{6,7},{7,4},{8,9},{9,10},{10,1... | collective-permute-start | bytes 786440 | tf_op jit(solution)/shard_map/ppermute | solution.py:475
  125.0 3.7 %copy-start.3 = (f32[4,512,128]{2,1,0:T(8,128)}, f32[4,512,128]{2,1,0:T(8,128)S(1)}, u32[]{:S(2)}) copy-start(f32[4,512,128]{2,1,0:T(8,128)S(1)} %bitcast_dynamic-update-slice_fusion) | copy-start | bytes 3145732
  128.7 1.0 copy-start.2

commit v4 on v3

--- a/solution.py
+++ b/solution.py
@@ -190,7 +190,7 @@
     return pl.pallas_call(
         scan_kernel,
         out_shape=jax.ShapeDtypeStruct((devices, both, lanes - 128), F32),
-        compiler_params=pltpu.CompilerParams(vmem_limit_bytes=VMEM_LIMIT),
+        compiler_params=pltpu.CompilerParams(vmem_limit_bytes=8 * 1024 * 1024),
         name="scan_devices",
     )(got)
 

time: 130 us -> 128 us (0.985)
    unnamed x12 -> x10, local copies, waits for them, and re-layouts: 2.95 us -> 1.93 us
where the time goes in v4:
time: 128 us; the launch traced here: 127 us
  Pallas kernels  77.5 us (61%)
  starting transfers between devices  26.7 us (21%)
  waiting for transfers between devices  18.3 us (14%)
  local copies, waits for them, and re-layouts  3.3 us (3%)
  between operations  1.44 us (1%)
    pallas_call x2, Pallas kernels, within(): pl.pallas_call(inner_kernel, grid=(blocks,), in_specs=[pl.BlockSpec(memor...  34.6 us
    pallas_call x2, Pallas kernels, row_grads(): pl.pallas_call(kernel, grid=(blocks,), in_specs=specs, out_specs=[pl.Bloc...  19.4 us
    ppermute x4, waiting for transfers between devices, up(): return lax.ppermute(v, 'tp', [(i, (i + 1) % 4) for i in range(4)])  12.6 us
    pallas_call x1, Pallas kernels, local_states(): pl.pallas_call(states_kernel, grid=(blocks // PER,), in_specs=[pl.BlockSp...  11.8 us
    pallas_call x1, Pallas kernels, basis_grads(): pl.pallas_call(basis_kernel, grid=(4,), in_specs=[pl.BlockSpec(memory_spa...  10.4 us
    ppermute x4, starting transfers between devices, down(): return lax.ppermute(v, 'tp', [(i, (i + 3) % 4) for i in range(4)])  8.45 us
    all_to_all x1, starting transfers between devices, shards(): got = lax.all_to_all(send, 'ctx', 0, 0, tiled=True)  8.26 us
    all_to_all x1, starting transfers between devices, shards(): got = lax.all_to_all(out, 'ctx', 0, 0, tiled=True)  5.66 us
  transfers between devices with their start and end apart: 10, of which 6 were waited for; matrix products, arithmetic and copies ran while one was open for 0% of the time, Pallas kernels for 42%

profile of v4, /device:TPU:0, one launch (start us, length us, event | category | flops | bytes accessed | tf_op | source)
XLA Modules:
  0.0 127.4 jit_solution(165262115912943499)
XLA Ops:
  1.3 11.8 %local_states.1 = (f32[8,2048]{1,0:T(8,128)}, f32[2048,128]{1,0:T(8,128)}, bf16[8,128,1024]{2,1,0:T(8,128)(2,1)}, bf16[8,128,1024]{2,1,0:T(8,128)(2,1)}, f32[32,8,1152]{2,1,0:T(8,128)}) custom-call(s32[1]{0:T(128)S(6)} %copy.37.count.refs_0_, bf16[2048,1024]{1,0:T(8,128)(2,1)} %refs_1_.3, bf16[2048,1024]{1,0:T(8,128)(2,1)} %refs_7_.3, ...), custom_call_target="tpu_custom_call" | custom-call | tf_op jit(solution)/shard_map/local_states/pallas_call | solution.py:130
  13.1 8.3 %all-to-all-start = ((f32[32,8,1152]{2,1,0:T(8,128)}), f32[32,8,1152]{2,1,0:T(8,128)S(1)}, u32[]{:S(2)}, u32[]{:S(2)}) async-start(f32[32,8,1152]{2,1,0:T(8,128)} %get-tuple-element.60), calls=%async_computation | async-start | bytes 2359296 | tf_op jit(solution)/shard_map/all_to_all | solution.py:488
  21.4 17.3 %within_blocks.2 = (bf16[2048,1024]{1,0:T(8,128)(2,1)}, f32[2048,128]{1,0:T(8,128)}, f32[2048,128]{1,0:T(8,128)}, f32[8,2048]{1,0:T(8,128)}, f32[2048,128]{1,0:T(8,128)}) custom-call(f32[8]{0:T(128)} %gain.3, bf16[2048,1024]{1,0:T(8,128)(2,1)} %refs_1_.3, bf16[2048,1024]{1,0:T(8,128)(2,1)} %refs_7_.3, bf16[2048,128]{1,0:T(8,128)(2,1)} %refs_2_.3, ...), custom_call_target="tpu_custom_call" | custom-call | tf_op jit(solution)/shard_map/within_blocks/pallas_call | solution.py:247
  38.7 1.7 %all-to-all-done.got_ref = f32[32,8,1152]{2,1,0:T(8,128)S(1)} async-done(((f32[32,8,1152]{2,1,0:T(8,128)}), f32[32,8,1152]{2,1,0:T(8,128)S(1)}, u32[]{:S(2)}, u32[]{:S(2)}) %all-to-all-start) | async-done | bytes 1179680 | tf_op jit(solution)/shard_map/all_to_all | solution.py:488
  40.4 1.3 %scan_devices.1 = f32[32,8,1024]{2,1,0:T(8,128)} custom-call(f32[32,8,1152]{2,1,0:T(8,128)S(1)} %all-to-all-done.got_ref), custom_call_target="tpu_custom_call" | custom-call | tf_op jit(solution)/shard_map/scan_devices/pallas_call | solution.py:190
  41.7 5.7 %all-to-all-start.1 = ((f32[32,8,1024]{2,1,0:T(8,128)}), f32[32,8,1024]{2,1,0:T(8,128)S(1)}, u32[]{:S(2)}, u32[]{:S(2)}) async-start(f32[32,8,1024]{2,1,0:T(8,128)} %scan_devices.1), calls=%async_computation.1 | async-start | bytes 2097152 | tf_op jit(solution)/shard_map/all_to_all | solution.py:492
  47.4 17.3 %within_blocks.3 = (bf16[2048,1024]{1,0:T(8,128)(2,1)}, f32[2048,128]{1,0:T(8,128)}, f32[2048,128]{1,0:T(8,128)}, f32[8,2048]{1,0:T(8,128)}, f32[2048,128]{1,0:T(8,128)}) custom-call(f32[8]{0:T(128)} %gain.3, bf16[2048,1024]{1,0:T(8,128)(2,1)} %refs_1_.3, ...), custom_call_target="tpu_custom_call", output_to_operand_aliasing={{0}: (9, {}), {1}: (10, {}), {2}: (11, {}), {3}: (12, {}), ... | custom-call | tf_op jit(solution)/shard_map/within_blocks/pallas_call | solution.py:247
  64.7 0.0 all-to-all-done.1.got_ref.refs_10_
  64.7 0.0 copy-start
  64.7 1.0 copy-done
  65.7 10.4 %basis_grads.1 = (f32[2,512,128]{2,1,0:T(8,128)}, f32[2,512,128]{2,1,0:T(8,128)}, f32[2,512,128]{2,1,0:T(8,128)}, f32[2,512,128]{2,1,0:T(8,128)}) custom-call(s32[1]{0:T(128)} %bitcast.me, f32[8,2048]{1,0:T(8,128)} %get-tuple-element.58.cum_ref.refs_4_, bf16[2048,1024]{1,0:T(8,128)(2,1)} %refs_1_.3, bf16[2048,1024]{1,0:T(8,128)(2,1)} %refs_7_.3, ...), custom_call_target="tpu_custom_call" | custom-call | tf_op jit(solution)/shard_map/basis_grads/pallas_call | solution.py:356
  76.1 1.6 %collective-permute-start = (f32[2,512,128]{2,1,0:T(8,128)}, f32[2,512,128]{2,1,0:T(8,128)S(1)}, u32[]{:S(2)}, u32[]{:S(2)}) collective-permute-start(f32[2,512,128]{2,1,0:T(8,128)} %get-tuple-element.83), channel_id=1, source_target_pairs={{0,1},{1,2},{2,3},{3,0},{4,5},{5,6},{6,7},{7,4},{8,9},{9,10},{10,1... | collective-permute-start | bytes 1572872 | tf_op jit(solution)/shard_map/ppermute | solution.py:475
  77.7 0.0 copy-start.3
  77.7 0.0 copy-start.4
  77.7 1.7 %collective-permute-start.1 = (f32[2,512,128]{2,1,0:T(8,128)}, f32[2,512,128]{2,1,0:T(8,128)S(1)}, u32[]{:S(2)}, u32[]{:S(2)}) collective-permute-start(f32[2,512,128]{2,1,0:T(8,128)} %get-tuple-element.84), channel_id=1, source_target_pairs={{0,3},{1,0},{2,1},{3,2},{4,7},{5,4},{6,5},{7,6},{8,11},{9,8},{10,9... | collective-permute-start | bytes 1572872 | tf_op jit(solution)/shard_map/ppermute | solution.py:479
  79.3 11.4 %row_grads.2 = (bf16[2048,1024]{1,0:T(8,128)(2,1)}, f32[8,2048]{1,0:T(8,128)}, f32[8,2048]{1,0:T(8,128)}) custom-call(s32[1]{0:T(128)S(6)} %copy.37.count.refs_0_, bf16[2048,1024]{1,0:T(8,128)(2,1)} %refs_1_.3, bf16[2048,128]{1,0:T(8,128)(2,1)} %refs_2_.3, bf16[2048,128]{1,0:T(8,128)(2,1)} %refs_3_.3, f32[8,2048]{1,0:T(8,128)} %get-tuple-element.58.cum_ref.refs_4_, ...), custom_call_target="tpu_custom_call" | custom-call | tf_op jit(solution)/shard_map/row_grads/pallas_call | solution.py:453
  90.7 1.0 collective-permute-done
  91.7 0.0 collective-permute-done.1
  91.7 0.0 copy-done.3
  91.7 0.1 add_bitcast_fusion.1
  91.8 1.7 %collective-permute-start.2 = (f32[512,128]{1,0:T(8,128)S(1)}, f32[512,128]{1,0:T(8,128)S(1)}, u32[]{:S(2)}, u32[]{:S(2)}) collective-permute-start(f32[512,128]{1,0:T(8,128)S(1)} %get-tuple-element.119), channel_id=1, source_target_pairs={{0,1},{1,2},{2,3},{3,0},{4,5},{5,6},{6,7},{7,4},{8,9},{9,10},{10,1... | collective-permute-start | bytes 786440 | tf_op jit(solution)/shard_map/ppermute | solution.py:475
  93.4 1.6 %collective-permute-start.3 = (f32[512,128]{1,0:T(8,128)S(1)}, f32[512,128]{1,0:T(8,128)S(1)}, u32[]{:S(2)}, u32[]{:S(2)}) collective-permute-start(f32[512,128]{1,0:T(8,128)S(1)} %get-tuple-element.120), channel_id=1, source_target_pairs={{0,3},{1,0},{2,1},{3,2},{4,7},{5,4},{6,5},{7,6},{8,11},{9,8},{10,9... | collective-permute-start | bytes 786440 | tf_op jit(solution)/shard_map/ppermute | solution.py:479
  95.1 5.7 %collective-permute-done.2 = f32[512,128]{1,0:T(8,128)S(1)} collective-permute-done((f32[512,128]{1,0:T(8,128)S(1)}, f32[512,128]{1,0:T(8,128)S(1)}, u32[]{:S(2)}, u32[]{:S(2)}) %collective-permute-start.2) | collective-permute-done | bytes 262176 | tf_op jit(solution)/shard_map/ppermute | solution.py:475
  100.8 0.0 collective-permute-done.3
  100.8 0.0 copy-done.4
  100.8 0.1 fusion.1
  100.9 1.1 collective-permute-start.4
  102.0 2.2 %collective-permute-start.5 = (f32[2,512,128]{2,1,0:T(8,128)S(1)}, f32[2,512,128]{2,1,0:T(8,128)S(1)}, u32[]{:S(2)}, u32[]{:S(2)}) collective-permute-start(f32[2,512,128]{2,1,0:T(8,128)S(1)} %pad_maximum_fusion), channel_id=1, source_target_pairs={{0,3},{1,0},{2,1},{3,2},{4,7},{5,4},{6,5},{7,6},{8,11},{9,8},{10,9... | collective-permute-start | bytes 1572872 | tf_op jit(solution)/shard_map/ppermute | solution.py:479
  104.2 8.0 %row_grads.3 = (bf16[2048,1024]{1,0:T(8,128)(2,1)}, f32[8,2048]{1,0:T(8,128)}, f32[8,2048]{1,0:T(8,128)}) custom-call(s32[1]{0:T(128)S(6)} %copy.37.count.refs_0_, bf16[2048,1024]{1,0:T(8,128)(2,1)} %refs_1_.3, bf16[2048,128]{1,0:T(8,128)(2,1)} %refs_2_.3, bf16[2048,128]{1,0:T(8,128)(2,1)} %refs_3_.3, ...), custom_call_target="tpu_custom_call", output_to_operand_aliasing={{0}: (14, {}), {1}: (15, {}), {2}: (16, {})} | custom-call | tf_op jit(solution)/shard_map/row_grads/pallas_call | solution.py:453
  112.2 0.1 broadcast_in_dim.9.clone
  112.3 0.1 broadcast_in_dim.9.clone.1
  112.4 2.3 %collective-permute-done.4 = f32[2,512,128]{2,1,0:T(8,128)} collective-permute-done((f32[2,512,128]{2,1,0:T(8,128)S(1)}, f32[2,512,128]{2,1,0:T(8,128)}, u32[]{:S(2)}, u32[]{:S(2)}) %collective-permute-start.4) | collective-permute-done | bytes 524320 | tf_op jit(solution)/shard_map/ppermute | solution.py:475
  114.7 0.0 collective-permute-done.5
  114.7 1.1 slice_dynamic-update-slice_fusion
  115.8 0.1 slice_bitcast_fusion
  115.9 2.9 %collective-permute-start.7 = (f32[512,128]{1,0:T(8,128)S(1)}, f32[512,128]{1,0:T(8,128)S(1)}, u32[]{:S(2)}, u32[]{:S(2)}) collective-permute-start(f32[512,128]{1,0:T(8,128)S(1)} %get-tuple-element.111), channel_id=1, source_target_pairs={{0,3},{1,0},{2,1},{3,2},{4,7},{5,4},{6,5},{7,6},{8,11},{9,8},{10,9... | collective-permute-start | bytes 786440 | tf_op jit(solution)/shard_map/ppermute | solution.py:479
  118.8 0.0 collective-permute-start.6
  118.8 3.9 %collective-permute-done.7 = f32[512,128]{1,0:T(8,128)S(1)} collective-permute-done((f32[512,128]{1,0:T(8,128)S(1)}, f32[512,128]{1,0:T(8,128)S(1)}, u32[]{:S(2)}, u32[]{:S(2)}) %collective-permute-start.7) | collective-permute-done | bytes 262176 | tf_op jit(solution)/shard_map/ppermute | solution.py:479
  122.7 0.0 copy-start.2
  122.7 3.7 %collective-permute-done.6 = f32[512,128]{1,0:T(8,128)S(1)} collective-permute-done((f32[512,128]{1,0:T(8,128)S(1)}, f32[512,128]{1,0:T(8,128)S(1)}, u32[]{:S(2)}, u32[]{:S(2)}) %collective-permute-start.6) | collective-permute-done | bytes 262176 | tf_op jit(solution)/shard_map/ppermute | solution.py:475
  126.4 0.0 copy-start.1
  126.4 0.0 copy-done.2
  126.4 1.0 copy-done.1
  (5 shorter events, 0.1 us)
Async XLA Ops:
  13.1 27.3 %all-to-all-start = ((f32[32,8,1152]{2,1,0:T(8,128)}), f32[32,8,1152]{2,1,0:T(8,128)S(1)}, u32[]{:S(2)}, u32[]{:S(2)}) async-start(f32[32,8,1152]{2,1,0:T(8,128)} %get-tuple-element.60), calls=%async_computation | async-start | bytes 2359296 | tf_op jit(solution)/shard_map/all_to_all | solution.py:488
  41.7 23.0 %all-to-all-start.1 = ((f32[32,8,1024]{2,1,0:T(8,128)}), f32[32,8,1024]{2,1,0:T(8,128)S(1)}, u32[]{:S(2)}, u32[]{:S(2)}) async-start(f32[32,8,1024]{2,1,0:T(8,128)} %scan_devices.1), calls=%async_computation.1 | async-start | bytes 2097152 | tf_op jit(solution)/shard_map/all_to_all | solution.py:492
  64.7 1.0 copy-start
  76.1 15.6 %collective-permute-start = (f32[2,512,128]{2,1,0:T(8,128)}, f32[2,512,128]{2,1,0:T(8,128)S(1)}, u32[]{:S(2)}, u32[]{:S(2)}) collective-permute-start(f32[2,512,128]{2,1,0:T(8,128)} %get-tuple-element.83), channel_id=1, source_target_pairs={{0,1},{1,2},{2,3},{3,0},{4,5},{5,6},{6,7},{7,4},{8,9},{9,10},{10,1... | collective-permute-start | bytes 1572872 | tf_op jit(solution)/shard_map/ppermute | solution.py:475
  77.7 14.0 %copy-start.3 = (f32[2,512,128]{2,1,0:T(8,128)S(1)}, f32[2,512,128]{2,1,0:T(8,128)}, u32[]{:S(2)}) copy-start(f32[2,512,128]{2,1,0:T(8,128)} %get-tuple-element.93) | copy-start | bytes 1572868
  77.7 23.1 %copy-start.4 = (f32[2,512,128]{2,1,0:T(8,128)S(1)}, f32[2,512,128]{2,1,0:T(8,128)}, u32[]{:S(2)}) copy-start(f32[2,512,128]{2,1,0:T(8,128)} %get-tuple-element.82) | copy-start | bytes 1572868
  77.7 14.0 %collective-permute-start.1 = (f32[2,512,128]{2,1,0:T(8,128)}, f32[2,512,128]{2,1,0:T(8,128)S(1)}, u32[]{:S(2)}, u32[]{:S(2)}) collective-permute-start(f32[2,512,128]{2,1,0:T(8,128)} %get-tuple-element.84), channel_id=1, source_target_pairs={{0,3},{1,0},{2,1},{3,2},{4,7},{5,4},{6,5},{7,6},{8,11},{9,8},{10,9... | collective-permute-start | bytes 1572872 | tf_op jit(solution)/shard_map/ppermute | solution.py:479
  91.8 9.0 %collective-permute-start.2 = (f32[512,128]{1,0:T(8,128)S(1)}, f32[512,128]{1,0:T(8,128)S(1)}, u32[]{:S(2)}, u32[]{:S(2)}) collective-permute-start(f32[512,128]{1,0:T(8,128)S(1)} %get-tuple-element.119), channel_id=1, source_target_pairs={{0,1},{1,2},{2,3},{3,0},{4,5},{5,6},{6,7},{7,4},{8,9},{9,10},{10,1... | collective-permute-start | bytes 786440 | tf_op jit(solution)/shard_map/ppermute | solution.py:475
  93.4 7.4 %collective-permute-start.3 = (f32[512,128]{1,0:T(8,128)S(1)}, f32[512,128]{1,0:T(8,128)S(1)}, u32[]{:S(2)}, u32[]{:S(2)}) collective-permute-start(f32[512,128]{1,0:T(8,128)S(1)} %get-tuple-element.120), channel_id=1, source_target_pairs={{0,3},{1,0},{2,1},{3,2},{4,7},{5,4},{6,5},{7,6},{8,11},{9,8},{10,9... | collective-permute-start | bytes 786440 | tf_op jit(solution)/shard_map/ppermute | solution.py:479
  100.9 13.8 %collective-permute-start.4 = (f32[2,512,128]{2,1,0:T(8,128)S(1)}, f32[2,512,128]{2,1,0:T(8,128)}, u32[]{:S(2)}, u32[]{:S(2)}) collective-permute-start(f32[2,512,128]{2,1,0:T(8,128)S(1)} %pad_maximum_fusion), channel_id=1, source_target_pairs={{0,1},{1,2},{2,3},{3,0},{4,5},{5,6},{6,7},{7,4},{8,9},{9,10},{10,1... | collective-permute-start | bytes 1572872 | tf_op jit(solution)/shard_map/ppermute | solution.py:475
  102.0 12.8 %collective-permute-start.5 = (f32[2,512,128]{2,1,0:T(8,128)S(1)}, f32[2,512,128]{2,1,0:T(8,128)S(1)}, u32[]{:S(2)}, u32[]{:S(2)}) collective-permute-start(f32[2,512,128]{2,1,0:T(8,128)S(1)} %pad_maximum_fusion), channel_id=1, source_target_pairs={{0,3},{1,0},{2,1},{3,2},{4,7},{5,4},{6,5},{7,6},{8,11},{9,8},{10,9... | collective-permute-start | bytes 1572872 | tf_op jit(solution)/shard_map/ppermute | solution.py:479
  115.9 6.8 %collective-permute-start.7 = (f32[512,128]{1,0:T(8,128)S(1)}, f32[512,128]{1,0:T(8,128)S(1)}, u32[]{:S(2)}, u32[]{:S(2)}) collective-permute-start(f32[512,128]{1,0:T(8,128)S(1)} %get-tuple-element.111), channel_id=1, source_target_pairs={{0,3},{1,0},{2,1},{3,2},{4,7},{5,4},{6,5},{7,6},{8,11},{9,8},{10,9... | collective-permute-start | bytes 786440 | tf_op jit(solution)/shard_map/ppermute | solution.py:479
  118.8 7.6 %collective-permute-start.6 = (f32[512,128]{1,0:T(8,128)S(1)}, f32[512,128]{1,0:T(8,128)S(1)}, u32[]{:S(2)}, u32[]{:S(2)}) collective-permute-start(f32[512,128]{1,0:T(8,128)S(1)} %get-tuple-element.115), channel_id=1, source_target_pairs={{0,1},{1,2},{2,3},{3,0},{4,5},{5,6},{6,7},{7,4},{8,9},{9,10},{10,1... | collective-permute-start | bytes 786440 | tf_op jit(solution)/shard_map/ppermute | solution.py:475
  122.7 3.7 %copy-start.2 = (f32[4,512,128]{2,1,0:T(8,128)}, f32[4,512,128]{2,1,0:T(8,128)S(1)}, u32[]{:S(2)}) copy-start(f32[4,512,128]{2,1,0:T(8,128)S(1)} %bitcast_dynamic-update-slice_fusion) | copy-start | bytes 3145732
  126.4 1.0 copy-start.1
